TPU v7x, 512 devices: a whole 4x8x8 slice. The times are simulated.
512 devices in a mesh: ctx: 64 (over x, z_lo, y), head: 8 (over z_hi, core).
Axes of the slice: x: 4, y: 8, z: 8 (z_hi: 4, z_lo: 2; z = z_hi * 2 + z_lo), core: 2. Of those that a mesh axis runs over, the one named last changes fastest.
Arguments:
- queries: bfloat16 [16384, 4096], P('ctx', 'head'), may hold values from -12 to 12
- keys: bfloat16 [16384, 4096], P('ctx', 'head'), may hold values from -4 to 4
- values: bfloat16 [16384, 4096], P('ctx', 'head'), may hold values from -6 to 6
- pool_weight: bfloat16 [512, 256], P('ctx'), may hold values from -0.375 to 0.375
- out_weight: bfloat16 [4096, 4096], P('head', 'ctx'), may hold values from -0.09375 to 0.09375
- pattern: int32 [128, 7], replicated, may hold values from 0 to 127, as said below
Outputs:
- mixed: bfloat16 [16384, 4096], P('ctx', 'head')
Inputs may be any that keep to these rules, and one draw needn't show every extreme that they name: `pattern`: the flat butterfly with the blocks of each shard relabelled: entry (i, b) names a key block that agrees with block i in all bits above b and differs from it in bit b. For b < 1 the lower bits are arbitrary. For b >= 1 the bits from 1 to b - 1 equal those of i, and over the 2 query blocks of one aligned group of 2 blocks the lowest 1 bits take each of their 2 values once.
All inputs are finite; a program needn't handle non-finite values.
Results may differ from a plain program's by a relative error of at most 0.019.
Values may be sent and summed in bfloat16 or wider, within the bound.
No kernel may reach another device: no remote copies, remote signals or barrier semaphores. Data moves between devices by JAX's collectives and lax.ppermute only.
A program may use at most 64 MiB of HBM per device.

v0:
```python
import jax
import jax.numpy as jnp
from jax import lax
from jax.sharding import PartitionSpec as P

HEAD_DIMENSION = 128
BLK = 128


def partner_2(x, axis, stride):
    return lax.ppermute(x, axis, [(i, i ^ 1 << stride) for i in range(lax.axis_size(axis))])


def merge_scores(running, scores, value_set, einsum_form):
    old_max, row_sum, weighted = running
    row_max = jnp.maximum(old_max, jnp.max(scores, axis=-1))
    weights = jnp.exp(scores - row_max[..., None])
    rescale = jnp.exp(old_max - row_max)
    row_sum = row_sum * rescale + jnp.sum(weights, axis=-1)
    weighted = weighted * rescale[..., None] + jnp.einsum(
        einsum_form, weights.astype(jnp.bfloat16), value_set, preferred_element_type=jnp.float32
    )
    return (row_max, row_sum, weighted)


def on_device(queries, keys, values, pool_weight, out_weight, pattern):
    tok_rows, col_width = queries.shape
    local_heads = col_width // HEAD_DIMENSION
    block_count = tok_rows // BLK
    local_bits = block_count.bit_length() - 1
    remote_bits = lax.axis_size("ctx").bit_length() - 1
    score_scale = HEAD_DIMENSION ** (-0.5)
    own_index = lax.axis_index("ctx")
    own_rows = lax.dynamic_slice_in_dim(pattern, own_index * block_count, block_count, 0)
    query_blk = queries.reshape(block_count, BLK, local_heads, HEAD_DIMENSION)
    key_rows = keys.reshape(block_count, BLK, col_width)
    value_rows = values.reshape(block_count, BLK, col_width)
    running = (
        jnp.full((block_count, local_heads, BLK), -jnp.inf, jnp.float32),
        jnp.zeros((block_count, local_heads, BLK), jnp.float32),
        jnp.zeros((block_count, local_heads, BLK, HEAD_DIMENSION), jnp.float32),
    )
    near_index = jnp.concatenate(
        [
            jnp.arange(block_count, dtype=jnp.int32)[:, None],
            own_rows[:, :local_bits] - own_index * block_count,
        ],
        axis=1,
    )
    near_keys = jnp.take(key_rows, near_index, axis=0).reshape(
        block_count, -1, local_heads, HEAD_DIMENSION
    )
    near_values = jnp.take(value_rows, near_index, axis=0).reshape(
        block_count, -1, local_heads, HEAD_DIMENSION
    )
    scores = (
        jnp.einsum("bqhd,bkhd->bhqk", query_blk, near_keys, preferred_element_type=jnp.float32)
        * score_scale
    )
    running = merge_scores(running, scores, near_values, "bhqk,bkhd->bhqd")
    pooled_landmark_keys = jnp.dot(pool_weight, keys, preferred_element_type=jnp.float32).astype(
        jnp.bfloat16
    )
    pooled_landmark_values = jnp.dot(
        pool_weight, values, preferred_element_type=jnp.float32
    ).astype(jnp.bfloat16)
    piece_keys = lax.all_gather(pooled_landmark_keys, "ctx", axis=0, tiled=True).reshape(
        -1, local_heads, HEAD_DIMENSION
    )
    piece_values = lax.all_gather(pooled_landmark_values, "ctx", axis=0, tiled=True).reshape(
        -1, local_heads, HEAD_DIMENSION
    )
    mark_scores = (
        jnp.einsum("bqhd,khd->bhqk", query_blk, piece_keys, preferred_element_type=jnp.float32)
        * score_scale
    )
    running = merge_scores(running, mark_scores, piece_values, "bhqk,khd->bhqd")
    for level in range(remote_bits):
        partner = jnp.bitwise_xor(own_index, 1 << level)
        wanted = own_rows[:, local_bits + level] - partner * block_count
        recv_keys, recv_values = partner_2((key_rows, value_rows), "ctx", level)
        far_keys = jnp.take(recv_keys, wanted, axis=0)
        far_values = jnp.take(recv_values, wanted, axis=0)
        far_scores = (
            jnp.einsum(
                "bqhd,bkhd->bhqk",
                query_blk,
                far_keys.reshape(block_count, BLK, local_heads, HEAD_DIMENSION),
                preferred_element_type=jnp.float32,
            )
            * score_scale
        )
        running = merge_scores(
            running,
            far_scores,
            far_values.reshape(block_count, BLK, local_heads, HEAD_DIMENSION),
            "bhqk,bkhd->bhqd",
        )
    row_max, row_sum, weighted = running
    attended = (
        (weighted / row_sum[..., None])
        .transpose(0, 2, 1, 3)
        .reshape(tok_rows, col_width)
        .astype(jnp.bfloat16)
    )
    partial_value = jnp.dot(
        attended,
        lax.all_gather(out_weight, "ctx", axis=1, tiled=True),
        preferred_element_type=jnp.float32,
    )
    return lax.psum_scatter(
        partial_value.astype(jnp.bfloat16), "head", scatter_dimension=1, tiled=True
    )


def solution(mesh):
    in_specs = (
        P("ctx", "head"),
        P("ctx", "head"),
        P("ctx", "head"),
        P("ctx", None),
        P("head", "ctx"),
        P(),
    )
    out_specs = P("ctx", "head")
    return jax.shard_map(
        on_device, mesh=mesh, in_specs=in_specs, out_specs=out_specs, check_vma=False
    )
```

profile of v0, /device:TPU:1, one launch (start us, length us, event | category | flops | bytes accessed | tf_op | source)
XLA Modules:
  0.0 503.7 jit_solution(15221089490795249946)
XLA Ops:
  6.5 8.4 %collective-permute-start.4 = (bf16[2,128,512]{2,1,0:T(8,128)(2,1)}, bf16[2,128,512]{2,1,0:T(8,128)(2,1)}, u32[]{:S(2)}, u32[]{:S(2)}) collective-permute-start(bf16[2,128,512]{2,1,0:T(8,128)(2,1)} %bitcast.272), channel_id=1, source_target_pairs={{0,32},{8,40},{16,48},{24,56},{32,0},{40,8},{48,16},{56,24},{64,96... | collective-permute-start | bytes 786440 | tf_op jit(solution)/shard_map/ppermute | solution.py:11
  15.0 4.0 collective-permute-start.6
  22.8 3.0 collective-permute-start
  30.5 139.3 %all_gather.9 = bf16[512,512]{1,0:T(8,128)(2,1)S(1)} all-gather(bf16[8,512]{1,0:T(8,128)(2,1)S(1)} %convolution_convert_fusion.2), channel_id=1, replica_groups=mesh['ctx'=64,'head'=8] {'ctx'}, dimensions={0}, use_global_device_ids=true | all-gather | bytes 532480 | tf_op jit(solution)/shard_map/all_gather | solution.py:67
  172.9 127.5 %all_gather.10 = bf16[512,512]{1,0:T(8,128)(2,1)S(1)} all-gather(bf16[8,512]{1,0:T(8,128)(2,1)S(1)} %convolution_convert_fusion.1), channel_id=1, replica_groups=mesh['ctx'=64,'head'=8] {'ctx'}, dimensions={0}, use_global_device_ids=true | all-gather | bytes 532480 | tf_op jit(solution)/shard_map/all_gather | solution.py:70
  302.9 3.6 collective-permute-start.1
  306.5 2.2 gather_fusion.6
  310.7 2.2 gather_fusion.7
  312.9 4.3 collective-permute-start.3
  317.2 2.2 gather_fusion.8
  321.3 2.2 gather_fusion.9
  323.5 2.3 broadcast_select_fusion.6
  329.4 3.4 collective-permute-start.9
  332.8 2.2 gather_fusion.2
  336.9 2.2 gather_fusion.3
  339.1 5.0 %collective-permute-start.10 = (bf16[2,128,512]{2,1,0:T(8,128)(2,1)}, bf16[2,128,512]{2,1,0:T(8,128)(2,1)}, u32[]{:S(2)}, u32[]{:S(2)}) collective-permute-start(bf16[2,128,512]{2,1,0:T(8,128)(2,1)} %bitcast.278), channel_id=1, source_target_pairs={{0,256},{8,264},{16,272},{24,280},{32,288},{40,296},{48,304},{56,3... | collective-permute-start | bytes 786440 | tf_op jit(solution)/shard_map/ppermute | solution.py:11
  344.2 2.2 gather_fusion.4
  346.4 2.2 gather_fusion.5
  348.6 2.3 broadcast_select_fusion.10
  358.9 2.2 gather_fusion.13
  361.1 2.2 gather_fusion.12
  363.4 2.3 broadcast_select_fusion.3
  398.5 4.8 convolution_convert_fusion
  403.4 93.5 %reduce-scatter.2.cloned.1.call-done = bf16[256,512]{1,0:T(8,128)(2,1)} async-done(((bf16[256,4096]{1,0:T(8,128)(2,1)}), bf16[256,512]{1,0:T(8,128)(2,1)}) %reduce-scatter.2.cloned.1.call-update) | async-done | bytes 262160 | tf_op jit(solution)/shard_map/reduce_scatter | solution.py:111
  (131 shorter events, 64.0 us)
Async XLA Ops:
  6.5 23.6 %copy-start = (bf16[8,256]{1,0:T(8,128)(2,1)S(1)}, bf16[8,256]{1,0:T(8,128)(2,1)}, u32[]{:S(2)}) copy-start(bf16[8,256]{1,0:T(8,128)(2,1)} %param.13) | copy-start | bytes 12292
  6.5 23.6 %copy-start.7 = (bf16[256,512]{1,0:T(8,128)(2,1)S(1)}, bf16[256,512]{1,0:T(8,128)(2,1)}, u32[]{:S(2)}) copy-start(bf16[256,512]{1,0:T(8,128)(2,1)} %param.11) | copy-start | bytes 786436
  6.5 392.0 %all-gather.2.cloned.1.call-start = ((), (), s32[]{:S(2)}) async-start(), calls=%async_computation.1 | async-start | bytes 4259840 | tf_op jit(solution)/shard_map/all_gather | solution.py:108
  6.5 296.4 %collective-permute-start.4 = (bf16[2,128,512]{2,1,0:T(8,128)(2,1)}, bf16[2,128,512]{2,1,0:T(8,128)(2,1)}, u32[]{:S(2)}, u32[]{:S(2)}) collective-permute-start(bf16[2,128,512]{2,1,0:T(8,128)(2,1)} %bitcast.272), channel_id=1, source_target_pairs={{0,32},{8,40},{16,48},{24,56},{32,0},{40,8},{48,16},{56,24},{64,96... | collective-permute-start | bytes 786440 | tf_op jit(solution)/shard_map/ppermute | solution.py:11
  15.0 297.9 %collective-permute-start.6 = (bf16[2,128,512]{2,1,0:T(8,128)(2,1)}, bf16[2,128,512]{2,1,0:T(8,128)(2,1)}, u32[]{:S(2)}, u32[]{:S(2)}) collective-permute-start(bf16[2,128,512]{2,1,0:T(8,128)(2,1)} %bitcast.273), channel_id=1, source_target_pairs={{0,64},{8,72},{16,80},{24,88},{32,96},{40,104},{48,112},{56,120},{... | collective-permute-start | bytes 786440 | tf_op jit(solution)/shard_map/ppermute | solution.py:11
  19.0 289.8 %collective-permute-start.5 = (bf16[2,128,512]{2,1,0:T(8,128)(2,1)}, bf16[2,128,512]{2,1,0:T(8,128)(2,1)}, u32[]{:S(2)}, u32[]{:S(2)}) collective-permute-start(bf16[2,128,512]{2,1,0:T(8,128)(2,1)} %bitcast.4), channel_id=1, source_target_pairs={{0,32},{8,40},{16,48},{24,56},{32,0},{40,8},{48,16},{56,24},{64,96... | collective-permute-start | bytes 786440 | tf_op jit(solution)/shard_map/ppermute | solution.py:11
  20.9 298.5 %collective-permute-start.7 = (bf16[2,128,512]{2,1,0:T(8,128)(2,1)}, bf16[2,128,512]{2,1,0:T(8,128)(2,1)}, u32[]{:S(2)}, u32[]{:S(2)}) collective-permute-start(bf16[2,128,512]{2,1,0:T(8,128)(2,1)} %bitcast.4), channel_id=1, source_target_pairs={{0,64},{8,72},{16,80},{24,88},{32,96},{40,104},{48,112},{56,120},{... | collective-permute-start | bytes 786440 | tf_op jit(solution)/shard_map/ppermute | solution.py:11
  22.8 306.6 %collective-permute-start = (bf16[2,128,512]{2,1,0:T(8,128)(2,1)}, bf16[2,128,512]{2,1,0:T(8,128)(2,1)}, u32[]{:S(2)}, u32[]{:S(2)}) collective-permute-start(bf16[2,128,512]{2,1,0:T(8,128)(2,1)} %bitcast.274), channel_id=1, source_target_pairs={{0,8},{8,0},{16,24},{24,16},{32,40},{40,32},{48,56},{56,48},{64,72... | collective-permute-start | bytes 786440 | tf_op jit(solution)/shard_map/ppermute | solution.py:11
  25.9 470.9 %reduce-scatter.2.cloned.1.call-start = ((), (), s32[]{:S(2)}) async-start(), calls=%async_computation.2 | async-start | bytes 2359296 | tf_op jit(solution)/shard_map/reduce_scatter | solution.py:111
  28.5 141.3 %copy-start.20 = (bf16[256,512]{1,0:T(8,128)(2,1)S(1)}, bf16[256,512]{1,0:T(8,128)(2,1)}, u32[]{:S(2)}) copy-start(bf16[256,512]{1,0:T(8,128)(2,1)} %param.10) | copy-start | bytes 786436
  302.9 32.1 %collective-permute-start.1 = (bf16[2,128,512]{2,1,0:T(8,128)(2,1)}, bf16[2,128,512]{2,1,0:T(8,128)(2,1)}, u32[]{:S(2)}, u32[]{:S(2)}) collective-permute-start(bf16[2,128,512]{2,1,0:T(8,128)(2,1)} %bitcast.4), channel_id=1, source_target_pairs={{0,8},{8,0},{16,24},{24,16},{32,40},{40,32},{48,56},{56,48},{64,72... | collective-permute-start | bytes 786440 | tf_op jit(solution)/shard_map/ppermute | solution.py:11
  308.7 30.4 %collective-permute-start.2 = (bf16[2,128,512]{2,1,0:T(8,128)(2,1)}, bf16[2,128,512]{2,1,0:T(8,128)(2,1)}, u32[]{:S(2)}, u32[]{:S(2)}) collective-permute-start(bf16[2,128,512]{2,1,0:T(8,128)(2,1)} %bitcast.276), channel_id=1, source_target_pairs={{0,16},{8,24},{16,0},{24,8},{32,48},{40,56},{48,32},{56,40},{64,80... | collective-permute-start | bytes 786440 | tf_op jit(solution)/shard_map/ppermute | solution.py:11
  312.9 33.5 %collective-permute-start.3 = (bf16[2,128,512]{2,1,0:T(8,128)(2,1)}, bf16[2,128,512]{2,1,0:T(8,128)(2,1)}, u32[]{:S(2)}, u32[]{:S(2)}) collective-permute-start(bf16[2,128,512]{2,1,0:T(8,128)(2,1)} %bitcast.4), channel_id=1, source_target_pairs={{0,16},{8,24},{16,0},{24,8},{32,48},{40,56},{48,32},{56,40},{64,80... | collective-permute-start | bytes 786440 | tf_op jit(solution)/shard_map/ppermute | solution.py:11
  319.4 35.1 %collective-permute-start.8 = (bf16[2,128,512]{2,1,0:T(8,128)(2,1)}, bf16[2,128,512]{2,1,0:T(8,128)(2,1)}, u32[]{:S(2)}, u32[]{:S(2)}) collective-permute-start(bf16[2,128,512]{2,1,0:T(8,128)(2,1)} %bitcast.277), channel_id=1, source_target_pairs={{0,128},{8,136},{16,144},{24,152},{32,160},{40,168},{48,176},{56,1... | collective-permute-start | bytes 786440 | tf_op jit(solution)/shard_map/ppermute | solution.py:11
  329.4 27.3 %collective-permute-start.9 = (bf16[2,128,512]{2,1,0:T(8,128)(2,1)}, bf16[2,128,512]{2,1,0:T(8,128)(2,1)}, u32[]{:S(2)}, u32[]{:S(2)}) collective-permute-start(bf16[2,128,512]{2,1,0:T(8,128)(2,1)} %bitcast.4), channel_id=1, source_target_pairs={{0,128},{8,136},{16,144},{24,152},{32,160},{40,168},{48,176},{56,1... | collective-permute-start | bytes 786440 | tf_op jit(solution)/shard_map/ppermute | solution.py:11
  335.0 23.9 %collective-permute-start.11 = (bf16[2,128,512]{2,1,0:T(8,128)(2,1)}, bf16[2,128,512]{2,1,0:T(8,128)(2,1)}, u32[]{:S(2)}, u32[]{:S(2)}) collective-permute-start(bf16[2,128,512]{2,1,0:T(8,128)(2,1)} %bitcast.4), channel_id=1, source_target_pairs={{0,256},{8,264},{16,272},{24,280},{32,288},{40,296},{48,304},{56,3... | collective-permute-start | bytes 786440 | tf_op jit(solution)/shard_map/ppermute | solution.py:11
  339.1 22.0 %collective-permute-start.10 = (bf16[2,128,512]{2,1,0:T(8,128)(2,1)}, bf16[2,128,512]{2,1,0:T(8,128)(2,1)}, u32[]{:S(2)}, u32[]{:S(2)}) collective-permute-start(bf16[2,128,512]{2,1,0:T(8,128)(2,1)} %bitcast.278), channel_id=1, source_target_pairs={{0,256},{8,264},{16,272},{24,280},{32,288},{40,296},{48,304},{56,3... | collective-permute-start | bytes 786440 | tf_op jit(solution)/shard_map/ppermute | solution.py:11
  369.3 4.3 copy-start.17
  369.3 5.4 %copy-start.16 = (bf16[2,128,512]{1,2,0:T(8,128)(2,1)S(1)}, bf16[2,128,512]{1,2,0:T(8,128)(2,1)}, u32[]{:S(2)}) copy-start(bf16[2,128,512]{1,2,0:T(8,128)(2,1)} %copy.203) | copy-start | bytes 786436
  369.3 6.6 %copy-start.19 = (bf16[2,128,512]{1,2,0:T(8,128)(2,1)S(1)}, bf16[2,128,512]{1,2,0:T(8,128)(2,1)}, u32[]{:S(2)}) copy-start(bf16[2,128,512]{1,2,0:T(8,128)(2,1)} %copy.233) | copy-start | bytes 786436
  371.4 5.5 %copy-start.18 = (bf16[2,128,512]{1,2,0:T(8,128)(2,1)S(1)}, bf16[2,128,512]{1,2,0:T(8,128)(2,1)}, u32[]{:S(2)}) copy-start(bf16[2,128,512]{1,2,0:T(8,128)(2,1)} %copy.227) | copy-start | bytes 786436
  388.3 4.7 copy-start.6
  388.3 4.8 copy-start.4
  393.7 1.5 copy-start.12
  (11 other events, 13.0 us)
Sparse Core Ops, SparseCore 0:
  26.0 268.7 all-gather.1
  403.5 93.2 reduce-scatter.1
where the time goes:
time: 507 us; the launch traced here: 504 us
  blocking collectives  267 us (53%)
  waiting for transfers between devices  93.6 us (18%)
  local copies, waits for them, and re-layouts  55.9 us (11%)
  starting transfers between devices  41.3 us (8%)
  matrix products  19.7 us (4%)
  between operations  13.9 us (3%)
  other arithmetic  12.6 us (2%)
    all_gather x1, blocking collectives, on_device(): lax.all_gather(pooled_landmark_keys, 'ctx', axis=0, tiled=True)  139 us
    all_gather x1, blocking collectives, on_device(): lax.all_gather(pooled_landmark_values, 'ctx', axis=0, tiled=True)  127 us
    reduce_scatter x1, waiting for transfers between devices, on_device(): lax.psum_scatter(partial_value.astype(jnp.bfloat16), 'head', scatter_dime...  93.5 us
    ppermute x12, starting transfers between devices, partner_2(): lax.ppermute(x, axis, [(i, i ^ 1 << stride) for i in range(lax.axis_size(...  41.2 us
    gather x6, local copies, waits for them, and re-layouts, on_device(): far_keys = jnp.take(recv_keys, wanted, axis=0)  13.3 us
    gather x6, local copies, waits for them, and re-layouts, on_device(): far_values = jnp.take(recv_values, wanted, axis=0)  13.3 us
    select_n x6, local copies, waits for them, and re-layouts, on_device(): far_keys = jnp.take(recv_keys, wanted, axis=0)  10.7 us
  transfers between devices with their start and end apart: 14, of which 1 were waited for; matrix products, arithmetic and copies ran while one was open for 16% of the time, Pallas kernels for 0%

commit v1 on v0

v1 whole, which is shorter than its diff:
```python
import functools

import jax
import jax.numpy as jnp
from jax import lax
from jax.experimental import pallas as pl
from jax.experimental.pallas import tpu as pltpu
from jax.sharding import PartitionSpec as P

HD = 128
BLK = 128
NX, NZL, NY, NZH, NC = 4, 2, 8, 4, 2
WROWS = 64
LROWS = 16
UNIT = WROWS + LROWS
AXES = ("ctx", "head")
SCALE = HD**-0.5
F32 = jnp.float32
BF16 = jnp.bfloat16
VLIM = 16 << 20


def coords(i):
    ctx, head = divmod(i, NZH * NC)
    x, r = divmod(ctx, NZL * NY)
    zl, y = divmod(r, NY)
    zh, c = divmod(head, NC)
    return x, zl, y, zh, c


def flat(x, zl, y, zh, c):
    return ((x * NZL + zl) * NY + y) * (NZH * NC) + zh * NC + c


def send(a, to):
    pairs = [(i, flat(*to(*coords(i)))) for i in range(NX * NZL * NY * NZH * NC)]
    return lax.ppermute(a, AXES, pairs)


def along_x(k):
    return lambda x, zl, y, zh, c: ((x + k) % NX, zl, y, zh, c)


def xor(level):
    def to(x, zl, y, zh, c):
        ctx = ((x * NZL + zl) * NY + y) ^ (1 << level)
        x, r = divmod(ctx, NZL * NY)
        zl, y = divmod(r, NY)
        return x, zl, y, zh, c

    return to


def after(a, far, levels):
    if levels:
        a, done = lax.optimization_barrier((a, [far[l] for l in levels]))
        far.update(zip(levels, done, strict=True))
    return a


def vmem(n):
    return [pl.BlockSpec(memory_space=pltpu.VMEM)] * n


SMEM = pl.BlockSpec(memory_space=pltpu.SMEM)


def params():
    return pltpu.CompilerParams(vmem_limit_bytes=VLIM)


def dot_nt(a, b):
    return lax.dot_general(a, b, (((1,), (1,)), ((), ())), preferred_element_type=F32)


def prepare_kernel(pool, keys, values, weight, kv, unit):
    k, v = keys[...], values[...]
    kv[0:256, :] = k
    kv[256:512, :] = v
    unit[0:WROWS, :] = weight[...].astype(F32).T.astype(BF16)
    pooled = [jnp.dot(pool[...], a, preferred_element_type=F32) for a in (k, v)]
    unit[WROWS:UNIT, :] = jnp.concatenate(pooled, axis=0).astype(BF16)


def prepare(pool, keys, values, weight):
    return pl.pallas_call(
        prepare_kernel,
        out_shape=(
            jax.ShapeDtypeStruct((512, 512), BF16),
            jax.ShapeDtypeStruct((UNIT, 512), BF16),
        ),
        in_specs=vmem(4),
        out_specs=tuple(vmem(2)),
        compiler_params=params(),
        name="prepare",
    )(pool, keys, values, weight)


def softmax_step(state, q, ks, vs):
    scores = [dot_nt(q, k) * SCALE for k in ks]
    top = functools.reduce(jnp.maximum, [jnp.max(s, axis=1, keepdims=True) for s in scores])
    if state is not None:
        old_top, old_sum, old_acc = state
        top = jnp.maximum(top, old_top)
    weights = [jnp.exp(s - top) for s in scores]
    total = sum(jnp.sum(w, axis=1, keepdims=True) for w in weights)
    acc = sum(
        jnp.dot(w.astype(BF16), v, preferred_element_type=F32)
        for w, v in zip(weights, vs, strict=True)
    )
    if state is not None:
        fade = jnp.exp(old_top - top)
        total = total + old_sum * fade
        acc = acc + old_acc * fade
    return top, total, acc


def far_blocks(place, pattern, j, level, ref):
    at = pl.multiple_of((pattern[place[3] + j, 1 + level] & 1) * BLK, BLK)
    return ref[pl.ds(at, BLK), :], ref[pl.ds(256 + at, BLK), :]


def by_head(rows):
    return pl.BlockSpec((rows, HD), lambda h: (0, h))


def first_kernel(levels, place, pattern, q, own, *refs):
    far, (top, total, acc) = refs[:-3], refs[-3:]
    for j in range(2):
        rows = slice(j * BLK, (j + 1) * BLK)
        ks, vs = [own[0:256, :]], [own[256:512, :]]
        for level, ref in zip(levels, far, strict=True):
            k, v = far_blocks(place, pattern, j, level, ref)
            ks.append(k)
            vs.append(v)
        m, s, a = softmax_step(None, q[rows, :], ks, vs)
        top[rows, :] = jnp.broadcast_to(m, (BLK, HD))
        total[rows, :] = jnp.broadcast_to(s, (BLK, HD))
        acc[rows, :] = a


def first(levels, place, pattern, q, own, far):
    return pl.pallas_call(
        functools.partial(first_kernel, levels),
        grid=(4,),
        out_shape=(jax.ShapeDtypeStruct((256, 512), F32),) * 3,
        in_specs=[SMEM, SMEM, by_head(256)] + [by_head(512)] * (1 + len(far)),
        out_specs=(by_head(256),) * 3,
        compiler_params=params(),
        name="first",
        cost_estimate=pl.CostEstimate(
            flops=4 * 256 * 512 * 768, bytes_accessed=4 << 20, transcendentals=786432
        ),
    )(place, pattern, q, own, *far)


def landmarks(units):
    ks, vs = [], []
    for ref, starts in units:
        for at in starts:
            pair = ref[at : at + LROWS, :].astype(F32)
            ks.append(pair[0:8])
            vs.append(pair[8:16])
    return jnp.concatenate(ks, axis=0).astype(BF16), jnp.concatenate(vs, axis=0).astype(BF16)


def lm_starts(lo, hi):
    rows = [b * UNIT + WROWS for b in range(NY)] + [NY * UNIT + b * LROWS for b in range(NY)]
    return [r - lo for r in rows if lo <= r < hi]


def last_kernel(levels, place, pattern, q, top, total, acc, wl0, wl1, wl3, wl2a, wl2b, *refs):
    far, out = refs[:-1], refs[-1]
    units = [(r, lm_starts(0, 768)) for r in (wl0, wl1, wl3)]
    units += [(wl2a, lm_starts(0, 400)), (wl2b, lm_starts(400, 768))]
    mark_k, mark_v = landmarks(units)
    for j in range(2):
        rows = slice(j * BLK, (j + 1) * BLK)
        ks, vs = [mark_k], [mark_v]
        for level, ref in zip(levels, far, strict=True):
            k, v = far_blocks(place, pattern, j, level, ref)
            ks.append(k)
            vs.append(v)
        state = (top[rows, 0:1], total[rows, 0:1], acc[rows, :])
        _, s, a = softmax_step(state, q[rows, :], ks, vs)
        out[rows, :] = (a / s).astype(BF16)


def last(levels, place, pattern, q, state, wl, far):
    return pl.pallas_call(
        functools.partial(last_kernel, levels),
        grid=(4,),
        out_shape=jax.ShapeDtypeStruct((256, 512), BF16),
        in_specs=[SMEM, SMEM]
        + [by_head(256)] * 4
        + [by_head(a.shape[0]) for a in wl]
        + [by_head(512)] * len(far),
        out_specs=by_head(256),
        compiler_params=params(),
        name="last",
        cost_estimate=pl.CostEstimate(
            flops=4 * 256 * 512 * 768, bytes_accessed=8 << 20, transcendentals=786432
        ),
    )(place, pattern, q, *state, *wl, *far)


def w_rows(pieces):
    out = []
    for y in range(NY):
        at = ((y & 1) * 4 + (y & 2) + (y >> 2)) * UNIT
        for ref, lo, hi in pieces:
            a, b = max(at, lo), min(at + WROWS, hi)
            if a < b:
                out.append(ref[a - lo : b - lo, :])
    return jnp.concatenate(out, axis=0)


def project_kernel(place, mine, other, wl0, wl1, wl3, wl2a, wl2b, keep, give):
    x, zh, same = place[0], place[1], place[2]
    swap = same == 0
    a, b = mine[...], other[...]
    kept = jnp.where(swap, b, a)
    given = jnp.where(swap, a, b)
    chunks = [(0, [(wl0, 0, 768)]), (1, [(wl1, 0, 768)]), (3, [(wl3, 0, 768)])]
    chunks += [(2, [(wl2a, 0, 400), (wl2b, 400, 768)])]
    for shift, pieces in chunks:
        w = w_rows(pieces)
        d = lax.rem(x + 8 - shift - zh, 4)
        give[d] = dot_nt(given, w).astype(BF16)
        keep[d] = dot_nt(kept, w)


def project(place, mine, other, wl):
    return pl.pallas_call(
        project_kernel,
        out_shape=(
            jax.ShapeDtypeStruct((4, 256, 512), F32),
            jax.ShapeDtypeStruct((4, 256, 512), BF16),
        ),
        in_specs=[SMEM, *vmem(7)],
        out_specs=tuple(vmem(2)),
        compiler_params=params(),
        name="project",
        cost_estimate=pl.CostEstimate(
            flops=2 * 512 * 512 * 2048, bytes_accessed=6 << 20, transcendentals=0
        ),
    )(place, mine, other, *wl)


def on_device(queries, keys, values, pool_weight, out_weight, pattern):
    ctx, head = lax.axis_index("ctx"), lax.axis_index("head")
    x, zl, y = ctx // (NZL * NY), (ctx // NY) % NZL, ctx % NY
    zh, c = head // NC, head % NC
    place = jnp.stack([x, zh, (zl == c).astype(jnp.int32), ctx * 2])

    kv, unit = prepare(pool_weight, keys, values, out_weight)
    far = {level: send(kv, xor(level)) for level in (5, 3, 4)}
    wl = unit
    for bit in (2, 1, 0):
        got = send(wl, xor(bit))
        up = ((y >> bit) & 1) == 1
        wl = jnp.concatenate([jnp.where(up, got, wl), jnp.where(up, wl, got)], axis=0)
    wl = after(wl, far, (3, 5))
    kv_y, wl = lax.optimization_barrier((kv, wl))
    far.update({level: send(kv_y, xor(level)) for level in (2, 1, 0)})
    marks = wl.reshape(NY, UNIT, 512)[:, WROWS:].reshape(NY * LROWS, 512)
    wl = jnp.concatenate([wl, send(marks, xor(3))], axis=0)
    wl = after(wl, far, (4,))
    wl1, wl3 = send(wl, along_x(1)), send(wl, along_x(-1))
    wl1 = after(wl1, far, (2,))
    wl2a, wl2b = send(wl1[:400], along_x(1)), send(wl3[400:], along_x(-1))
    pieces = (wl, wl1, wl3, wl2a, wl2b)

    early, late = (5, 3, 4, 2), (1, 0)
    state = first(early, place, pattern, queries, kv, [far[l] for l in early])
    mine = last(late, place, pattern, queries, state, pieces, [far[l] for l in late])
    other = send(mine, xor(3))
    keep, give = project(place, mine, other, pieces)
    got = send(give, lambda x, zl, y, zh, c: (x, zl, y, zh, 1 - c))
    part = (keep + got.astype(F32)).astype(BF16)
    total = 0.0
    for d in range(4):
        total += send(
            part[d], lambda x, zl, y, zh, c: (x, c, y, (zh + d) % NZH, zl)
        ).astype(F32)
    return total.astype(BF16)


def solution(mesh):
    in_specs = (
        P("ctx", "head"),
        P("ctx", "head"),
        P("ctx", "head"),
        P("ctx", None),
        P("head", "ctx"),
        P(),
    )
    return jax.shard_map(
        on_device, mesh=mesh, in_specs=in_specs, out_specs=P("ctx", "head"), check_vma=False
    )
```

time: 507 us -> 183 us (0.36)
  blocking collectives: 267 us -> 0 us
  local copies, waits for them, and re-layouts: 55.9 us -> 12.6 us
  starting transfers between devices: 41.3 us -> 79.7 us
  waiting for transfers between devices: 93.6 us -> 72.8 us
  matrix products: 19.7 us -> 0 us
  Pallas kernels: 0 us -> 15.2 us
  between operations: 13.9 us -> 0.42 us
  other arithmetic: 12.6 us -> 1.66 us
    all_gather x2 -> x0, blocking collectives: 267 us -> none  [the longest x1 139 us: on_device(): lax.all_gather(pooled_landmark_keys, 'ctx', axis=0, tiled=True)]
    reduce_scatter x1 -> x0, waiting for transfers between devices: 93.5 us -> none  [on_device(): lax.psum_scatter(partial_value.astype(jnp.bfloat16), 'head', scatter_dime...]
    ppermute x12 -> x20, waiting for transfers between devices: 0.03 us -> 72.8 us  [send(): return lax.ppermute(a, AXES, pairs)]
    ppermute x12 -> x20, starting transfers between devices: 41.2 us -> 79.7 us  [send(): return lax.ppermute(a, AXES, pairs)]
    gather x14 -> x0, local copies, waits for them, and re-layouts: 29.7 us -> none  [the longest x6 13.3 us: on_device(): far_keys = jnp.take(recv_keys, wanted, axis=0)]
    select_n x13 -> x0, local copies, waits for them, and re-layouts: 21 us -> none  [the longest x6 10.7 us: on_device(): far_keys = jnp.take(recv_keys, wanted, axis=0)]
    dot_general x19 -> x0, matrix products: 19.7 us -> none  [the longest x6 8.84 us: on_device(): jnp.einsum('bqhd,bkhd->bhqk', query_blk, far_keys.reshape(block_count, BL...]
    pallas_call x0 -> x4, Pallas kernels: none -> 15.2 us  [the longest x1 6.68 us: last(): pl.pallas_call(functools.partial(last_kernel, levels), grid=(4,), out_sha...]
  transfers between devices with their start and end apart: 14 -> 20, of which waited for: 1 -> 12; matrix products, arithmetic and copies ran while one was open for 16% -> 1% of each run, Pallas kernels for 0% -> 3%
where the time goes in v1:
time: 183 us; the launch traced here: 182 us
  starting transfers between devices  79.7 us (44%)
  waiting for transfers between devices  72.8 us (40%)
  Pallas kernels  15.2 us (8%)
  local copies, waits for them, and re-layouts  12.6 us (7%)
    ppermute x20, starting transfers between devices, send(): return lax.ppermute(a, AXES, pairs)  79.7 us
    ppermute x20, waiting for transfers between devices, send(): return lax.ppermute(a, AXES, pairs)  72.8 us
    unnamed x28, local copies, waits for them, and re-layouts  11 us
    pallas_call x1, Pallas kernels, last(): pl.pallas_call(functools.partial(last_kernel, levels), grid=(4,), out_sha...  6.68 us
    pallas_call x1, Pallas kernels, first(): pl.pallas_call(functools.partial(first_kernel, levels), grid=(4,), out_sh...  5.9 us
  transfers between devices with their start and end apart: 20, of which 12 were waited for; matrix products, arithmetic and copies ran while one was open for 1% of the time, Pallas kernels for 3%

profile of v1, /device:TPU:1, one launch (start us, length us, event | category | flops | bytes accessed | tf_op | source)
XLA Modules:
  0.0 182.4 jit_solution(3318122033850721136)
XLA Ops:
  3.8 8.3 %collective-permute-start = (bf16[80,512]{1,0:T(8,128)(2,1)S(1)}, bf16[80,512]{1,0:T(8,128)(2,1)S(1)}, u32[]{:S(2)}, u32[]{:S(2)}) collective-permute-start(bf16[80,512]{1,0:T(8,128)(2,1)S(1)} %get-tuple-element.22), channel_id=1, source_target_pairs={{0,32},{1,33},{2,34},{3,35},{4,36},{5,37},{6,38},{7,39},{8,40},{9,... | collective-permute-start | bytes 245768 | tf_op jit(solution)/shard_map/ppermute | solution.py:37
  14.0 5.7 %collective-permute-start.1 = (bf16[160,512]{1,0:T(8,128)(2,1)S(1)}, bf16[160,512]{1,0:T(8,128)(2,1)S(1)}, u32[]{:S(2)}, u32[]{:S(2)}) collective-permute-start(bf16[160,512]{1,0:T(8,128)(2,1)S(1)} %pad_maximum_fusion.3), channel_id=1, source_target_pairs={{0,16},{1,17},{2,18},{3,19},{4,20},{5,21},{6,22},{7,23},{8,24},{9,... | collective-permute-start | bytes 491528 | tf_op jit(solution)/shard_map/ppermute | solution.py:37
  19.6 5.7 %collective-permute-done.1 = bf16[160,512]{1,0:T(8,128)(2,1)S(1)} collective-permute-done((bf16[160,512]{1,0:T(8,128)(2,1)S(1)}, bf16[160,512]{1,0:T(8,128)(2,1)S(1)}, u32[]{:S(2)}, u32[]{:S(2)}) %collective-permute-start.1) | collective-permute-done | bytes 163872 | tf_op jit(solution)/shard_map/ppermute | solution.py:37
  27.3 5.7 %collective-permute-start.3 = (bf16[512,512]{1,0:T(8,128)(2,1)S(1)}, bf16[512,512]{1,0:T(8,128)(2,1)S(1)}, u32[]{:S(2)}, u32[]{:S(2)}) collective-permute-start(bf16[512,512]{1,0:T(8,128)(2,1)S(1)} %get-tuple-element.29.own), channel_id=1, source_target_pairs={{0,64},{1,65},{2,66},{3,67},{4,68},{5,69},{6,70},{7,71},{8,72},{9,... | collective-permute-start | bytes 1572872 | tf_op jit(solution)/shard_map/ppermute | solution.py:37
  33.0 4.7 %collective-permute-start.4 = (bf16[512,512]{1,0:T(8,128)(2,1)S(1)}, bf16[512,512]{1,0:T(8,128)(2,1)S(1)}, u32[]{:S(2)}, u32[]{:S(2)}) collective-permute-start(bf16[512,512]{1,0:T(8,128)(2,1)S(1)} %get-tuple-element.29.own), channel_id=1, source_target_pairs={{0,256},{1,257},{2,258},{3,259},{4,260},{5,261},{6,262},{7,263},{8... | collective-permute-start | bytes 1572872 | tf_op jit(solution)/shard_map/ppermute | solution.py:37
  40.1 3.4 %collective-permute-done.3.refs_1_ = bf16[512,512]{1,0:T(8,128)(2,1)S(1)} collective-permute-done((bf16[512,512]{1,0:T(8,128)(2,1)S(1)}, bf16[512,512]{1,0:T(8,128)(2,1)S(1)}, u32[]{:S(2)}, u32[]{:S(2)}) %collective-permute-start.3) | collective-permute-done | bytes 524320 | tf_op jit(solution)/shard_map/ppermute | solution.py:37
  44.3 4.2 %collective-permute-done.4.refs_0_ = bf16[512,512]{1,0:T(8,128)(2,1)S(1)} collective-permute-done((bf16[512,512]{1,0:T(8,128)(2,1)S(1)}, bf16[512,512]{1,0:T(8,128)(2,1)S(1)}, u32[]{:S(2)}, u32[]{:S(2)}) %collective-permute-start.4) | collective-permute-done | bytes 524320 | tf_op jit(solution)/shard_map/ppermute | solution.py:37
  51.4 4.1 %collective-permute-done.5 = bf16[128,512]{1,0:T(8,128)(2,1)S(1)} collective-permute-done((bf16[128,512]{1,0:T(8,128)(2,1)S(1)}, bf16[128,512]{1,0:T(8,128)(2,1)S(1)}, u32[]{:S(2)}, u32[]{:S(2)}) %collective-permute-start.5) | collective-permute-done | bytes 131104 | tf_op jit(solution)/shard_map/ppermute | solution.py:37
  55.6 4.3 %collective-permute-done.6.refs_2_ = bf16[512,512]{1,0:T(8,128)(2,1)S(1)} collective-permute-done((bf16[512,512]{1,0:T(8,128)(2,1)S(1)}, bf16[512,512]{1,0:T(8,128)(2,1)S(1)}, u32[]{:S(2)}, u32[]{:S(2)}) %collective-permute-start.6) | collective-permute-done | bytes 524320 | tf_op jit(solution)/shard_map/ppermute | solution.py:37
  60.7 3.0 %collective-permute-start.7 = (bf16[768,512]{1,0:T(8,128)(2,1)S(1)}, bf16[768,512]{1,0:T(8,128)(2,1)S(1)}, u32[]{:S(2)}, u32[]{:S(2)}) collective-permute-start(bf16[768,512]{1,0:T(8,128)(2,1)S(1)} %pad_maximum_fusion.wl0), channel_id=1, source_target_pairs={{0,128},{1,129},{2,130},{3,131},{4,132},{5,133},{6,134},{7,135},{8... | collective-permute-start | bytes 2359304 | tf_op jit(solution)/shard_map/ppermute | solution.py:37
  63.7 3.4 %collective-permute-start.9 = (bf16[768,512]{1,0:T(8,128)(2,1)S(1)}, bf16[768,512]{1,0:T(8,128)(2,1)S(1)}, u32[]{:S(2)}, u32[]{:S(2)}) collective-permute-start(bf16[768,512]{1,0:T(8,128)(2,1)S(1)} %pad_maximum_fusion.wl0), channel_id=1, source_target_pairs={{0,384},{1,385},{2,386},{3,387},{4,388},{5,389},{6,390},{7,391},{8... | collective-permute-start | bytes 2359304 | tf_op jit(solution)/shard_map/ppermute | solution.py:37
  67.2 5.5 %collective-permute-start.8 = (bf16[512,512]{1,0:T(8,128)(2,1)S(1)}, bf16[512,512]{1,0:T(8,128)(2,1)S(1)}, u32[]{:S(2)}, u32[]{:S(2)}) collective-permute-start(bf16[512,512]{1,0:T(8,128)(2,1)S(1)} %get-tuple-element.29.own), channel_id=1, source_target_pairs={{0,32},{1,33},{2,34},{3,35},{4,36},{5,37},{6,38},{7,39},{8,40},{9,... | collective-permute-start | bytes 1572872 | tf_op jit(solution)/shard_map/ppermute | solution.py:37
  77.7 15.1 %collective-permute-done.8.refs_3_ = bf16[512,512]{1,0:T(8,128)(2,1)S(1)} collective-permute-done((bf16[512,512]{1,0:T(8,128)(2,1)S(1)}, bf16[512,512]{1,0:T(8,128)(2,1)S(1)}, u32[]{:S(2)}, u32[]{:S(2)}) %collective-permute-start.8) | collective-permute-done | bytes 524320 | tf_op jit(solution)/shard_map/ppermute | solution.py:37
  97.1 4.6 %collective-permute-start.11 = (bf16[368,512]{1,0:T(8,128)(2,1)}, bf16[368,512]{1,0:T(8,128)(2,1)}, u32[]{:S(2)}, u32[]{:S(2)}) collective-permute-start(bf16[368,512]{1,0:T(8,128)(2,1)} %slice.29), channel_id=1, source_target_pairs={{0,384},{1,385},{2,386},{3,387},{4,388},{5,389},{6,390},{7,391},{8... | collective-permute-start | bytes 1130504 | tf_op jit(solution)/shard_map/ppermute | solution.py:37
  106.1 5.9 %first.1 = (f32[256,512]{1,0:T(8,128)S(1)}, f32[256,512]{1,0:T(8,128)S(1)}, f32[256,512]{1,0:T(8,128)S(1)}) custom-call(s32[4]{0:T(128)S(1)} %pad_add_fusion.place, s32[128,7]{1,0:T(8,128)S(1)} %copy.9.pattern, bf16[256,512]{1,0:T(8,128)(2,1)S(1)} %copy-done, bf16[512,512]{1,0:T(8,128)(2,1)S(1)} %get-tuple-element.29.own, bf16[512,512]{1,0:T(8,128)(2,1)S(1)} %copy-done.4, ...), custom_call_target="tpu_custom_call" | custom-call | flops 402653184 | bytes 4194304 | tf_op jit(solution)/shard_map/first/pallas_call | solution.py:143
  112.0 7.7 %collective-permute-done.12.refs_0_ = bf16[512,512]{1,0:T(8,128)(2,1)} collective-permute-done((bf16[512,512]{1,0:T(8,128)(2,1)S(1)}, bf16[512,512]{1,0:T(8,128)(2,1)}, u32[]{:S(2)}, u32[]{:S(2)}) %collective-permute-start.12) | collective-permute-done | bytes 524320 | tf_op jit(solution)/shard_map/ppermute | solution.py:37
  119.8 6.7 %last.1.mine = bf16[256,512]{1,0:T(8,128)(2,1)S(1)} custom-call(s32[4]{0:T(128)S(1)} %pad_add_fusion.place, s32[128,7]{1,0:T(8,128)S(1)} %copy.9.pattern, bf16[256,512]{1,0:T(8,128)(2,1)S(1)} %copy-done, f32[256,512]{1,0:T(8,128)S(1)} %get-tuple-element.31.top, f32[256,512]{1,0:T(8,128)S(1)} %get-tuple-element.32.total, ...), custom_call_target="tpu_custom_call" | custom-call | flops 402653184 | bytes 8388608 | tf_op jit(solution)/shard_map/last/pallas_call | solution.py:190
  129.1 6.6 %collective-permute-done.14.other = bf16[256,512]{1,0:T(8,128)(2,1)S(1)} collective-permute-done((bf16[256,512]{1,0:T(8,128)(2,1)S(1)}, bf16[256,512]{1,0:T(8,128)(2,1)S(1)}, u32[]{:S(2)}, u32[]{:S(2)}) %collective-permute-start.14) | collective-permute-done | bytes 262176 | tf_op jit(solution)/shard_map/ppermute | solution.py:37
  138.2 3.2 %collective-permute-start.15 = (bf16[4,256,512]{2,1,0:T(8,128)(2,1)S(1)}, bf16[4,256,512]{2,1,0:T(8,128)(2,1)S(1)}, u32[]{:S(2)}, u32[]{:S(2)}) collective-permute-start(bf16[4,256,512]{2,1,0:T(8,128)(2,1)S(1)} %get-tuple-element.36), channel_id=1, source_target_pairs={{0,1},{1,0},{2,3},{3,2},{4,5},{5,4},{6,7},{7,6},{8,9},{9,8},{10,11... | collective-permute-start | bytes 3145736 | tf_op jit(solution)/shard_map/ppermute | solution.py:37
  147.1 6.3 %collective-permute-start.17 = (bf16[256,512]{1,0:T(8,128)(2,1)S(1)}, bf16[256,512]{1,0:T(8,128)(2,1)S(1)}, u32[]{:S(2)}, u32[]{:S(2)}) collective-permute-start(bf16[256,512]{1,0:T(8,128)(2,1)S(1)} %get-tuple-element.40), channel_id=1, source_target_pairs={{0,2},{1,66},{2,4},{3,68},{4,6},{5,70},{6,0},{7,64},{8,10},{9,74},... | collective-permute-start | bytes 786440 | tf_op jit(solution)/shard_map/ppermute | solution.py:37
  153.4 6.4 %collective-permute-start.18 = (bf16[256,512]{1,0:T(8,128)(2,1)S(1)}, bf16[256,512]{1,0:T(8,128)(2,1)S(1)}, u32[]{:S(2)}, u32[]{:S(2)}) collective-permute-start(bf16[256,512]{1,0:T(8,128)(2,1)S(1)} %get-tuple-element.39), channel_id=1, source_target_pairs={{0,4},{1,68},{2,6},{3,70},{4,0},{5,64},{6,2},{7,66},{8,12},{9,76},... | collective-permute-start | bytes 786440 | tf_op jit(solution)/shard_map/ppermute | solution.py:37
  159.8 4.3 %collective-permute-start.19 = (bf16[256,512]{1,0:T(8,128)(2,1)S(1)}, bf16[256,512]{1,0:T(8,128)(2,1)S(1)}, u32[]{:S(2)}, u32[]{:S(2)}) collective-permute-start(bf16[256,512]{1,0:T(8,128)(2,1)S(1)} %get-tuple-element.38), channel_id=1, source_target_pairs={{0,6},{1,70},{2,0},{3,64},{4,2},{5,66},{6,4},{7,68},{8,14},{9,78},... | collective-permute-start | bytes 786440 | tf_op jit(solution)/shard_map/ppermute | solution.py:37
  164.1 13.9 %collective-permute-done.18 = bf16[256,512]{1,0:T(8,128)(2,1)S(1)} collective-permute-done((bf16[256,512]{1,0:T(8,128)(2,1)S(1)}, bf16[256,512]{1,0:T(8,128)(2,1)S(1)}, u32[]{:S(2)}, u32[]{:S(2)}) %collective-permute-start.18) | collective-permute-done | bytes 262176 | tf_op jit(solution)/shard_map/ppermute | solution.py:37
  178.1 3.5 %collective-permute-done.19 = bf16[256,512]{1,0:T(8,128)(2,1)S(1)} collective-permute-done((bf16[256,512]{1,0:T(8,128)(2,1)S(1)}, bf16[256,512]{1,0:T(8,128)(2,1)S(1)}, u32[]{:S(2)}, u32[]{:S(2)}) %collective-permute-start.19) | collective-permute-done | bytes 262176 | tf_op jit(solution)/shard_map/ppermute | solution.py:37
  (62 shorter events, 39.8 us)
Async XLA Ops:
  3.8 10.2 %collective-permute-start = (bf16[80,512]{1,0:T(8,128)(2,1)S(1)}, bf16[80,512]{1,0:T(8,128)(2,1)S(1)}, u32[]{:S(2)}, u32[]{:S(2)}) collective-permute-start(bf16[80,512]{1,0:T(8,128)(2,1)S(1)} %get-tuple-element.22), channel_id=1, source_target_pairs={{0,32},{1,33},{2,34},{3,35},{4,36},{5,37},{6,38},{7,39},{8,40},{9,... | collective-permute-start | bytes 245768 | tf_op jit(solution)/shard_map/ppermute | solution.py:37
  14.0 11.3 %collective-permute-start.1 = (bf16[160,512]{1,0:T(8,128)(2,1)S(1)}, bf16[160,512]{1,0:T(8,128)(2,1)S(1)}, u32[]{:S(2)}, u32[]{:S(2)}) collective-permute-start(bf16[160,512]{1,0:T(8,128)(2,1)S(1)} %pad_maximum_fusion.3), channel_id=1, source_target_pairs={{0,16},{1,17},{2,18},{3,19},{4,20},{5,21},{6,22},{7,23},{8,24},{9,... | collective-permute-start | bytes 491528 | tf_op jit(solution)/shard_map/ppermute | solution.py:37
  25.4 14.5 %collective-permute-start.2 = (bf16[320,512]{1,0:T(8,128)(2,1)S(1)}, bf16[320,512]{1,0:T(8,128)(2,1)S(1)}, u32[]{:S(2)}, u32[]{:S(2)}) collective-permute-start(bf16[320,512]{1,0:T(8,128)(2,1)S(1)} %pad_maximum_fusion.2), channel_id=1, source_target_pairs={{0,8},{1,9},{2,10},{3,11},{4,12},{5,13},{6,14},{7,15},{8,0},{9,1},... | collective-permute-start | bytes 983048 | tf_op jit(solution)/shard_map/ppermute | solution.py:37
  27.3 16.2 %collective-permute-start.3 = (bf16[512,512]{1,0:T(8,128)(2,1)S(1)}, bf16[512,512]{1,0:T(8,128)(2,1)S(1)}, u32[]{:S(2)}, u32[]{:S(2)}) collective-permute-start(bf16[512,512]{1,0:T(8,128)(2,1)S(1)} %get-tuple-element.29.own), channel_id=1, source_target_pairs={{0,64},{1,65},{2,66},{3,67},{4,68},{5,69},{6,70},{7,71},{8,72},{9,... | collective-permute-start | bytes 1572872 | tf_op jit(solution)/shard_map/ppermute | solution.py:37
  33.0 15.6 %collective-permute-start.4 = (bf16[512,512]{1,0:T(8,128)(2,1)S(1)}, bf16[512,512]{1,0:T(8,128)(2,1)S(1)}, u32[]{:S(2)}, u32[]{:S(2)}) collective-permute-start(bf16[512,512]{1,0:T(8,128)(2,1)S(1)} %get-tuple-element.29.own), channel_id=1, source_target_pairs={{0,256},{1,257},{2,258},{3,259},{4,260},{5,261},{6,262},{7,263},{8... | collective-permute-start | bytes 1572872 | tf_op jit(solution)/shard_map/ppermute | solution.py:37
  37.6 22.2 %collective-permute-start.6 = (bf16[512,512]{1,0:T(8,128)(2,1)S(1)}, bf16[512,512]{1,0:T(8,128)(2,1)S(1)}, u32[]{:S(2)}, u32[]{:S(2)}) collective-permute-start(bf16[512,512]{1,0:T(8,128)(2,1)S(1)} %get-tuple-element.29.own), channel_id=1, source_target_pairs={{0,128},{1,129},{2,130},{3,131},{4,132},{5,133},{6,134},{7,135},{8... | collective-permute-start | bytes 1572872 | tf_op jit(solution)/shard_map/ppermute | solution.py:37
  49.3 52.4 %copy-start.12 = (s32[128,7]{0,1:T(8,128)S(1)}, s32[128,7]{0,1:T(8,128)}, u32[]{:S(2)}) copy-start(s32[128,7]{0,1:T(8,128)} %param.11) | copy-start | bytes 10756
  49.4 52.6 %copy-start = (bf16[256,512]{1,0:T(8,128)(2,1)S(1)}, bf16[256,512]{1,0:T(8,128)(2,1)}, u32[]{:S(2)}) copy-start(bf16[256,512]{1,0:T(8,128)(2,1)} %q.3) | copy-start | bytes 786436
  49.4 6.1 %collective-permute-start.5 = (bf16[128,512]{1,0:T(8,128)(2,1)S(1)}, bf16[128,512]{1,0:T(8,128)(2,1)S(1)}, u32[]{:S(2)}, u32[]{:S(2)}) collective-permute-start(bf16[128,512]{1,0:T(8,128)(2,1)S(1)} %bitcast.15), channel_id=1, source_target_pairs={{0,64},{1,65},{2,66},{3,67},{4,68},{5,69},{6,70},{7,71},{8,72},{9,... | collective-permute-start | bytes 393224 | tf_op jit(solution)/shard_map/ppermute | solution.py:37
  60.7 33.0 %collective-permute-start.7 = (bf16[768,512]{1,0:T(8,128)(2,1)S(1)}, bf16[768,512]{1,0:T(8,128)(2,1)S(1)}, u32[]{:S(2)}, u32[]{:S(2)}) collective-permute-start(bf16[768,512]{1,0:T(8,128)(2,1)S(1)} %pad_maximum_fusion.wl0), channel_id=1, source_target_pairs={{0,128},{1,129},{2,130},{3,131},{4,132},{5,133},{6,134},{7,135},{8... | collective-permute-start | bytes 2359304 | tf_op jit(solution)/shard_map/ppermute | solution.py:37
  63.7 32.6 %collective-permute-start.9 = (bf16[768,512]{1,0:T(8,128)(2,1)S(1)}, bf16[768,512]{1,0:T(8,128)(2,1)S(1)}, u32[]{:S(2)}, u32[]{:S(2)}) collective-permute-start(bf16[768,512]{1,0:T(8,128)(2,1)S(1)} %pad_maximum_fusion.wl0), channel_id=1, source_target_pairs={{0,384},{1,385},{2,386},{3,387},{4,388},{5,389},{6,390},{7,391},{8... | collective-permute-start | bytes 2359304 | tf_op jit(solution)/shard_map/ppermute | solution.py:37
  67.2 25.7 %collective-permute-start.8 = (bf16[512,512]{1,0:T(8,128)(2,1)S(1)}, bf16[512,512]{1,0:T(8,128)(2,1)S(1)}, u32[]{:S(2)}, u32[]{:S(2)}) collective-permute-start(bf16[512,512]{1,0:T(8,128)(2,1)S(1)} %get-tuple-element.29.own), channel_id=1, source_target_pairs={{0,32},{1,33},{2,34},{3,35},{4,36},{5,37},{6,38},{7,39},{8,40},{9,... | collective-permute-start | bytes 1572872 | tf_op jit(solution)/shard_map/ppermute | solution.py:37
  72.7 47.1 %collective-permute-start.12 = (bf16[512,512]{1,0:T(8,128)(2,1)S(1)}, bf16[512,512]{1,0:T(8,128)(2,1)}, u32[]{:S(2)}, u32[]{:S(2)}) collective-permute-start(bf16[512,512]{1,0:T(8,128)(2,1)S(1)} %get-tuple-element.29.own), channel_id=1, source_target_pairs={{0,16},{1,17},{2,18},{3,19},{4,20},{5,21},{6,22},{7,23},{8,24},{9,... | collective-permute-start | bytes 1572872 | tf_op jit(solution)/shard_map/ppermute | solution.py:37
  75.5 44.3 %collective-permute-start.13 = (bf16[512,512]{1,0:T(8,128)(2,1)S(1)}, bf16[512,512]{1,0:T(8,128)(2,1)}, u32[]{:S(2)}, u32[]{:S(2)}) collective-permute-start(bf16[512,512]{1,0:T(8,128)(2,1)S(1)} %get-tuple-element.29.own), channel_id=1, source_target_pairs={{0,8},{1,9},{2,10},{3,11},{4,12},{5,13},{6,14},{7,15},{8,0},{9,1},... | collective-permute-start | bytes 1572872 | tf_op jit(solution)/shard_map/ppermute | solution.py:37
  94.4 25.4 %collective-permute-start.10 = (bf16[400,512]{1,0:T(8,128)(2,1)}, bf16[400,512]{1,0:T(8,128)(2,1)}, u32[]{:S(2)}, u32[]{:S(2)}) collective-permute-start(bf16[400,512]{1,0:T(8,128)(2,1)} %slice.22), channel_id=1, source_target_pairs={{0,128},{1,129},{2,130},{3,131},{4,132},{5,133},{6,134},{7,135},{8... | collective-permute-start | bytes 1228808 | tf_op jit(solution)/shard_map/ppermute | solution.py:37
  97.1 22.7 %collective-permute-start.11 = (bf16[368,512]{1,0:T(8,128)(2,1)}, bf16[368,512]{1,0:T(8,128)(2,1)}, u32[]{:S(2)}, u32[]{:S(2)}) collective-permute-start(bf16[368,512]{1,0:T(8,128)(2,1)} %slice.29), channel_id=1, source_target_pairs={{0,384},{1,385},{2,386},{3,387},{4,388},{5,389},{6,390},{7,391},{8... | collective-permute-start | bytes 1130504 | tf_op jit(solution)/shard_map/ppermute | solution.py:37
  102.0 1.0 copy-start.2
  103.0 1.0 copy-start.4
  126.5 9.3 %collective-permute-start.14 = (bf16[256,512]{1,0:T(8,128)(2,1)S(1)}, bf16[256,512]{1,0:T(8,128)(2,1)S(1)}, u32[]{:S(2)}, u32[]{:S(2)}) collective-permute-start(bf16[256,512]{1,0:T(8,128)(2,1)S(1)} %last.1.mine), channel_id=1, source_target_pairs={{0,64},{1,65},{2,66},{3,67},{4,68},{5,69},{6,70},{7,71},{8,72},{9,... | collective-permute-start | bytes 786440 | tf_op jit(solution)/shard_map/ppermute | solution.py:37
  138.2 5.5 %collective-permute-start.15 = (bf16[4,256,512]{2,1,0:T(8,128)(2,1)S(1)}, bf16[4,256,512]{2,1,0:T(8,128)(2,1)S(1)}, u32[]{:S(2)}, u32[]{:S(2)}) collective-permute-start(bf16[4,256,512]{2,1,0:T(8,128)(2,1)S(1)} %get-tuple-element.36), channel_id=1, source_target_pairs={{0,1},{1,0},{2,3},{3,2},{4,5},{5,4},{6,7},{7,6},{8,9},{9,8},{10,11... | collective-permute-start | bytes 3145736 | tf_op jit(solution)/shard_map/ppermute | solution.py:37
  144.2 19.9 %collective-permute-start.16 = (bf16[256,512]{1,0:T(8,128)(2,1)S(1)}, bf16[256,512]{1,0:T(8,128)(2,1)S(1)}, u32[]{:S(2)}, u32[]{:S(2)}) collective-permute-start(bf16[256,512]{1,0:T(8,128)(2,1)S(1)} %get-tuple-element.37), channel_id=1, source_target_pairs={{0,0},{1,64},{2,2},{3,66},{4,4},{5,68},{6,6},{7,70},{8,8},{9,72},{... | collective-permute-start | bytes 786440 | tf_op jit(solution)/shard_map/ppermute | solution.py:37
  147.1 17.0 %collective-permute-start.17 = (bf16[256,512]{1,0:T(8,128)(2,1)S(1)}, bf16[256,512]{1,0:T(8,128)(2,1)S(1)}, u32[]{:S(2)}, u32[]{:S(2)}) collective-permute-start(bf16[256,512]{1,0:T(8,128)(2,1)S(1)} %get-tuple-element.40), channel_id=1, source_target_pairs={{0,2},{1,66},{2,4},{3,68},{4,6},{5,70},{6,0},{7,64},{8,10},{9,74},... | collective-permute-start | bytes 786440 | tf_op jit(solution)/shard_map/ppermute | solution.py:37
  153.4 24.6 %collective-permute-start.18 = (bf16[256,512]{1,0:T(8,128)(2,1)S(1)}, bf16[256,512]{1,0:T(8,128)(2,1)S(1)}, u32[]{:S(2)}, u32[]{:S(2)}) collective-permute-start(bf16[256,512]{1,0:T(8,128)(2,1)S(1)} %get-tuple-element.39), channel_id=1, source_target_pairs={{0,4},{1,68},{2,6},{3,70},{4,0},{5,64},{6,2},{7,66},{8,12},{9,76},... | collective-permute-start | bytes 786440 | tf_op jit(solution)/shard_map/ppermute | solution.py:37
  159.8 21.8 %collective-permute-start.19 = (bf16[256,512]{1,0:T(8,128)(2,1)S(1)}, bf16[256,512]{1,0:T(8,128)(2,1)S(1)}, u32[]{:S(2)}, u32[]{:S(2)}) collective-permute-start(bf16[256,512]{1,0:T(8,128)(2,1)S(1)} %get-tuple-element.38), channel_id=1, source_target_pairs={{0,6},{1,70},{2,0},{3,64},{4,2},{5,66},{6,4},{7,68},{8,14},{9,78},... | collective-permute-start | bytes 786440 | tf_op jit(solution)/shard_map/ppermute | solution.py:37
  (9 other events, 7.9 us)

commit v2 on v1

v2 whole, which is shorter than its diff:
```python
import functools

import jax
import jax.numpy as jnp
from jax import lax
from jax.experimental import pallas as pl
from jax.experimental.pallas import tpu as pltpu
from jax.sharding import PartitionSpec as P

HD = 128
BLK = 128
NX, NZL, NY, NZH, NC = 4, 2, 8, 4, 2
WROWS = 64
LROWS = 16
UNIT = WROWS + LROWS
HALF = 400
COST = 64
AXES = ("ctx", "head")
SCALE = HD**-0.5
F32 = jnp.float32
BF16 = jnp.bfloat16
VLIM = 16 << 20
HBM = pl.BlockSpec(memory_space=pltpu.HBM)
ANY = pl.BlockSpec(memory_space=pl.ANY)
SMEM = pl.BlockSpec(memory_space=pltpu.SMEM)
VMEM = pl.BlockSpec(memory_space=pltpu.VMEM)


def coords(i):
    ctx, head = divmod(i, NZH * NC)
    x, r = divmod(ctx, NZL * NY)
    zl, y = divmod(r, NY)
    zh, c = divmod(head, NC)
    return x, zl, y, zh, c


def flat(x, zl, y, zh, c):
    return ((x * NZL + zl) * NY + y) * (NZH * NC) + zh * NC + c


def send(a, to):
    pairs = [(i, flat(*to(*coords(i)))) for i in range(NX * NZL * NY * NZH * NC)]
    return lax.ppermute(a, AXES, pairs)


def xor(level):
    def to(x, zl, y, zh, c):
        ctx = ((x * NZL + zl) * NY + y) ^ (1 << level)
        x, r = divmod(ctx, NZL * NY)
        zl, y = divmod(r, NY)
        return x, zl, y, zh, c

    return to


def after(a, far, levels):
    if levels:
        a, done = lax.optimization_barrier((a, [far[l] for l in levels]))
        far.update(zip(levels, done, strict=True))
    return a


def in_hbm(a):
    return pltpu.with_memory_space_constraint(a, pltpu.HBM)


def params():
    return pltpu.CompilerParams(vmem_limit_bytes=VLIM)


def dot_nt(a, b):
    return lax.dot_general(a, b, (((1,), (1,)), ((), ())), preferred_element_type=F32)


def prepare_kernel(pool, keys, values, weight, kv, unit, pool_v, sem):
    copies = [
        pltpu.make_async_copy(weight, unit.at[pl.ds(0, WROWS)], sem.at[0]),
        pltpu.make_async_copy(pool, pool_v, sem.at[1]),
        pltpu.make_async_copy(keys, kv.at[pl.ds(0, 256)], sem.at[2]),
        pltpu.make_async_copy(values, kv.at[pl.ds(256, 256)], sem.at[3]),
    ]
    for copy in copies:
        copy.start()
    for copy in copies:
        copy.wait()
    pooled = [
        jnp.dot(pool_v[...], kv[r : r + 256, :], preferred_element_type=F32) for r in (0, 256)
    ]
    unit[WROWS:UNIT, :] = jnp.concatenate(pooled, axis=0).astype(BF16)


def prepare(pool, keys, values, weight):
    return pl.pallas_call(
        prepare_kernel,
        out_shape=(
            jax.ShapeDtypeStruct((512, 512), BF16),
            jax.ShapeDtypeStruct((UNIT, 512), BF16),
        ),
        in_specs=[HBM] * 4,
        out_specs=(VMEM,) * 2,
        scratch_shapes=[
            pltpu.VMEM((8, 256), BF16),
            pltpu.SemaphoreType.DMA((4,)),
        ],
        compiler_params=params(),
        name="prepare",
    )(*[in_hbm(a) for a in (pool, keys, values, weight)])


def softmax_step(state, q, ks, vs):
    scores = [dot_nt(q, k) * SCALE for k in ks]
    top = functools.reduce(jnp.maximum, [jnp.max(s, axis=1, keepdims=True) for s in scores])
    if state is not None:
        old_top, old_sum, old_acc = state
        top = jnp.maximum(top, old_top)
    weights = [jnp.exp(s - top) for s in scores]
    total = sum(jnp.sum(w, axis=1, keepdims=True) for w in weights)
    acc = sum(
        jnp.dot(w.astype(BF16), v, preferred_element_type=F32)
        for w, v in zip(weights, vs, strict=True)
    )
    if state is not None:
        fade = jnp.exp(old_top - top)
        total = total + old_sum * fade
        acc = acc + old_acc * fade
    return top, total, acc


def mark_rows(refs):
    rows = [b * UNIT + WROWS for b in range(NY)] + [NY * UNIT + b * LROWS for b in range(NY)]
    found = [(r, at) for r in refs[:3] for at in rows]
    found += [(refs[3], at) for at in rows if at < HALF]
    return found + [(refs[4], at - HALF) for at in rows if at >= HALF]


def landmarks(marks, cols):
    rows = marks[:, cols].astype(F32)
    groups = [rows[g * 8 : g * 8 + 8] for g in range(2 * NX * 16)]
    ks = jnp.concatenate(groups[0::2], axis=0)
    vs = jnp.concatenate(groups[1::2], axis=0)
    return ks.astype(BF16), vs.astype(BF16)


def attend_kernel(levels, own, carry, mark, final, place, pattern, q, *refs):
    refs = list(refs)
    own_ref = refs.pop(0) if own else None
    state_refs = [refs.pop(0) for _ in range(3)] if carry else None
    mark_refs = [refs.pop(0) for _ in range(5)] if mark else []
    far = [refs.pop(0) for _ in levels]
    outs = [refs.pop(0) for _ in range(1 if final else 3)]
    far_v = refs.pop(0) if levels else None
    mark_v = refs.pop(0) if mark else None
    sem = refs.pop(0)
    mark_sem = refs.pop(0) if mark else None
    copies = [pltpu.make_async_copy(r, far_v.at[i], sem.at[i]) for i, r in enumerate(far)]
    if mark:
        for i, (r, at) in enumerate(mark_rows(mark_refs)):
            dst = mark_v.at[pl.ds(i * LROWS, LROWS), :]
            copies.append(pltpu.make_async_copy(r.at[pl.ds(at, LROWS), :], dst, mark_sem.at[i]))
    for copy in copies:
        copy.start()
    for copy in copies:
        copy.wait()
    for h in range(4):
        cols = slice(h * HD, (h + 1) * HD)
        marks = landmarks(mark_v, cols) if mark else None
        for j in range(2):
            rows = slice(j * BLK, (j + 1) * BLK)
            ks, vs = [], []
            if own:
                ks.append(own_ref[0:256, cols])
                vs.append(own_ref[256:512, cols])
            if mark:
                ks.append(marks[0])
                vs.append(marks[1])
            for i, level in enumerate(levels):
                at = pl.multiple_of((pattern[1 + level, place[3] + j] & 1) * BLK, BLK)
                ks.append(far_v[i, pl.ds(at, BLK), cols])
                vs.append(far_v[i, pl.ds(256 + at, BLK), cols])
            state = None
            if carry:
                top, total, acc = state_refs
                first = slice(h * HD, h * HD + 1)
                state = (top[rows, first], total[rows, first], acc[rows, cols])
            m, s, a = softmax_step(state, q[rows, cols], ks, vs)
            if final:
                outs[0][rows, cols] = (a / s).astype(BF16)
            else:
                outs[0][rows, cols] = jnp.broadcast_to(m, (BLK, HD))
                outs[1][rows, cols] = jnp.broadcast_to(s, (BLK, HD))
                outs[2][rows, cols] = a


def attend(place, pattern, q, levels, far, own=None, state=None, mark=None, final=False, cost=1):
    args, specs = [place, pattern, q], [SMEM, SMEM, VMEM]
    if own is not None:
        args, specs = [*args, own], [*specs, VMEM]
    if state is not None:
        args, specs = [*args, *state], specs + [VMEM] * 3
    if mark is not None:
        args, specs = [*args, *mark], specs + [ANY] * 5
    args += [in_hbm(far[l]) for l in levels]
    specs += [HBM] * len(levels)
    scratch = [pltpu.VMEM((len(levels), 512, 512), BF16)] if levels else []
    if mark is not None:
        scratch.append(pltpu.VMEM((NX * 16 * LROWS, 512), BF16))
    scratch.append(pltpu.SemaphoreType.DMA((len(levels) + 1,)))
    if mark is not None:
        scratch.append(pltpu.SemaphoreType.DMA((NX * 16,)))
    count = 128 * len(levels) + 256 * (own is not None) + 512 * (mark is not None)
    return pl.pallas_call(
        functools.partial(
            attend_kernel, levels, own is not None, state is not None, mark is not None, final
        ),
        out_shape=jax.ShapeDtypeStruct((256, 512), BF16)
        if final
        else (jax.ShapeDtypeStruct((256, 512), F32),) * 3,
        in_specs=specs,
        out_specs=VMEM if final else (VMEM,) * 3,
        scratch_shapes=scratch,
        compiler_params=params(),
        name="attend",
        cost_estimate=pl.CostEstimate(
            flops=cost * 4 * 256 * 512 * count,
            bytes_accessed=4 << 20,
            transcendentals=1024 * count,
        ),
    )(*args)


def project_kernel(place, mine, other, w0, w1, w3, w2a, w2b, keep, give, w_v, sem):
    x, zh, same, y = place[0], place[1], place[2], place[4]
    chunks = ((0, ((w0, 0, 768),)), (1, ((w1, 0, 768),)), (3, ((w3, 0, 768),)))
    chunks += ((2, ((w2a, 0, HALF), (w2b, HALF, 768))),)
    copies = []
    for i, (_, pieces) in enumerate(chunks):
        for p in range(NY):
            at = y ^ (4 * (p & 1) + (p & 2) + (p >> 2))
            dst = w_v.at[i, pl.ds(pl.multiple_of(at * WROWS, WROWS), WROWS), :]
            [src] = [
                r.at[pl.ds(p * UNIT - lo, WROWS), :] for r, lo, hi in pieces if lo <= p * UNIT < hi
            ]
            copies.append(pltpu.make_async_copy(src, dst, sem.at[i * NY + p]))
    for copy in copies:
        copy.start()
    swap = same == 0
    a, b = mine[...], other[...]
    kept = jnp.where(swap, b, a)
    given = jnp.where(swap, a, b)
    for i, (shift, _) in enumerate(chunks):
        for copy in copies[i * NY : (i + 1) * NY]:
            copy.wait()
        d = (x + 2 * NX - shift - zh) & 3
        give[d] = dot_nt(given, w_v[i]).astype(BF16)
        keep[d] = dot_nt(kept, w_v[i])


def project(place, mine, other, wl):
    return pl.pallas_call(
        project_kernel,
        out_shape=(
            jax.ShapeDtypeStruct((4, 256, 512), F32),
            jax.ShapeDtypeStruct((4, 256, 512), BF16),
        ),
        in_specs=[SMEM] + [VMEM] * 2 + [ANY] * 5,
        out_specs=(VMEM,) * 2,
        scratch_shapes=[
            pltpu.VMEM((NX, NY * WROWS, 512), BF16),
            pltpu.SemaphoreType.DMA((NX * NY,)),
        ],
        compiler_params=params(),
        name="project",
        cost_estimate=pl.CostEstimate(
            flops=2 * 512 * 512 * 2048, bytes_accessed=6 << 20, transcendentals=0
        ),
    )(place, mine, other, *wl)


def join_kernel(a, b, out):
    n = a.shape[0]
    out[0:n, :] = a[...]
    out[n:, :] = b[...]


def join(a, b):
    return pl.pallas_call(
        join_kernel,
        out_shape=jax.ShapeDtypeStruct((a.shape[0] + b.shape[0], 512), BF16),
        in_specs=[VMEM] * 2,
        out_specs=VMEM,
        compiler_params=params(),
        name="join",
    )(a, b)


def pick_kernel(a, out):
    for p in range(NY):
        out[p * LROWS : (p + 1) * LROWS, :] = a[p * UNIT + WROWS : (p + 1) * UNIT, :]


def pick(a):
    return pl.pallas_call(
        pick_kernel,
        out_shape=jax.ShapeDtypeStruct((NY * LROWS, 512), BF16),
        in_specs=[VMEM],
        out_specs=VMEM,
        compiler_params=params(),
        name="pick",
    )(a)


def combine_kernel(keep, got, *outs):
    for d in range(4):
        outs[d][...] = (keep[d] + got[d].astype(F32)).astype(BF16)


def combine(keep, got):
    return pl.pallas_call(
        combine_kernel,
        out_shape=(jax.ShapeDtypeStruct((256, 512), BF16),) * 4,
        in_specs=[VMEM] * 2,
        out_specs=(VMEM,) * 4,
        compiler_params=params(),
        name="combine",
    )(keep, got)


def along_x(k):
    return lambda x, zl, y, zh, c: ((x + k) % NX, zl, y, zh, c)


def on_device(queries, keys, values, pool_weight, out_weight, pattern):
    ctx, head = lax.axis_index("ctx"), lax.axis_index("head")
    zl, c = (ctx >> 3) & 1, head & 1
    place = jnp.stack([ctx >> 4, head >> 1, (zl == c).astype(jnp.int32), ctx * 2, ctx & 7])

    kv, wl = prepare(pool_weight, keys, values, out_weight.T)
    step = functools.partial(attend, place, pattern.T, queries)
    far = {level: send(kv, xor(level)) for level in (5, 3)}
    wl = join(wl, send(wl, xor(2)))
    kv, wl = lax.optimization_barrier((kv, wl))
    far.update({level: send(kv, xor(level)) for level in (4, 0)})
    wl = join(wl, send(wl, xor(1)))
    wl = after(wl, far, (5, 3))
    kv, wl = lax.optimization_barrier((kv, wl))
    far.update({level: send(kv, xor(level)) for level in (2, 1)})
    wl = join(wl, send(wl, xor(0)))
    marks = after(pick(wl), far, (4, 0))
    state = step((5, 3, 4, 0), far, own=kv)
    wl = join(wl, send(marks, xor(3)))
    wl1, wl3 = send(wl, along_x(1)), send(wl, along_x(-1))
    state = step((2,), far, state=state, cost=COST)
    wl1, wl3, state = lax.optimization_barrier((wl1, wl3, state))
    wl2a, wl2b = send(wl1[:HALF], along_x(1)), send(wl3[HALF:], along_x(-1))
    pieces = (wl, wl1, wl3, wl2a, wl2b)
    state = step((1,), far, state=state, cost=COST)
    mine = step((), far, state=state, mark=pieces, final=True)
    other = send(mine, xor(3))
    keep, give = project(place, mine, other, pieces)
    got = send(give, lambda x, zl, y, zh, c: (x, zl, y, zh, 1 - c))
    part = combine(keep, got)
    total = 0.0
    for d in range(4):
        total += send(
            part[d], lambda x, zl, y, zh, c: (x, c, y, (zh + d) % NZH, zl)
        ).astype(F32)
    return total.astype(BF16)


def solution(mesh):
    in_specs = (
        P("ctx", "head"),
        P("ctx", "head"),
        P("ctx", "head"),
        P("ctx", None),
        P("head", "ctx"),
        P(),
    )
    return jax.shard_map(
        on_device, mesh=mesh, in_specs=in_specs, out_specs=P("ctx", "head"), check_vma=False
    )
```

time: 183 us -> 167 us (0.913)
  waiting for transfers between devices: 72.8 us -> 51.9 us
  local copies, waits for them, and re-layouts: 12.6 us -> 0.17 us
  Pallas kernels: 15.2 us -> 26.6 us
  starting transfers between devices: 79.7 us -> 85.6 us
    ppermute x20, waiting for transfers between devices: 72.8 us -> 51.9 us  [send(): return lax.ppermute(a, AXES, pairs)]
    unnamed x28 -> x12, local copies, waits for them, and re-layouts: 11 us -> 0.03 us
    pallas_call x2 -> x10, Pallas kernels: 12.6 us -> 19.8 us  [the longest x4 19.5 us: attend(): pl.pallas_call(functools.partial(attend_kernel, levels, own is not None,...]
    ppermute x20, starting transfers between devices: 79.7 us -> 85.6 us  [send(): return lax.ppermute(a, AXES, pairs)]
    pallas_call x1, Pallas kernels: 2.43 us -> 5.51 us  [project(): pl.pallas_call(project_kernel, out_shape=(jax.ShapeDtypeStruct((4, 256, 5...]
  transfers between devices with their start and end apart: 20 -> 20, of which waited for: 12 -> 10; matrix products, arithmetic and copies ran while one was open for 1% -> 0% of each run, Pallas kernels for 3% -> 8%
where the time goes in v2:
time: 167 us; the launch traced here: 166 us
  starting transfers between devices  85.6 us (51%)
  waiting for transfers between devices  51.9 us (31%)
  Pallas kernels  26.6 us (16%)
    ppermute x20, starting transfers between devices, send(): return lax.ppermute(a, AXES, pairs)  85.6 us
    ppermute x20, waiting for transfers between devices, send(): return lax.ppermute(a, AXES, pairs)  51.9 us
    pallas_call x4, Pallas kernels, attend(): pl.pallas_call(functools.partial(attend_kernel, levels, own is not None,...  19.5 us
    pallas_call x1, Pallas kernels, project(): pl.pallas_call(project_kernel, out_shape=(jax.ShapeDtypeStruct((4, 256, 5...  5.51 us
  transfers between devices with their start and end apart: 20, of which 10 were waited for; matrix products, arithmetic and copies ran while one was open for 0% of the time, Pallas kernels for 8%

profile of v2, /device:TPU:1, one launch (start us, length us, event | category | flops | bytes accessed | tf_op | source)
XLA Modules:
  0.0 165.5 jit_solution(3071534831386506210)
XLA Ops:
  1.3 4.8 %collective-permute-start.3 = (bf16[512,512]{1,0:T(8,128)(2,1)S(1)}, bf16[512,512]{1,0:T(8,128)(2,1)S(1)}, u32[]{:S(2)}, u32[]{:S(2)}) collective-permute-start(bf16[512,512]{1,0:T(8,128)(2,1)S(1)} %get-tuple-element.44.refs_0_), channel_id=1, source_target_pairs={{0,64},{1,65},{2,66},{3,67},{4,68},{5,69},{6,70},{7,71},{8,72},{9,... | collective-permute-start | bytes 1572872 | tf_op jit(solution)/shard_map/ppermute | solution.py:43
  6.1 4.7 %collective-permute-start.2 = (bf16[512,512]{1,0:T(8,128)(2,1)S(1)}, bf16[512,512]{1,0:T(8,128)(2,1)S(1)}, u32[]{:S(2)}, u32[]{:S(2)}) collective-permute-start(bf16[512,512]{1,0:T(8,128)(2,1)S(1)} %get-tuple-element.44.refs_0_), channel_id=1, source_target_pairs={{0,256},{1,257},{2,258},{3,259},{4,260},{5,261},{6,262},{7,263},{8... | collective-permute-start | bytes 1572872 | tf_op jit(solution)/shard_map/ppermute | solution.py:43
  10.8 7.5 %collective-permute-start = (bf16[80,512]{1,0:T(8,128)(2,1)S(1)}, bf16[80,512]{1,0:T(8,128)(2,1)S(1)}, u32[]{:S(2)}, u32[]{:S(2)}) collective-permute-start(bf16[80,512]{1,0:T(8,128)(2,1)S(1)} %get-tuple-element.38.a), channel_id=1, source_target_pairs={{0,32},{1,33},{2,34},{3,35},{4,36},{5,37},{6,38},{7,39},{8,40},{9,... | collective-permute-start | bytes 245768 | tf_op jit(solution)/shard_map/ppermute | solution.py:43
  25.6 4.9 %collective-permute-start.1 = (bf16[160,512]{1,0:T(8,128)(2,1)S(1)}, bf16[160,512]{1,0:T(8,128)(2,1)S(1)}, u32[]{:S(2)}, u32[]{:S(2)}) collective-permute-start(bf16[160,512]{1,0:T(8,128)(2,1)S(1)} %join.4.a), channel_id=1, source_target_pairs={{0,16},{1,17},{2,18},{3,19},{4,20},{5,21},{6,22},{7,23},{8,24},{9,... | collective-permute-start | bytes 491528 | tf_op jit(solution)/shard_map/ppermute | solution.py:43
  30.5 4.4 %collective-permute-done.1.b = bf16[160,512]{1,0:T(8,128)(2,1)S(1)} collective-permute-done((bf16[160,512]{1,0:T(8,128)(2,1)S(1)}, bf16[160,512]{1,0:T(8,128)(2,1)S(1)}, u32[]{:S(2)}, u32[]{:S(2)}) %collective-permute-start.1) | collective-permute-done | bytes 163872 | tf_op jit(solution)/shard_map/ppermute | solution.py:43
  35.0 8.7 %collective-permute-start.4 = (bf16[320,512]{1,0:T(8,128)(2,1)S(1)}, bf16[320,512]{1,0:T(8,128)(2,1)S(1)}, u32[]{:S(2)}, u32[]{:S(2)}) collective-permute-start(bf16[320,512]{1,0:T(8,128)(2,1)S(1)} %join.5.a), channel_id=1, source_target_pairs={{0,8},{1,9},{2,10},{3,11},{4,12},{5,13},{6,14},{7,15},{8,0},{9,1},... | collective-permute-start | bytes 983048 | tf_op jit(solution)/shard_map/ppermute | solution.py:43
  45.6 3.6 %collective-permute-done.4.b = bf16[320,512]{1,0:T(8,128)(2,1)S(1)} collective-permute-done((bf16[320,512]{1,0:T(8,128)(2,1)S(1)}, bf16[320,512]{1,0:T(8,128)(2,1)S(1)}, u32[]{:S(2)}, u32[]{:S(2)}) %collective-permute-start.4) | collective-permute-done | bytes 327712 | tf_op jit(solution)/shard_map/ppermute | solution.py:43
  51.4 3.9 %collective-permute-done.7.b = bf16[128,512]{1,0:T(8,128)(2,1)S(1)} collective-permute-done((bf16[128,512]{1,0:T(8,128)(2,1)S(1)}, bf16[128,512]{1,0:T(8,128)(2,1)S(1)}, u32[]{:S(2)}, u32[]{:S(2)}) %collective-permute-start.7) | collective-permute-done | bytes 131104 | tf_op jit(solution)/shard_map/ppermute | solution.py:43
  55.4 4.2 %collective-permute-start.9 = (bf16[768,512]{1,0:T(8,128)(2,1)S(1)}, bf16[768,512]{1,0:T(8,128)(2,1)S(1)}, u32[]{:S(2)}, u32[]{:S(2)}) collective-permute-start(bf16[768,512]{1,0:T(8,128)(2,1)S(1)} %join.7.refs_3_.w0), channel_id=1, source_target_pairs={{0,384},{1,385},{2,386},{3,387},{4,388},{5,389},{6,390},{7,391},{8... | collective-permute-start | bytes 2359304 | tf_op jit(solution)/shard_map/ppermute | solution.py:43
  63.6 5.2 %attend.4 = (f32[256,512]{1,0:T(8,128)S(1)}, f32[256,512]{1,0:T(8,128)S(1)}, f32[256,512]{1,0:T(8,128)S(1)}) custom-call(s32[5]{0:T(128)S(1)} %stack.27.place, s32[7,128]{1,0:T(8,128)S(1)} %bitcast.7, bf16[256,512]{1,0:T(8,128)(2,1)S(1)} %copy-done, bf16[512,512]{1,0:T(8,128)(2,1)S(1)} %get-tuple-element.44.refs_0_, bf16[512,512]{1,0:T(8,128)(2,1)} %copy-done.3, ...), custom_call_target="tpu_custom_call" | custom-call | flops 402653184 | bytes 4194304 | tf_op jit(solution)/shard_map/attend/pallas_call | solution.py:211
  68.7 5.9 %collective-permute-done.10.refs_3_ = bf16[512,512]{1,0:T(8,128)(2,1)} collective-permute-done((bf16[512,512]{1,0:T(8,128)(2,1)S(1)}, bf16[512,512]{1,0:T(8,128)(2,1)}, u32[]{:S(2)}, u32[]{:S(2)}) %collective-permute-start.10) | collective-permute-done | bytes 524320 | tf_op jit(solution)/shard_map/ppermute | solution.py:43
  74.6 4.3 %attend.5 = (f32[256,512]{1,0:T(8,128)S(1)}, f32[256,512]{1,0:T(8,128)S(1)}, f32[256,512]{1,0:T(8,128)S(1)}) custom-call(s32[5]{0:T(128)S(1)} %stack.27.place, s32[7,128]{1,0:T(8,128)S(1)} %bitcast.8, bf16[256,512]{1,0:T(8,128)(2,1)S(1)} %copy-done, f32[256,512]{1,0:T(8,128)S(1)} %get-tuple-element.49.refs_0_, f32[256,512]{1,0:T(8,128)S(1)} %get-tuple-element.50.refs_1_, ...), custom_call_target="tpu_custom_call" | custom-call | flops 4294967296 | bytes 4194304 | tf_op jit(solution)/shard_map/attend/pallas_call | solution.py:211
  81.1 4.5 %collective-permute-start.13 = (bf16[368,512]{1,0:T(8,128)(2,1)S(1)}, bf16[368,512]{1,0:T(8,128)(2,1)S(1)}, u32[]{:S(2)}, u32[]{:S(2)}) collective-permute-start(bf16[368,512]{1,0:T(8,128)(2,1)S(1)} %slice.7), channel_id=1, source_target_pairs={{0,384},{1,385},{2,386},{3,387},{4,388},{5,389},{6,390},{7,391},{8... | collective-permute-start | bytes 1130504 | tf_op jit(solution)/shard_map/ppermute | solution.py:43
  85.6 7.4 %collective-permute-done.11.refs_3_ = bf16[512,512]{1,0:T(8,128)(2,1)} collective-permute-done((bf16[512,512]{1,0:T(8,128)(2,1)S(1)}, bf16[512,512]{1,0:T(8,128)(2,1)}, u32[]{:S(2)}, u32[]{:S(2)}) %collective-permute-start.11) | collective-permute-done | bytes 524320 | tf_op jit(solution)/shard_map/ppermute | solution.py:43
  93.0 4.3 %attend.6 = (f32[256,512]{1,0:T(8,128)S(1)}, f32[256,512]{1,0:T(8,128)S(1)}, f32[256,512]{1,0:T(8,128)S(1)}) custom-call(s32[5]{0:T(128)S(1)} %stack.27.place, s32[7,128]{1,0:T(8,128)S(1)} %bitcast.9, bf16[256,512]{1,0:T(8,128)(2,1)S(1)} %copy-done, f32[256,512]{1,0:T(8,128)S(1)} %get-tuple-element.55.refs_0_, f32[256,512]{1,0:T(8,128)S(1)} %get-tuple-element.56.refs_1_, ...), custom_call_target="tpu_custom_call" | custom-call | flops 4294967296 | bytes 4194304 | tf_op jit(solution)/shard_map/attend/pallas_call | solution.py:211
  97.3 5.7 %attend.7.mine = bf16[256,512]{1,0:T(8,128)(2,1)S(1)} custom-call(s32[5]{0:T(128)S(1)} %stack.27.place, s32[7,128]{1,0:T(8,128)S(1)} %bitcast.10, bf16[256,512]{1,0:T(8,128)(2,1)S(1)} %copy-done, f32[256,512]{1,0:T(8,128)S(1)} %get-tuple-element.58.refs_0_, f32[256,512]{1,0:T(8,128)S(1)} %get-tuple-element.59.refs_1_, ...), custom_call_target="tpu_custom_call" | custom-call | flops 268435456 | bytes 4194304 | tf_op jit(solution)/shard_map/attend/pallas_call | solution.py:211
  104.9 5.2 %collective-permute-done.14.other = bf16[256,512]{1,0:T(8,128)(2,1)S(1)} collective-permute-done((bf16[256,512]{1,0:T(8,128)(2,1)S(1)}, bf16[256,512]{1,0:T(8,128)(2,1)S(1)}, u32[]{:S(2)}, u32[]{:S(2)}) %collective-permute-start.14) | collective-permute-done | bytes 262176 | tf_op jit(solution)/shard_map/ppermute | solution.py:43
  110.1 5.5 %project.1 = (f32[4,256,512]{2,1,0:T(8,128)S(1)}, bf16[4,256,512]{2,1,0:T(8,128)(2,1)S(1)}) custom-call(s32[5]{0:T(128)S(1)} %stack.27.place, bf16[256,512]{1,0:T(8,128)(2,1)S(1)} %attend.7.mine, bf16[256,512]{1,0:T(8,128)(2,1)S(1)} %collective-permute-done.14.other, bf16[768,512]{1,0:T(8,128)(2,1)S(1)} %join.7.refs_3_.w0, ...), custom_call_target="tpu_custom_call" | custom-call | flops 1073741824 | bytes 6291456 | tf_op jit(solution)/shard_map/project/pallas_call | solution.py:259
  115.7 12.1 %collective-permute-start.15 = (bf16[4,256,512]{2,1,0:T(8,128)(2,1)S(1)}, bf16[4,256,512]{2,1,0:T(8,128)(2,1)S(1)}, u32[]{:S(2)}, u32[]{:S(2)}) collective-permute-start(bf16[4,256,512]{2,1,0:T(8,128)(2,1)S(1)} %get-tuple-element.64), channel_id=1, source_target_pairs={{0,1},{1,0},{2,3},{3,2},{4,5},{5,4},{6,7},{7,6},{8,9},{9,8},{10,11... | collective-permute-start | bytes 3145736 | tf_op jit(solution)/shard_map/ppermute | solution.py:43
  130.2 3.9 %collective-permute-start.16 = (bf16[256,512]{1,0:T(8,128)(2,1)S(1)}, bf16[256,512]{1,0:T(8,128)(2,1)S(1)}, u32[]{:S(2)}, u32[]{:S(2)}) collective-permute-start(bf16[256,512]{1,0:T(8,128)(2,1)S(1)} %get-tuple-element.65), channel_id=1, source_target_pairs={{0,0},{1,64},{2,2},{3,66},{4,4},{5,68},{6,6},{7,70},{8,8},{9,72},{... | collective-permute-start | bytes 786440 | tf_op jit(solution)/shard_map/ppermute | solution.py:43
  134.1 5.5 %collective-permute-start.17 = (bf16[256,512]{1,0:T(8,128)(2,1)S(1)}, bf16[256,512]{1,0:T(8,128)(2,1)S(1)}, u32[]{:S(2)}, u32[]{:S(2)}) collective-permute-start(bf16[256,512]{1,0:T(8,128)(2,1)S(1)} %get-tuple-element.66), channel_id=1, source_target_pairs={{0,2},{1,66},{2,4},{3,68},{4,6},{5,70},{6,0},{7,64},{8,10},{9,74},... | collective-permute-start | bytes 786440 | tf_op jit(solution)/shard_map/ppermute | solution.py:43
  139.7 3.4 %collective-permute-start.18 = (bf16[256,512]{1,0:T(8,128)(2,1)S(1)}, bf16[256,512]{1,0:T(8,128)(2,1)S(1)}, u32[]{:S(2)}, u32[]{:S(2)}) collective-permute-start(bf16[256,512]{1,0:T(8,128)(2,1)S(1)} %get-tuple-element.67), channel_id=1, source_target_pairs={{0,4},{1,68},{2,6},{3,70},{4,0},{5,64},{6,2},{7,66},{8,12},{9,76},... | collective-permute-start | bytes 786440 | tf_op jit(solution)/shard_map/ppermute | solution.py:43
  143.1 4.3 %collective-permute-start.19 = (bf16[256,512]{1,0:T(8,128)(2,1)S(1)}, bf16[256,512]{1,0:T(8,128)(2,1)S(1)}, u32[]{:S(2)}, u32[]{:S(2)}) collective-permute-start(bf16[256,512]{1,0:T(8,128)(2,1)S(1)} %get-tuple-element.68), channel_id=1, source_target_pairs={{0,6},{1,70},{2,0},{3,64},{4,2},{5,66},{6,4},{7,68},{8,14},{9,78},... | collective-permute-start | bytes 786440 | tf_op jit(solution)/shard_map/ppermute | solution.py:43
  147.4 15.1 %collective-permute-done.18 = bf16[256,512]{1,0:T(8,128)(2,1)S(1)} collective-permute-done((bf16[256,512]{1,0:T(8,128)(2,1)S(1)}, bf16[256,512]{1,0:T(8,128)(2,1)S(1)}, u32[]{:S(2)}, u32[]{:S(2)}) %collective-permute-start.18) | collective-permute-done | bytes 262176 | tf_op jit(solution)/shard_map/ppermute | solution.py:43
  (44 shorter events, 26.1 us)
Async XLA Ops:
  1.3 33.7 %collective-permute-start.3 = (bf16[512,512]{1,0:T(8,128)(2,1)S(1)}, bf16[512,512]{1,0:T(8,128)(2,1)S(1)}, u32[]{:S(2)}, u32[]{:S(2)}) collective-permute-start(bf16[512,512]{1,0:T(8,128)(2,1)S(1)} %get-tuple-element.44.refs_0_), channel_id=1, source_target_pairs={{0,64},{1,65},{2,66},{3,67},{4,68},{5,69},{6,70},{7,71},{8,72},{9,... | collective-permute-start | bytes 1572872 | tf_op jit(solution)/shard_map/ppermute | solution.py:43
  6.1 28.8 %collective-permute-start.2 = (bf16[512,512]{1,0:T(8,128)(2,1)S(1)}, bf16[512,512]{1,0:T(8,128)(2,1)S(1)}, u32[]{:S(2)}, u32[]{:S(2)}) collective-permute-start(bf16[512,512]{1,0:T(8,128)(2,1)S(1)} %get-tuple-element.44.refs_0_), channel_id=1, source_target_pairs={{0,256},{1,257},{2,258},{3,259},{4,260},{5,261},{6,262},{7,263},{8... | collective-permute-start | bytes 1572872 | tf_op jit(solution)/shard_map/ppermute | solution.py:43
  10.8 9.4 %collective-permute-start = (bf16[80,512]{1,0:T(8,128)(2,1)S(1)}, bf16[80,512]{1,0:T(8,128)(2,1)S(1)}, u32[]{:S(2)}, u32[]{:S(2)}) collective-permute-start(bf16[80,512]{1,0:T(8,128)(2,1)S(1)} %get-tuple-element.38.a), channel_id=1, source_target_pairs={{0,32},{1,33},{2,34},{3,35},{4,36},{5,37},{6,38},{7,39},{8,40},{9,... | collective-permute-start | bytes 245768 | tf_op jit(solution)/shard_map/ppermute | solution.py:43
  20.2 43.4 %copy-start = (bf16[256,512]{1,0:T(8,128)(2,1)S(1)}, bf16[256,512]{1,0:T(8,128)(2,1)}, u32[]{:S(2)}) copy-start(bf16[256,512]{1,0:T(8,128)(2,1)} %q.7) | copy-start | bytes 786436
  20.2 43.4 %copy-start.1 = (s32[128,7]{0,1:T(8,128)S(1)}, s32[128,7]{0,1:T(8,128)}, u32[]{:S(2)}) copy-start(s32[128,7]{0,1:T(8,128)} %param.11) | copy-start | bytes 10756
  20.2 29.1 %collective-permute-start.6 = (bf16[512,512]{1,0:T(8,128)(2,1)S(1)}, bf16[512,512]{1,0:T(8,128)(2,1)S(1)}, u32[]{:S(2)}, u32[]{:S(2)}) collective-permute-start(bf16[512,512]{1,0:T(8,128)(2,1)S(1)} %get-tuple-element.44.refs_0_), channel_id=1, source_target_pairs={{0,8},{1,9},{2,10},{3,11},{4,12},{5,13},{6,14},{7,15},{8,0},{9,1},... | collective-permute-start | bytes 1572872 | tf_op jit(solution)/shard_map/ppermute | solution.py:43
  23.4 25.9 %collective-permute-start.5 = (bf16[512,512]{1,0:T(8,128)(2,1)S(1)}, bf16[512,512]{1,0:T(8,128)(2,1)S(1)}, u32[]{:S(2)}, u32[]{:S(2)}) collective-permute-start(bf16[512,512]{1,0:T(8,128)(2,1)S(1)} %get-tuple-element.44.refs_0_), channel_id=1, source_target_pairs={{0,128},{1,129},{2,130},{3,131},{4,132},{5,133},{6,134},{7,135},{8... | collective-permute-start | bytes 1572872 | tf_op jit(solution)/shard_map/ppermute | solution.py:43
  25.6 9.3 %collective-permute-start.1 = (bf16[160,512]{1,0:T(8,128)(2,1)S(1)}, bf16[160,512]{1,0:T(8,128)(2,1)S(1)}, u32[]{:S(2)}, u32[]{:S(2)}) collective-permute-start(bf16[160,512]{1,0:T(8,128)(2,1)S(1)} %join.4.a), channel_id=1, source_target_pairs={{0,16},{1,17},{2,18},{3,19},{4,20},{5,21},{6,22},{7,23},{8,24},{9,... | collective-permute-start | bytes 491528 | tf_op jit(solution)/shard_map/ppermute | solution.py:43
  35.0 24.6 %copy-start.2 = (bf16[512,512]{1,0:T(8,128)(2,1)}, bf16[512,512]{1,0:T(8,128)(2,1)S(1)}, u32[]{:S(2)}) copy-start(bf16[512,512]{1,0:T(8,128)(2,1)S(1)} %collective-permute-done.3.refs_2_) | copy-start | bytes 1572868
  35.0 14.2 %collective-permute-start.4 = (bf16[320,512]{1,0:T(8,128)(2,1)S(1)}, bf16[320,512]{1,0:T(8,128)(2,1)S(1)}, u32[]{:S(2)}, u32[]{:S(2)}) collective-permute-start(bf16[320,512]{1,0:T(8,128)(2,1)S(1)} %join.5.a), channel_id=1, source_target_pairs={{0,8},{1,9},{2,10},{3,11},{4,12},{5,13},{6,14},{7,15},{8,0},{9,1},... | collective-permute-start | bytes 983048 | tf_op jit(solution)/shard_map/ppermute | solution.py:43
  43.7 31.0 %collective-permute-start.10 = (bf16[512,512]{1,0:T(8,128)(2,1)S(1)}, bf16[512,512]{1,0:T(8,128)(2,1)}, u32[]{:S(2)}, u32[]{:S(2)}) collective-permute-start(bf16[512,512]{1,0:T(8,128)(2,1)S(1)} %get-tuple-element.44.refs_0_), channel_id=1, source_target_pairs={{0,32},{1,33},{2,34},{3,35},{4,36},{5,37},{6,38},{7,39},{8,40},{9,... | collective-permute-start | bytes 1572872 | tf_op jit(solution)/shard_map/ppermute | solution.py:43
  49.3 14.1 %copy-start.5 = (bf16[512,512]{1,0:T(8,128)(2,1)}, bf16[512,512]{1,0:T(8,128)(2,1)S(1)}, u32[]{:S(2)}) copy-start(bf16[512,512]{1,0:T(8,128)(2,1)S(1)} %collective-permute-done.5.refs_3_) | copy-start | bytes 1572868
  49.3 6.0 %collective-permute-start.7 = (bf16[128,512]{1,0:T(8,128)(2,1)S(1)}, bf16[128,512]{1,0:T(8,128)(2,1)S(1)}, u32[]{:S(2)}, u32[]{:S(2)}) collective-permute-start(bf16[128,512]{1,0:T(8,128)(2,1)S(1)} %pick.1), channel_id=1, source_target_pairs={{0,64},{1,65},{2,66},{3,67},{4,68},{5,69},{6,70},{7,71},{8,72},{9,... | collective-permute-start | bytes 393224 | tf_op jit(solution)/shard_map/ppermute | solution.py:43
  55.4 23.6 %collective-permute-start.9 = (bf16[768,512]{1,0:T(8,128)(2,1)S(1)}, bf16[768,512]{1,0:T(8,128)(2,1)S(1)}, u32[]{:S(2)}, u32[]{:S(2)}) collective-permute-start(bf16[768,512]{1,0:T(8,128)(2,1)S(1)} %join.7.refs_3_.w0), channel_id=1, source_target_pairs={{0,384},{1,385},{2,386},{3,387},{4,388},{5,389},{6,390},{7,391},{8... | collective-permute-start | bytes 2359304 | tf_op jit(solution)/shard_map/ppermute | solution.py:43
  59.6 19.4 %collective-permute-start.8 = (bf16[768,512]{1,0:T(8,128)(2,1)S(1)}, bf16[768,512]{1,0:T(8,128)(2,1)S(1)}, u32[]{:S(2)}, u32[]{:S(2)}) collective-permute-start(bf16[768,512]{1,0:T(8,128)(2,1)S(1)} %join.7.refs_3_.w0), channel_id=1, source_target_pairs={{0,128},{1,129},{2,130},{3,131},{4,132},{5,133},{6,134},{7,135},{8... | collective-permute-start | bytes 2359304 | tf_op jit(solution)/shard_map/ppermute | solution.py:43
  61.5 31.4 %collective-permute-start.11 = (bf16[512,512]{1,0:T(8,128)(2,1)S(1)}, bf16[512,512]{1,0:T(8,128)(2,1)}, u32[]{:S(2)}, u32[]{:S(2)}) collective-permute-start(bf16[512,512]{1,0:T(8,128)(2,1)S(1)} %get-tuple-element.44.refs_0_), channel_id=1, source_target_pairs={{0,16},{1,17},{2,18},{3,19},{4,20},{5,21},{6,22},{7,23},{8,24},{9,... | collective-permute-start | bytes 1572872 | tf_op jit(solution)/shard_map/ppermute | solution.py:43
  79.0 18.3 %collective-permute-start.12 = (bf16[400,512]{1,0:T(8,128)(2,1)S(1)}, bf16[400,512]{1,0:T(8,128)(2,1)S(1)}, u32[]{:S(2)}, u32[]{:S(2)}) collective-permute-start(bf16[400,512]{1,0:T(8,128)(2,1)S(1)} %slice.6), channel_id=1, source_target_pairs={{0,128},{1,129},{2,130},{3,131},{4,132},{5,133},{6,134},{7,135},{8... | collective-permute-start | bytes 1228808 | tf_op jit(solution)/shard_map/ppermute | solution.py:43
  81.1 16.2 %collective-permute-start.13 = (bf16[368,512]{1,0:T(8,128)(2,1)S(1)}, bf16[368,512]{1,0:T(8,128)(2,1)S(1)}, u32[]{:S(2)}, u32[]{:S(2)}) collective-permute-start(bf16[368,512]{1,0:T(8,128)(2,1)S(1)} %slice.7), channel_id=1, source_target_pairs={{0,384},{1,385},{2,386},{3,387},{4,388},{5,389},{6,390},{7,391},{8... | collective-permute-start | bytes 1130504 | tf_op jit(solution)/shard_map/ppermute | solution.py:43
  103.0 7.1 %collective-permute-start.14 = (bf16[256,512]{1,0:T(8,128)(2,1)S(1)}, bf16[256,512]{1,0:T(8,128)(2,1)S(1)}, u32[]{:S(2)}, u32[]{:S(2)}) collective-permute-start(bf16[256,512]{1,0:T(8,128)(2,1)S(1)} %attend.7.mine), channel_id=1, source_target_pairs={{0,64},{1,65},{2,66},{3,67},{4,68},{5,69},{6,70},{7,71},{8,72},{9,... | collective-permute-start | bytes 786440 | tf_op jit(solution)/shard_map/ppermute | solution.py:43
  115.7 14.3 %collective-permute-start.15 = (bf16[4,256,512]{2,1,0:T(8,128)(2,1)S(1)}, bf16[4,256,512]{2,1,0:T(8,128)(2,1)S(1)}, u32[]{:S(2)}, u32[]{:S(2)}) collective-permute-start(bf16[4,256,512]{2,1,0:T(8,128)(2,1)S(1)} %get-tuple-element.64), channel_id=1, source_target_pairs={{0,1},{1,0},{2,3},{3,2},{4,5},{5,4},{6,7},{7,6},{8,9},{9,8},{10,11... | collective-permute-start | bytes 3145736 | tf_op jit(solution)/shard_map/ppermute | solution.py:43
  130.2 17.2 %collective-permute-start.16 = (bf16[256,512]{1,0:T(8,128)(2,1)S(1)}, bf16[256,512]{1,0:T(8,128)(2,1)S(1)}, u32[]{:S(2)}, u32[]{:S(2)}) collective-permute-start(bf16[256,512]{1,0:T(8,128)(2,1)S(1)} %get-tuple-element.65), channel_id=1, source_target_pairs={{0,0},{1,64},{2,2},{3,66},{4,4},{5,68},{6,6},{7,70},{8,8},{9,72},{... | collective-permute-start | bytes 786440 | tf_op jit(solution)/shard_map/ppermute | solution.py:43
  134.1 13.3 %collective-permute-start.17 = (bf16[256,512]{1,0:T(8,128)(2,1)S(1)}, bf16[256,512]{1,0:T(8,128)(2,1)S(1)}, u32[]{:S(2)}, u32[]{:S(2)}) collective-permute-start(bf16[256,512]{1,0:T(8,128)(2,1)S(1)} %get-tuple-element.66), channel_id=1, source_target_pairs={{0,2},{1,66},{2,4},{3,68},{4,6},{5,70},{6,0},{7,64},{8,10},{9,74},... | collective-permute-start | bytes 786440 | tf_op jit(solution)/shard_map/ppermute | solution.py:43
  139.7 22.9 %collective-permute-start.18 = (bf16[256,512]{1,0:T(8,128)(2,1)S(1)}, bf16[256,512]{1,0:T(8,128)(2,1)S(1)}, u32[]{:S(2)}, u32[]{:S(2)}) collective-permute-start(bf16[256,512]{1,0:T(8,128)(2,1)S(1)} %get-tuple-element.67), channel_id=1, source_target_pairs={{0,4},{1,68},{2,6},{3,70},{4,0},{5,64},{6,2},{7,66},{8,12},{9,76},... | collective-permute-start | bytes 786440 | tf_op jit(solution)/shard_map/ppermute | solution.py:43
  143.1 21.6 %collective-permute-start.19 = (bf16[256,512]{1,0:T(8,128)(2,1)S(1)}, bf16[256,512]{1,0:T(8,128)(2,1)S(1)}, u32[]{:S(2)}, u32[]{:S(2)}) collective-permute-start(bf16[256,512]{1,0:T(8,128)(2,1)S(1)} %get-tuple-element.68), channel_id=1, source_target_pairs={{0,6},{1,70},{2,0},{3,64},{4,2},{5,66},{6,4},{7,68},{8,14},{9,78},... | collective-permute-start | bytes 786440 | tf_op jit(solution)/shard_map/ppermute | solution.py:43
  (2 other events, 22.8 us)

commit v3 on v2

v3 whole, which is shorter than its diff:
```python
import functools

import jax
import jax.numpy as jnp
from jax import lax
from jax.experimental import pallas as pl
from jax.experimental.pallas import tpu as pltpu
from jax.sharding import PartitionSpec as P

HD = 128
BLK = 128
NX, NZL, NY, NZH, NC = 4, 2, 8, 4, 2
WROWS = 64
LROWS = 16
UNIT = WROWS + LROWS
HALF = 400
COST = 64
COST0 = 64
COST1 = 0
AXES = ("ctx", "head")
SCALE = HD**-0.5
F32 = jnp.float32
BF16 = jnp.bfloat16
VLIM = 16 << 20
HBM = pl.BlockSpec(memory_space=pltpu.HBM)
ANY = pl.BlockSpec(memory_space=pl.ANY)
SMEM = pl.BlockSpec(memory_space=pltpu.SMEM)
VMEM = pl.BlockSpec(memory_space=pltpu.VMEM)


def coords(i):
    ctx, head = divmod(i, NZH * NC)
    x, r = divmod(ctx, NZL * NY)
    zl, y = divmod(r, NY)
    zh, c = divmod(head, NC)
    return x, zl, y, zh, c


def flat(x, zl, y, zh, c):
    return ((x * NZL + zl) * NY + y) * (NZH * NC) + zh * NC + c


def send(a, to):
    pairs = [(i, flat(*to(*coords(i)))) for i in range(NX * NZL * NY * NZH * NC)]
    return lax.ppermute(a, AXES, pairs)


def xor(level):
    def to(x, zl, y, zh, c):
        ctx = ((x * NZL + zl) * NY + y) ^ (1 << level)
        x, r = divmod(ctx, NZL * NY)
        zl, y = divmod(r, NY)
        return x, zl, y, zh, c

    return to


def after(a, far, levels):
    if levels:
        a, done = lax.optimization_barrier((a, [far[l] for l in levels]))
        far.update(zip(levels, done, strict=True))
    return a


def in_hbm(a):
    return pltpu.with_memory_space_constraint(a, pltpu.HBM)


def params():
    return pltpu.CompilerParams(vmem_limit_bytes=VLIM)


def dot_nt(a, b):
    return lax.dot_general(a, b, (((1,), (1,)), ((), ())), preferred_element_type=F32)


def prepare_kernel(pool, keys, values, weight, unit, pool_v, kv_v, sem):
    copies = [
        pltpu.make_async_copy(weight, unit.at[pl.ds(0, WROWS)], sem.at[0]),
        pltpu.make_async_copy(pool, pool_v, sem.at[1]),
        pltpu.make_async_copy(keys, kv_v.at[pl.ds(0, 256)], sem.at[2]),
        pltpu.make_async_copy(values, kv_v.at[pl.ds(256, 256)], sem.at[3]),
    ]
    for copy in copies:
        copy.start()
    for copy in copies:
        copy.wait()
    pooled = [
        jnp.dot(pool_v[...], kv_v[r : r + 256, :], preferred_element_type=F32) for r in (0, 256)
    ]
    unit[WROWS:UNIT, :] = jnp.concatenate(pooled, axis=0).astype(BF16)


def prepare(pool, keys, values, weight):
    return pl.pallas_call(
        prepare_kernel,
        out_shape=jax.ShapeDtypeStruct((UNIT, 512), BF16),
        in_specs=[HBM] * 4,
        out_specs=VMEM,
        scratch_shapes=[
            pltpu.VMEM((8, 256), BF16),
            pltpu.VMEM((512, 512), BF16),
            pltpu.SemaphoreType.DMA((4,)),
        ],
        compiler_params=params(),
        name="prepare",
    )(*[in_hbm(a) for a in (pool, keys, values, weight)])


def stack_kernel(keys, values, kv, sem):
    copies = [
        pltpu.make_async_copy(keys, kv.at[pl.ds(0, 256)], sem.at[0]),
        pltpu.make_async_copy(values, kv.at[pl.ds(256, 256)], sem.at[1]),
    ]
    for copy in copies:
        copy.start()
    for copy in copies:
        copy.wait()


def stack(keys, values):
    return pl.pallas_call(
        stack_kernel,
        out_shape=jax.ShapeDtypeStruct((512, 512), BF16),
        in_specs=[HBM] * 2,
        out_specs=VMEM,
        scratch_shapes=[pltpu.SemaphoreType.DMA((2,))],
        compiler_params=params(),
        name="stack",
    )(in_hbm(keys), in_hbm(values))


def softmax_step(state, q, ks, vs):
    scores = [dot_nt(q, k) * SCALE for k in ks]
    top = functools.reduce(jnp.maximum, [jnp.max(s, axis=1, keepdims=True) for s in scores])
    if state is not None:
        old_top, old_sum, old_acc = state
        top = jnp.maximum(top, old_top)
    weights = [jnp.exp(s - top) for s in scores]
    total = sum(jnp.sum(w, axis=1, keepdims=True) for w in weights)
    acc = sum(
        jnp.dot(w.astype(BF16), v, preferred_element_type=F32)
        for w, v in zip(weights, vs, strict=True)
    )
    if state is not None:
        fade = jnp.exp(old_top - top)
        total = total + old_sum * fade
        acc = acc + old_acc * fade
    return top, total, acc


def mark_starts(lo, hi):
    rows = [b * UNIT + WROWS for b in range(NY)] + [NY * UNIT + b * LROWS for b in range(NY)]
    return tuple(r - lo for r in rows if lo <= r < hi)


def landmarks(marks, cols):
    rows = marks[:, cols].astype(F32)
    groups = [rows[g : g + 8] for g in range(0, rows.shape[0], 8)]
    ks = jnp.concatenate(groups[0::2], axis=0)
    vs = jnp.concatenate(groups[1::2], axis=0)
    return ks.astype(BF16), vs.astype(BF16)


def attend_kernel(levels, own, carry, mark, final, token, place, pattern, q, *refs):
    refs = list(refs)
    own_ref = refs.pop(0) if own else None
    state_refs = [refs.pop(0) for _ in range(3)] if carry else None
    mark_refs = [refs.pop(0) for _ in mark]
    far = [refs.pop(0) for _ in levels]
    if token:
        refs.pop(0)
    outs = [refs.pop(0) for _ in range(1 if final else 3)]
    far_v = refs.pop(0) if levels else None
    mark_v = refs.pop(0) if mark else None
    sem = refs.pop(0)
    mark_sem = refs.pop(0) if mark else None
    copies = [pltpu.make_async_copy(r, far_v.at[i], sem.at[i]) for i, r in enumerate(far)]
    if mark:
        rows = [(r, at) for r, starts in zip(mark_refs, mark, strict=True) for at in starts]
        for i, (r, at) in enumerate(rows):
            dst = mark_v.at[pl.ds(i * LROWS, LROWS), :]
            copies.append(pltpu.make_async_copy(r.at[pl.ds(at, LROWS), :], dst, mark_sem.at[i]))
    for copy in copies:
        copy.start()
    for copy in copies:
        copy.wait()
    for h in range(4):
        cols = slice(h * HD, (h + 1) * HD)
        marks = landmarks(mark_v, cols) if mark else None
        for j in range(2):
            rows = slice(j * BLK, (j + 1) * BLK)
            ks, vs = [], []
            if own:
                ks.append(own_ref[0:256, cols])
                vs.append(own_ref[256:512, cols])
            if mark:
                ks.append(marks[0])
                vs.append(marks[1])
            for i, level in enumerate(levels):
                at = pl.multiple_of((pattern[1 + level, place[2] + j] & 1) * BLK, BLK)
                ks.append(far_v[i, pl.ds(at, BLK), cols])
                vs.append(far_v[i, pl.ds(256 + at, BLK), cols])
            state = None
            if carry:
                top, total, acc = state_refs
                first = slice(h * HD, h * HD + 1)
                state = (top[rows, first], total[rows, first], acc[rows, cols])
            m, s, a = softmax_step(state, q[rows, cols], ks, vs)
            if final:
                outs[0][rows, cols] = (a / s).astype(BF16)
            else:
                outs[0][rows, cols] = jnp.broadcast_to(m, (BLK, HD))
                outs[1][rows, cols] = jnp.broadcast_to(s, (BLK, HD))
                outs[2][rows, cols] = a


def attend(place, pattern, q, levels, far, own=None, state=None, mark=(), final=False, cost=1, token=None):
    args, specs = [place, pattern, q], [SMEM, SMEM, VMEM]
    if own is not None:
        args, specs = [*args, own], [*specs, VMEM]
    if state is not None:
        args, specs = [*args, *state], specs + [VMEM] * 3
    args += [a for a, _ in mark]
    specs += [ANY] * len(mark)
    args += [in_hbm(far[l]) for l in levels]
    specs += [HBM] * len(levels)
    if token is not None:
        args, specs = [*args, token], [*specs, ANY]
    scratch = [pltpu.VMEM((len(levels), 512, 512), BF16)] if levels else []
    groups = sum(len(starts) for _, starts in mark)
    if mark:
        scratch.append(pltpu.VMEM((groups * LROWS, 512), BF16))
    scratch.append(pltpu.SemaphoreType.DMA((len(levels) + 1,)))
    if mark:
        scratch.append(pltpu.SemaphoreType.DMA((groups,)))
    count = 128 * len(levels) + 256 * (own is not None) + 8 * groups
    return pl.pallas_call(
        functools.partial(
            attend_kernel,
            levels,
            own is not None,
            state is not None,
            tuple(starts for _, starts in mark),
            final,
            token is not None,
        ),
        out_shape=jax.ShapeDtypeStruct((256, 512), BF16)
        if final
        else (jax.ShapeDtypeStruct((256, 512), F32),) * 3,
        in_specs=specs,
        out_specs=VMEM if final else (VMEM,) * 3,
        scratch_shapes=scratch,
        compiler_params=params(),
        name="attend",
        cost_estimate=pl.CostEstimate(
            flops=cost * 4 * 256 * 512 * count,
            bytes_accessed=4 << 20,
            transcendentals=1024 * count,
        ),
    )(*args)


def pack_kernel(place, w0, w1, w2a, w2b, w3, out):
    y = place[3]
    chunks = (((w0, 0, 768),), ((w1, 0, 768),), ((w2a, 0, HALF), (w2b, HALF, 768)))
    chunks += (((w3, 0, 768),),)
    for i, pieces in enumerate(chunks):
        for p in range(NY):
            at = pl.multiple_of((y ^ (4 * (p & 1) + (p & 2) + (p >> 2))) * WROWS, WROWS)
            [(ref, lo)] = [(r, lo) for r, lo, hi in pieces if lo <= p * UNIT < hi]
            out[i, pl.ds(at, WROWS), :] = ref[p * UNIT - lo : p * UNIT - lo + WROWS, :]


def pack(place, wl):
    return pl.pallas_call(
        pack_kernel,
        out_shape=jax.ShapeDtypeStruct((NX, NY * WROWS, 512), BF16),
        in_specs=[SMEM] + [VMEM] * 5,
        out_specs=VMEM,
        compiler_params=params(),
        name="pack",
    )(place, *wl)


def project_kernel(place, mine, got1, got2, w_mine, w_other, *outs):
    step, same = place[0], place[1] == 1
    a, b = mine[...], got1[...]
    first = jnp.where(same, a, b)
    second = jnp.where(same, b, got2[...])
    for d in range(4):
        shift = (step - d) & 3
        outs[d][...] = (dot_nt(first, w_mine[shift]) + dot_nt(second, w_other[shift])).astype(BF16)


def project(place, mine, got1, got2, w_mine, w_other):
    return pl.pallas_call(
        project_kernel,
        out_shape=(jax.ShapeDtypeStruct((256, 512), BF16),) * 4,
        in_specs=[SMEM] + [VMEM] * 5,
        out_specs=(VMEM,) * 4,
        compiler_params=params(),
        name="project",
        cost_estimate=pl.CostEstimate(
            flops=2 * 512 * 512 * 2048, bytes_accessed=6 << 20, transcendentals=0
        ),
    )(place, mine, got1, got2, w_mine, w_other)


def join_kernel(a, b, out):
    n = a.shape[0]
    out[0:n, :] = a[...]
    out[n:, :] = b[...]


def join(a, b):
    return pl.pallas_call(
        join_kernel,
        out_shape=jax.ShapeDtypeStruct((a.shape[0] + b.shape[0], 512), BF16),
        in_specs=[VMEM] * 2,
        out_specs=VMEM,
        compiler_params=params(),
        name="join",
    )(a, b)


def arrived_kernel(*refs):
    refs[-1][...] = jnp.zeros_like(refs[-1])


def arrived(cost, *arrays):
    return pl.pallas_call(
        arrived_kernel,
        out_shape=jax.ShapeDtypeStruct((8, 128), F32),
        in_specs=[HBM] * len(arrays),
        out_specs=VMEM,
        compiler_params=params(),
        name="arrived",
        cost_estimate=pl.CostEstimate(flops=cost << 27, bytes_accessed=4 << 20, transcendentals=0),
    )(*[in_hbm(a) for a in arrays])


def pick_kernel(a, out):
    for p in range(NY):
        out[p * LROWS : (p + 1) * LROWS, :] = a[p * UNIT + WROWS : (p + 1) * UNIT, :]


def pick(a):
    return pl.pallas_call(
        pick_kernel,
        out_shape=jax.ShapeDtypeStruct((NY * LROWS, 512), BF16),
        in_specs=[VMEM],
        out_specs=VMEM,
        compiler_params=params(),
        name="pick",
    )(a)


def along_x(k):
    return lambda x, zl, y, zh, c: ((x + k) % NX, zl, y, zh, c)


def to_first(x, zl, y, zh, c):
    return (x, zl, y, zh, 1 - c) if zl != c else (x, 1 - zl, y, zh, c)


def to_second(x, zl, y, zh, c):
    return (x, 1 - zl, y, zh, 1 - c) if zl != c else (x, zl, y, zh, c)


def on_device(queries, keys, values, pool_weight, out_weight, pattern):
    ctx, head = lax.axis_index("ctx"), lax.axis_index("head")
    same = (((ctx >> 3) ^ head) & 1) ^ 1
    place = jnp.stack([(ctx >> 4) + NX - (head >> 1), same, ctx * 2, ctx & 7])

    wl = prepare(pool_weight, keys, values, out_weight.T)
    step = functools.partial(attend, place, pattern.T, queries)
    keys, values, wl = lax.optimization_barrier((keys, values, wl))
    kv = stack(keys, values)
    wl = join(wl, send(wl, xor(2)))
    kv, wl = lax.optimization_barrier((kv, wl))
    far = {level: send(kv, xor(level)) for level in (3, 5)}
    wl = join(wl, send(wl, xor(1)))
    kv, wl = lax.optimization_barrier((kv, wl))
    far[4] = send(kv, xor(4))
    wl = join(wl, send(wl, xor(0)))
    marks = pick(wl)
    kv, marks = lax.optimization_barrier((kv, marks))
    far[2] = send(kv, xor(2))
    wl = join(wl, send(marks, xor(3)))
    wl1, wl3 = send(wl, along_x(1)), send(wl, along_x(-1))
    every = mark_starts(0, 768)
    token = arrived(COST0, far[3], far[5], far[4])
    kv, token, wl = lax.optimization_barrier((kv, token, wl))
    far.update({level: send(kv, xor(level)) for level in (1, 0)})
    state = step((3, 5, 4, 2), far, own=kv, mark=[(wl, every)], token=token, cost=COST)
    wl1, wl3, state = lax.optimization_barrier((wl1, wl3, state))
    wl2a, wl2b = send(wl1[:HALF], along_x(1)), send(wl3[HALF:], along_x(-1))
    state = step((), far, state=state, mark=[(wl1, every), (wl3, every)])
    rest = [(wl2a, mark_starts(0, HALF)), (wl2b, mark_starts(HALF, 768))]
    late, state = lax.optimization_barrier(((far[1], far[0]), state))
    far[1], far[0] = late
    token = arrived(COST1, *late)
    pieces = (wl, wl1, wl2a, wl2b, wl3)
    pieces, token, state = lax.optimization_barrier((pieces, token, state))
    mine = step((1, 0), far, state=state, mark=rest, final=True, token=token)
    w_mine = pack(place, pieces)
    w_other = send(w_mine, lambda x, zl, y, zh, c: (x, zl, y, zh, 1 - c))
    part = project(place, mine, send(mine, to_first), send(mine, to_second), w_mine, w_other)
    total = 0.0
    for d in range(4):
        total += send(
            part[d], lambda x, zl, y, zh, c: (x, c, y, (zh + d) % NZH, zl)
        ).astype(F32)
    return total.astype(BF16)


def solution(mesh):
    in_specs = (
        P("ctx", "head"),
        P("ctx", "head"),
        P("ctx", "head"),
        P("ctx", None),
        P("head", "ctx"),
        P(),
    )
    return jax.shard_map(
        on_device, mesh=mesh, in_specs=in_specs, out_specs=P("ctx", "head"), check_vma=False
    )
```

time: 167 us -> 161 us (0.964)
  the two profiles are of different devices: /device:TPU:1 before, /device:TPU:17 now
where the time goes in v3:
time: 161 us; the launch traced here: 160 us
  starting transfers between devices  86.2 us (54%)
  waiting for transfers between devices  49.2 us (31%)
  Pallas kernels  20.2 us (13%)
  local copies, waits for them, and re-layouts  3.27 us (2%)
    ppermute x21, starting transfers between devices, send(): return lax.ppermute(a, AXES, pairs)  86.2 us
    ppermute x21, waiting for transfers between devices, send(): return lax.ppermute(a, AXES, pairs)  49.2 us
    pallas_call x3, Pallas kernels, attend(): pl.pallas_call(functools.partial(attend_kernel, levels, own is not None,...  15.2 us
  transfers between devices with their start and end apart: 21, of which 9 were waited for; matrix products, arithmetic and copies ran while one was open for 0% of the time, Pallas kernels for 10%

profile of v3, /device:TPU:17, one launch (start us, length us, event | category | flops | bytes accessed | tf_op | source)
XLA Modules:
  0.0 160.2 jit_solution(9542364611816877265)
XLA Ops:
  1.3 5.7 %collective-permute-start = (bf16[80,512]{1,0:T(8,128)(2,1)S(1)}, bf16[80,512]{1,0:T(8,128)(2,1)S(1)}, u32[]{:S(2)}, u32[]{:S(2)}) collective-permute-start(bf16[80,512]{1,0:T(8,128)(2,1)S(1)} %prepare.1.a), channel_id=1, source_target_pairs={{0,32},{1,33},{2,34},{3,35},{4,36},{5,37},{6,38},{7,39},{8,40},{9,... | collective-permute-start | bytes 245768 | tf_op jit(solution)/shard_map/ppermute | solution.py:45
  8.0 4.1 %collective-permute-done.b = bf16[80,512]{1,0:T(8,128)(2,1)S(1)} collective-permute-done((bf16[80,512]{1,0:T(8,128)(2,1)S(1)}, bf16[80,512]{1,0:T(8,128)(2,1)S(1)}, u32[]{:S(2)}, u32[]{:S(2)}) %collective-permute-start) | collective-permute-done | bytes 81952 | tf_op jit(solution)/shard_map/ppermute | solution.py:45
  14.1 5.7 %collective-permute-start.4 = (bf16[512,512]{1,0:T(8,128)(2,1)S(1)}, bf16[512,512]{1,0:T(8,128)(2,1)S(1)}, u32[]{:S(2)}, u32[]{:S(2)}) collective-permute-start(bf16[512,512]{1,0:T(8,128)(2,1)S(1)} %stack.21.refs_0_), channel_id=1, source_target_pairs={{0,256},{1,257},{2,258},{3,259},{4,260},{5,261},{6,262},{7,263},{8... | collective-permute-start | bytes 1572872 | tf_op jit(solution)/shard_map/ppermute | solution.py:45
  19.8 4.0 %collective-permute-start.3 = (bf16[512,512]{1,0:T(8,128)(2,1)S(1)}, bf16[512,512]{1,0:T(8,128)(2,1)S(1)}, u32[]{:S(2)}, u32[]{:S(2)}) collective-permute-start(bf16[512,512]{1,0:T(8,128)(2,1)S(1)} %stack.21.refs_0_), channel_id=1, source_target_pairs={{0,64},{1,65},{2,66},{3,67},{4,68},{5,69},{6,70},{7,71},{8,72},{9,... | collective-permute-start | bytes 1572872 | tf_op jit(solution)/shard_map/ppermute | solution.py:45
  28.0 7.7 %collective-permute-done.2.b = bf16[320,512]{1,0:T(8,128)(2,1)S(1)} collective-permute-done((bf16[320,512]{1,0:T(8,128)(2,1)S(1)}, bf16[320,512]{1,0:T(8,128)(2,1)S(1)}, u32[]{:S(2)}, u32[]{:S(2)}) %collective-permute-start.2) | collective-permute-done | bytes 327712 | tf_op jit(solution)/shard_map/ppermute | solution.py:45
  37.8 5.2 %collective-permute-start.9 = (bf16[512,512]{1,0:T(8,128)(2,1)S(1)}, bf16[512,512]{1,0:T(8,128)(2,1)S(1)}, u32[]{:S(2)}, u32[]{:S(2)}) collective-permute-start(bf16[512,512]{1,0:T(8,128)(2,1)S(1)} %stack.21.refs_0_), channel_id=1, source_target_pairs={{0,32},{1,33},{2,34},{3,35},{4,36},{5,37},{6,38},{7,39},{8,40},{9,... | collective-permute-start | bytes 1572872 | tf_op jit(solution)/shard_map/ppermute | solution.py:45
  43.1 4.9 %collective-permute-start.8 = (bf16[768,512]{1,0:T(8,128)(2,1)S(1)}, bf16[768,512]{1,0:T(8,128)(2,1)S(1)}, u32[]{:S(2)}, u32[]{:S(2)}) collective-permute-start(bf16[768,512]{1,0:T(8,128)(2,1)S(1)} %join.7.refs_1_.w0), channel_id=1, source_target_pairs={{0,384},{1,385},{2,386},{3,387},{4,388},{5,389},{6,390},{7,391},{8... | collective-permute-start | bytes 2359304 | tf_op jit(solution)/shard_map/ppermute | solution.py:45
  51.6 3.1 %collective-permute-start.13 = (bf16[512,512]{1,0:T(8,128)(2,1)S(1)}, bf16[512,512]{1,0:T(8,128)(2,1)S(1)}, u32[]{:S(2)}, u32[]{:S(2)}) collective-permute-start(bf16[512,512]{1,0:T(8,128)(2,1)S(1)} %stack.21.refs_0_), channel_id=1, source_target_pairs={{0,8},{1,9},{2,10},{3,11},{4,12},{5,13},{6,14},{7,15},{8,0},{9,1},... | collective-permute-start | bytes 1572872 | tf_op jit(solution)/shard_map/ppermute | solution.py:45
  54.6 3.4 %collective-permute-start.12 = (bf16[512,512]{1,0:T(8,128)(2,1)S(1)}, bf16[512,512]{1,0:T(8,128)(2,1)S(1)}, u32[]{:S(2)}, u32[]{:S(2)}) collective-permute-start(bf16[512,512]{1,0:T(8,128)(2,1)S(1)} %stack.21.refs_0_), channel_id=1, source_target_pairs={{0,16},{1,17},{2,18},{3,19},{4,20},{5,21},{6,22},{7,23},{8,24},{9,... | collective-permute-start | bytes 1572872 | tf_op jit(solution)/shard_map/ppermute | solution.py:45
  58.9 5.7 %attend.3 = (f32[256,512]{1,0:T(8,128)S(1)}, f32[256,512]{1,0:T(8,128)S(1)}, f32[256,512]{1,0:T(8,128)S(1)}) custom-call(s32[4]{0:T(128)S(1)} %pad_add_fusion.place, s32[7,128]{1,0:T(8,128)S(1)} %bitcast.6, bf16[256,512]{1,0:T(8,128)(2,1)S(1)} %copy-done, bf16[512,512]{1,0:T(8,128)(2,1)S(1)} %stack.21.refs_0_, bf16[768,512]{1,0:T(8,128)(2,1)S(1)} %join.7.refs_1_.w0, ...), custom_call_target="tpu_custom_call" | custom-call | flops 30064771072 | bytes 4194304 | tf_op jit(solution)/shard_map/attend/pallas_call | solution.py:238
  68.8 4.6 %collective-permute-start.11 = (bf16[368,512]{1,0:T(8,128)(2,1)S(1)}, bf16[368,512]{1,0:T(8,128)(2,1)S(1)}, u32[]{:S(2)}, u32[]{:S(2)}) collective-permute-start(bf16[368,512]{1,0:T(8,128)(2,1)S(1)} %slice.7), channel_id=1, source_target_pairs={{0,384},{1,385},{2,386},{3,387},{4,388},{5,389},{6,390},{7,391},{8... | collective-permute-start | bytes 1130504 | tf_op jit(solution)/shard_map/ppermute | solution.py:45
  73.4 4.4 %attend.4 = (f32[256,512]{1,0:T(8,128)S(1)}, f32[256,512]{1,0:T(8,128)S(1)}, f32[256,512]{1,0:T(8,128)S(1)}) custom-call(s32[4]{0:T(128)S(1)} %pad_add_fusion.place, s32[7,128]{1,0:T(8,128)S(1)} %bitcast.7, bf16[256,512]{1,0:T(8,128)(2,1)S(1)} %copy-done, f32[256,512]{1,0:T(8,128)S(1)} %get-tuple-element.63.refs_0_, ...), custom_call_target="tpu_custom_call" | custom-call | flops 134217728 | bytes 4194304 | tf_op jit(solution)/shard_map/attend/pallas_call | solution.py:238
  77.8 9.1 %collective-permute-done.13.refs_1_.refs_6_ = bf16[512,512]{1,0:T(8,128)(2,1)S(1)} collective-permute-done((bf16[512,512]{1,0:T(8,128)(2,1)S(1)}, bf16[512,512]{1,0:T(8,128)(2,1)S(1)}, u32[]{:S(2)}, u32[]{:S(2)}) %collective-permute-start.13) | collective-permute-done | bytes 524320 | tf_op jit(solution)/shard_map/ppermute | solution.py:45
  86.9 4.3 %collective-permute-done.12.refs_0_.refs_5_ = bf16[512,512]{1,0:T(8,128)(2,1)S(1)} collective-permute-done((bf16[512,512]{1,0:T(8,128)(2,1)S(1)}, bf16[512,512]{1,0:T(8,128)(2,1)S(1)}, u32[]{:S(2)}, u32[]{:S(2)}) %collective-permute-start.12) | collective-permute-done | bytes 524320 | tf_op jit(solution)/shard_map/ppermute | solution.py:45
  92.7 11.4 %collective-permute-start.16 = (bf16[4,512,512]{2,1,0:T(8,128)(2,1)S(1)}, bf16[4,512,512]{2,1,0:T(8,128)(2,1)S(1)}, u32[]{:S(2)}, u32[]{:S(2)}) collective-permute-start(bf16[4,512,512]{2,1,0:T(8,128)(2,1)S(1)} %pack.1.w_mine), channel_id=1, source_target_pairs={{0,1},{1,0},{2,3},{3,2},{4,5},{5,4},{6,7},{7,6},{8,9},{9,8},{10,11... | collective-permute-start | bytes 6291464 | tf_op jit(solution)/shard_map/ppermute | solution.py:45
  104.1 5.1 %attend.5.mine = bf16[256,512]{1,0:T(8,128)(2,1)S(1)} custom-call(s32[4]{0:T(128)S(1)} %pad_add_fusion.place, s32[7,128]{1,0:T(8,128)S(1)} %bitcast.8, bf16[256,512]{1,0:T(8,128)(2,1)S(1)} %copy-done, f32[256,512]{1,0:T(8,128)S(1)} %get-tuple-element.74.refs_0_, f32[256,512]{1,0:T(8,128)S(1)} %get-tuple-element.75.refs_1_, ...), custom_call_target="tpu_custom_call" | custom-call | flops 201326592 | bytes 4194304 | tf_op jit(solution)/shard_map/attend/pallas_call | solution.py:238
  109.2 3.4 %collective-permute-start.15 = (bf16[256,512]{1,0:T(8,128)(2,1)S(1)}, bf16[256,512]{1,0:T(8,128)(2,1)S(1)}, u32[]{:S(2)}, u32[]{:S(2)}) collective-permute-start(bf16[256,512]{1,0:T(8,128)(2,1)S(1)} %attend.5.mine), channel_id=1, source_target_pairs={{0,0},{1,64},{2,2},{3,66},{4,4},{5,68},{6,6},{7,70},{8,8},{9,72},{... | collective-permute-start | bytes 786440 | tf_op jit(solution)/shard_map/ppermute | solution.py:45
  116.9 2.8 %collective-permute-done.14.got1 = bf16[256,512]{1,0:T(8,128)(2,1)S(1)} collective-permute-done((bf16[256,512]{1,0:T(8,128)(2,1)S(1)}, bf16[256,512]{1,0:T(8,128)(2,1)S(1)}, u32[]{:S(2)}, u32[]{:S(2)}) %collective-permute-start.14) | collective-permute-done | bytes 262176 | tf_op jit(solution)/shard_map/ppermute | solution.py:45
  121.5 3.4 %collective-permute-start.17 = (bf16[256,512]{1,0:T(8,128)(2,1)S(1)}, bf16[256,512]{1,0:T(8,128)(2,1)S(1)}, u32[]{:S(2)}, u32[]{:S(2)}) collective-permute-start(bf16[256,512]{1,0:T(8,128)(2,1)S(1)} %get-tuple-element.83), channel_id=1, source_target_pairs={{0,0},{1,64},{2,2},{3,66},{4,4},{5,68},{6,6},{7,70},{8,8},{9,72},{... | collective-permute-start | bytes 786440 | tf_op jit(solution)/shard_map/ppermute | solution.py:45
  124.9 7.1 %collective-permute-start.18 = (bf16[256,512]{1,0:T(8,128)(2,1)S(1)}, bf16[256,512]{1,0:T(8,128)(2,1)S(1)}, u32[]{:S(2)}, u32[]{:S(2)}) collective-permute-start(bf16[256,512]{1,0:T(8,128)(2,1)S(1)} %get-tuple-element.84), channel_id=1, source_target_pairs={{0,2},{1,66},{2,4},{3,68},{4,6},{5,70},{6,0},{7,64},{8,10},{9,74},... | collective-permute-start | bytes 786440 | tf_op jit(solution)/shard_map/ppermute | solution.py:45
  132.0 7.3 %collective-permute-start.19 = (bf16[256,512]{1,0:T(8,128)(2,1)S(1)}, bf16[256,512]{1,0:T(8,128)(2,1)S(1)}, u32[]{:S(2)}, u32[]{:S(2)}) collective-permute-start(bf16[256,512]{1,0:T(8,128)(2,1)S(1)} %get-tuple-element.85), channel_id=1, source_target_pairs={{0,4},{1,68},{2,6},{3,70},{4,0},{5,64},{6,2},{7,66},{8,12},{9,76},... | collective-permute-start | bytes 786440 | tf_op jit(solution)/shard_map/ppermute | solution.py:45
  139.4 3.4 %collective-permute-start.20 = (bf16[256,512]{1,0:T(8,128)(2,1)S(1)}, bf16[256,512]{1,0:T(8,128)(2,1)S(1)}, u32[]{:S(2)}, u32[]{:S(2)}) collective-permute-start(bf16[256,512]{1,0:T(8,128)(2,1)S(1)} %get-tuple-element.86), channel_id=1, source_target_pairs={{0,6},{1,70},{2,0},{3,64},{4,2},{5,66},{6,4},{7,68},{8,14},{9,78},... | collective-permute-start | bytes 786440 | tf_op jit(solution)/shard_map/ppermute | solution.py:45
  142.8 13.5 %collective-permute-done.19 = bf16[256,512]{1,0:T(8,128)(2,1)S(1)} collective-permute-done((bf16[256,512]{1,0:T(8,128)(2,1)S(1)}, bf16[256,512]{1,0:T(8,128)(2,1)S(1)}, u32[]{:S(2)}, u32[]{:S(2)}) %collective-permute-start.19) | collective-permute-done | bytes 262176 | tf_op jit(solution)/shard_map/ppermute | solution.py:45
  156.2 3.1 %collective-permute-done.20 = bf16[256,512]{1,0:T(8,128)(2,1)S(1)} collective-permute-done((bf16[256,512]{1,0:T(8,128)(2,1)S(1)}, bf16[256,512]{1,0:T(8,128)(2,1)S(1)}, u32[]{:S(2)}, u32[]{:S(2)}) %collective-permute-start.20) | collective-permute-done | bytes 262176 | tf_op jit(solution)/shard_map/ppermute | solution.py:45
  (52 shorter events, 27.6 us)
Async XLA Ops:
  1.3 10.8 %collective-permute-start = (bf16[80,512]{1,0:T(8,128)(2,1)S(1)}, bf16[80,512]{1,0:T(8,128)(2,1)S(1)}, u32[]{:S(2)}, u32[]{:S(2)}) collective-permute-start(bf16[80,512]{1,0:T(8,128)(2,1)S(1)} %prepare.1.a), channel_id=1, source_target_pairs={{0,32},{1,33},{2,34},{3,35},{4,36},{5,37},{6,38},{7,39},{8,40},{9,... | collective-permute-start | bytes 245768 | tf_op jit(solution)/shard_map/ppermute | solution.py:45
  12.1 11.7 %collective-permute-start.1 = (bf16[160,512]{1,0:T(8,128)(2,1)S(1)}, bf16[160,512]{1,0:T(8,128)(2,1)S(1)}, u32[]{:S(2)}, u32[]{:S(2)}) collective-permute-start(bf16[160,512]{1,0:T(8,128)(2,1)S(1)} %join.4.a), channel_id=1, source_target_pairs={{0,16},{1,17},{2,18},{3,19},{4,20},{5,21},{6,22},{7,23},{8,24},{9,... | collective-permute-start | bytes 491528 | tf_op jit(solution)/shard_map/ppermute | solution.py:45
  14.1 33.9 %collective-permute-start.4 = (bf16[512,512]{1,0:T(8,128)(2,1)S(1)}, bf16[512,512]{1,0:T(8,128)(2,1)S(1)}, u32[]{:S(2)}, u32[]{:S(2)}) collective-permute-start(bf16[512,512]{1,0:T(8,128)(2,1)S(1)} %stack.21.refs_0_), channel_id=1, source_target_pairs={{0,256},{1,257},{2,258},{3,259},{4,260},{5,261},{6,262},{7,263},{8... | collective-permute-start | bytes 1572872 | tf_op jit(solution)/shard_map/ppermute | solution.py:45
  19.8 30.1 %collective-permute-start.3 = (bf16[512,512]{1,0:T(8,128)(2,1)S(1)}, bf16[512,512]{1,0:T(8,128)(2,1)S(1)}, u32[]{:S(2)}, u32[]{:S(2)}) collective-permute-start(bf16[512,512]{1,0:T(8,128)(2,1)S(1)} %stack.21.refs_0_), channel_id=1, source_target_pairs={{0,64},{1,65},{2,66},{3,67},{4,68},{5,69},{6,70},{7,71},{8,72},{9,... | collective-permute-start | bytes 1572872 | tf_op jit(solution)/shard_map/ppermute | solution.py:45
  23.8 26.1 %collective-permute-start.5 = (bf16[512,512]{1,0:T(8,128)(2,1)S(1)}, bf16[512,512]{1,0:T(8,128)(2,1)S(1)}, u32[]{:S(2)}, u32[]{:S(2)}) collective-permute-start(bf16[512,512]{1,0:T(8,128)(2,1)S(1)} %stack.21.refs_0_), channel_id=1, source_target_pairs={{0,128},{1,129},{2,130},{3,131},{4,132},{5,133},{6,134},{7,135},{8... | collective-permute-start | bytes 1572872 | tf_op jit(solution)/shard_map/ppermute | solution.py:45
  26.1 9.7 %collective-permute-start.2 = (bf16[320,512]{1,0:T(8,128)(2,1)S(1)}, bf16[320,512]{1,0:T(8,128)(2,1)S(1)}, u32[]{:S(2)}, u32[]{:S(2)}) collective-permute-start(bf16[320,512]{1,0:T(8,128)(2,1)S(1)} %join.5.a), channel_id=1, source_target_pairs={{0,8},{1,9},{2,10},{3,11},{4,12},{5,13},{6,14},{7,15},{8,0},{9,1},... | collective-permute-start | bytes 983048 | tf_op jit(solution)/shard_map/ppermute | solution.py:45
  35.8 7.2 %collective-permute-start.6 = (bf16[128,512]{1,0:T(8,128)(2,1)S(1)}, bf16[128,512]{1,0:T(8,128)(2,1)S(1)}, u32[]{:S(2)}, u32[]{:S(2)}) collective-permute-start(bf16[128,512]{1,0:T(8,128)(2,1)S(1)} %pick.1), channel_id=1, source_target_pairs={{0,64},{1,65},{2,66},{3,67},{4,68},{5,69},{6,70},{7,71},{8,72},{9,... | collective-permute-start | bytes 393224 | tf_op jit(solution)/shard_map/ppermute | solution.py:45
  37.8 20.2 %collective-permute-start.9 = (bf16[512,512]{1,0:T(8,128)(2,1)S(1)}, bf16[512,512]{1,0:T(8,128)(2,1)S(1)}, u32[]{:S(2)}, u32[]{:S(2)}) collective-permute-start(bf16[512,512]{1,0:T(8,128)(2,1)S(1)} %stack.21.refs_0_), channel_id=1, source_target_pairs={{0,32},{1,33},{2,34},{3,35},{4,36},{5,37},{6,38},{7,39},{8,40},{9,... | collective-permute-start | bytes 1572872 | tf_op jit(solution)/shard_map/ppermute | solution.py:45
  43.1 15.8 %copy-start = (bf16[256,512]{1,0:T(8,128)(2,1)S(1)}, bf16[256,512]{1,0:T(8,128)(2,1)}, u32[]{:S(2)}) copy-start(bf16[256,512]{1,0:T(8,128)(2,1)} %q.5) | copy-start | bytes 786436
  43.1 15.8 %copy-start.1 = (s32[128,7]{0,1:T(8,128)S(1)}, s32[128,7]{0,1:T(8,128)}, u32[]{:S(2)}) copy-start(s32[128,7]{0,1:T(8,128)} %param.11) | copy-start | bytes 10756
  43.1 21.5 %collective-permute-start.8 = (bf16[768,512]{1,0:T(8,128)(2,1)S(1)}, bf16[768,512]{1,0:T(8,128)(2,1)S(1)}, u32[]{:S(2)}, u32[]{:S(2)}) collective-permute-start(bf16[768,512]{1,0:T(8,128)(2,1)S(1)} %join.7.refs_1_.w0), channel_id=1, source_target_pairs={{0,384},{1,385},{2,386},{3,387},{4,388},{5,389},{6,390},{7,391},{8... | collective-permute-start | bytes 2359304 | tf_op jit(solution)/shard_map/ppermute | solution.py:45
  48.0 18.8 %collective-permute-start.7 = (bf16[768,512]{1,0:T(8,128)(2,1)S(1)}, bf16[768,512]{1,0:T(8,128)(2,1)S(1)}, u32[]{:S(2)}, u32[]{:S(2)}) collective-permute-start(bf16[768,512]{1,0:T(8,128)(2,1)S(1)} %join.7.refs_1_.w0), channel_id=1, source_target_pairs={{0,128},{1,129},{2,130},{3,131},{4,132},{5,133},{6,134},{7,135},{8... | collective-permute-start | bytes 2359304 | tf_op jit(solution)/shard_map/ppermute | solution.py:45
  51.6 35.3 %collective-permute-start.13 = (bf16[512,512]{1,0:T(8,128)(2,1)S(1)}, bf16[512,512]{1,0:T(8,128)(2,1)S(1)}, u32[]{:S(2)}, u32[]{:S(2)}) collective-permute-start(bf16[512,512]{1,0:T(8,128)(2,1)S(1)} %stack.21.refs_0_), channel_id=1, source_target_pairs={{0,8},{1,9},{2,10},{3,11},{4,12},{5,13},{6,14},{7,15},{8,0},{9,1},... | collective-permute-start | bytes 1572872 | tf_op jit(solution)/shard_map/ppermute | solution.py:45
  54.6 36.5 %collective-permute-start.12 = (bf16[512,512]{1,0:T(8,128)(2,1)S(1)}, bf16[512,512]{1,0:T(8,128)(2,1)S(1)}, u32[]{:S(2)}, u32[]{:S(2)}) collective-permute-start(bf16[512,512]{1,0:T(8,128)(2,1)S(1)} %stack.21.refs_0_), channel_id=1, source_target_pairs={{0,16},{1,17},{2,18},{3,19},{4,20},{5,21},{6,22},{7,23},{8,24},{9,... | collective-permute-start | bytes 1572872 | tf_op jit(solution)/shard_map/ppermute | solution.py:45
  66.8 25.2 %collective-permute-start.10 = (bf16[400,512]{1,0:T(8,128)(2,1)S(1)}, bf16[400,512]{1,0:T(8,128)(2,1)S(1)}, u32[]{:S(2)}, u32[]{:S(2)}) collective-permute-start(bf16[400,512]{1,0:T(8,128)(2,1)S(1)} %slice.6), channel_id=1, source_target_pairs={{0,128},{1,129},{2,130},{3,131},{4,132},{5,133},{6,134},{7,135},{8... | collective-permute-start | bytes 1228808 | tf_op jit(solution)/shard_map/ppermute | solution.py:45
  68.8 23.2 %collective-permute-start.11 = (bf16[368,512]{1,0:T(8,128)(2,1)S(1)}, bf16[368,512]{1,0:T(8,128)(2,1)S(1)}, u32[]{:S(2)}, u32[]{:S(2)}) collective-permute-start(bf16[368,512]{1,0:T(8,128)(2,1)S(1)} %slice.7), channel_id=1, source_target_pairs={{0,384},{1,385},{2,386},{3,387},{4,388},{5,389},{6,390},{7,391},{8... | collective-permute-start | bytes 1130504 | tf_op jit(solution)/shard_map/ppermute | solution.py:45
  86.9 4.3 %copy-start.2 = (bf16[512,512]{1,0:T(8,128)(2,1)}, bf16[512,512]{1,0:T(8,128)(2,1)S(1)}, u32[]{:S(2)}) copy-start(bf16[512,512]{1,0:T(8,128)(2,1)S(1)} %collective-permute-done.13.refs_1_.refs_6_) | copy-start | bytes 1572868
  92.7 27.0 %collective-permute-start.16 = (bf16[4,512,512]{2,1,0:T(8,128)(2,1)S(1)}, bf16[4,512,512]{2,1,0:T(8,128)(2,1)S(1)}, u32[]{:S(2)}, u32[]{:S(2)}) collective-permute-start(bf16[4,512,512]{2,1,0:T(8,128)(2,1)S(1)} %pack.1.w_mine), channel_id=1, source_target_pairs={{0,1},{1,0},{2,3},{3,2},{4,5},{5,4},{6,7},{7,6},{8,9},{9,8},{10,11... | collective-permute-start | bytes 6291464 | tf_op jit(solution)/shard_map/ppermute | solution.py:45
  109.2 7.7 %collective-permute-start.15 = (bf16[256,512]{1,0:T(8,128)(2,1)S(1)}, bf16[256,512]{1,0:T(8,128)(2,1)S(1)}, u32[]{:S(2)}, u32[]{:S(2)}) collective-permute-start(bf16[256,512]{1,0:T(8,128)(2,1)S(1)} %attend.5.mine), channel_id=1, source_target_pairs={{0,0},{1,64},{2,2},{3,66},{4,4},{5,68},{6,6},{7,70},{8,8},{9,72},{... | collective-permute-start | bytes 786440 | tf_op jit(solution)/shard_map/ppermute | solution.py:45
  112.6 7.1 %collective-permute-start.14 = (bf16[256,512]{1,0:T(8,128)(2,1)S(1)}, bf16[256,512]{1,0:T(8,128)(2,1)S(1)}, u32[]{:S(2)}, u32[]{:S(2)}) collective-permute-start(bf16[256,512]{1,0:T(8,128)(2,1)S(1)} %attend.5.mine), channel_id=1, source_target_pairs={{0,64},{1,0},{2,66},{3,2},{4,68},{5,4},{6,70},{7,6},{8,72},{9,8},{... | collective-permute-start | bytes 786440 | tf_op jit(solution)/shard_map/ppermute | solution.py:45
  121.5 21.2 %collective-permute-start.17 = (bf16[256,512]{1,0:T(8,128)(2,1)S(1)}, bf16[256,512]{1,0:T(8,128)(2,1)S(1)}, u32[]{:S(2)}, u32[]{:S(2)}) collective-permute-start(bf16[256,512]{1,0:T(8,128)(2,1)S(1)} %get-tuple-element.83), channel_id=1, source_target_pairs={{0,0},{1,64},{2,2},{3,66},{4,4},{5,68},{6,6},{7,70},{8,8},{9,72},{... | collective-permute-start | bytes 786440 | tf_op jit(solution)/shard_map/ppermute | solution.py:45
  124.9 17.9 %collective-permute-start.18 = (bf16[256,512]{1,0:T(8,128)(2,1)S(1)}, bf16[256,512]{1,0:T(8,128)(2,1)S(1)}, u32[]{:S(2)}, u32[]{:S(2)}) collective-permute-start(bf16[256,512]{1,0:T(8,128)(2,1)S(1)} %get-tuple-element.84), channel_id=1, source_target_pairs={{0,2},{1,66},{2,4},{3,68},{4,6},{5,70},{6,0},{7,64},{8,10},{9,74},... | collective-permute-start | bytes 786440 | tf_op jit(solution)/shard_map/ppermute | solution.py:45
  132.0 24.2 %collective-permute-start.19 = (bf16[256,512]{1,0:T(8,128)(2,1)S(1)}, bf16[256,512]{1,0:T(8,128)(2,1)S(1)}, u32[]{:S(2)}, u32[]{:S(2)}) collective-permute-start(bf16[256,512]{1,0:T(8,128)(2,1)S(1)} %get-tuple-element.85), channel_id=1, source_target_pairs={{0,4},{1,68},{2,6},{3,70},{4,0},{5,64},{6,2},{7,66},{8,12},{9,76},... | collective-permute-start | bytes 786440 | tf_op jit(solution)/shard_map/ppermute | solution.py:45
  139.4 20.0 %collective-permute-start.20 = (bf16[256,512]{1,0:T(8,128)(2,1)S(1)}, bf16[256,512]{1,0:T(8,128)(2,1)S(1)}, u32[]{:S(2)}, u32[]{:S(2)}) collective-permute-start(bf16[256,512]{1,0:T(8,128)(2,1)S(1)} %get-tuple-element.86), channel_id=1, source_target_pairs={{0,6},{1,70},{2,0},{3,64},{4,2},{5,66},{6,4},{7,68},{8,14},{9,78},... | collective-permute-start | bytes 786440 | tf_op jit(solution)/shard_map/ppermute | solution.py:45
  (5 other events, 5.2 us)

commit v4 on v3

--- a/solution.py
+++ b/solution.py
@@ -14,8 +14,10 @@
 LROWS = 16
 UNIT = WROWS + LROWS
 HALF = 400
-COST = 64
+COST = 1
 COST0 = 64
+COST2 = 1
+COST3 = 0
 COST1 = 0
 AXES = ("ctx", "head")
 SCALE = HD**-0.5
@@ -393,10 +395,11 @@
     token = arrived(COST0, far[3], far[5], far[4])
     kv, token, wl = lax.optimization_barrier((kv, token, wl))
     far.update({level: send(kv, xor(level)) for level in (1, 0)})
-    state = step((3, 5, 4, 2), far, own=kv, mark=[(wl, every)], token=token, cost=COST)
+    state = step((3, 5, 4), far, own=kv, mark=[(wl, every)], token=token, cost=COST2)
     wl1, wl3, state = lax.optimization_barrier((wl1, wl3, state))
     wl2a, wl2b = send(wl1[:HALF], along_x(1)), send(wl3[HALF:], along_x(-1))
-    state = step((), far, state=state, mark=[(wl1, every), (wl3, every)])
+    token = arrived(COST3, far[2])
+    state = step((2,), far, state=state, mark=[(wl1, every), (wl3, every)], token=token, cost=COST)
     rest = [(wl2a, mark_starts(0, HALF)), (wl2b, mark_starts(HALF, 768))]
     late, state = lax.optimization_barrier(((far[1], far[0]), state))
     far[1], far[0] = late

time: 161 us -> 154 us (0.957)
  the two profiles are of different devices: /device:TPU:17 before, /device:TPU:1 now
where the time goes in v4:
time: 154 us; the launch traced here: 153 us
  starting transfers between devices  80.5 us (52%)
  waiting for transfers between devices  48.1 us (31%)
  Pallas kernels  20.2 us (13%)
  local copies, waits for them, and re-layouts  3.28 us (2%)
    ppermute x21, starting transfers between devices, send(): return lax.ppermute(a, AXES, pairs)  80.5 us
    ppermute x21, waiting for transfers between devices, send(): return lax.ppermute(a, AXES, pairs)  48.1 us
    pallas_call x3, Pallas kernels, attend(): pl.pallas_call(functools.partial(attend_kernel, levels, own is not None,...  15.2 us
    unnamed x16, local copies, waits for them, and re-layouts  3.22 us
  transfers between devices with their start and end apart: 21, of which 10 were waited for; matrix products, arithmetic and copies ran while one was open for 0% of the time, Pallas kernels for 11%

profile of v4, /device:TPU:1, one launch (start us, length us, event | category | flops | bytes accessed | tf_op | source)
XLA Modules:
  0.0 153.4 jit_solution(6784409602943340842)
XLA Ops:
  1.3 8.3 %collective-permute-start = (bf16[80,512]{1,0:T(8,128)(2,1)S(1)}, bf16[80,512]{1,0:T(8,128)(2,1)S(1)}, u32[]{:S(2)}, u32[]{:S(2)}) collective-permute-start(bf16[80,512]{1,0:T(8,128)(2,1)S(1)} %prepare.1.a), channel_id=1, source_target_pairs={{0,32},{1,33},{2,34},{3,35},{4,36},{5,37},{6,38},{7,39},{8,40},{9,... | collective-permute-start | bytes 245768 | tf_op jit(solution)/shard_map/ppermute | solution.py:47
  11.5 5.7 %collective-permute-start.1 = (bf16[160,512]{1,0:T(8,128)(2,1)S(1)}, bf16[160,512]{1,0:T(8,128)(2,1)S(1)}, u32[]{:S(2)}, u32[]{:S(2)}) collective-permute-start(bf16[160,512]{1,0:T(8,128)(2,1)S(1)} %join.4.a), channel_id=1, source_target_pairs={{0,16},{1,17},{2,18},{3,19},{4,20},{5,21},{6,22},{7,23},{8,24},{9,... | collective-permute-start | bytes 491528 | tf_op jit(solution)/shard_map/ppermute | solution.py:47
  17.2 5.7 %collective-permute-start.4 = (bf16[512,512]{1,0:T(8,128)(2,1)S(1)}, bf16[512,512]{1,0:T(8,128)(2,1)S(1)}, u32[]{:S(2)}, u32[]{:S(2)}) collective-permute-start(bf16[512,512]{1,0:T(8,128)(2,1)S(1)} %stack.21.refs_0_), channel_id=1, source_target_pairs={{0,256},{1,257},{2,258},{3,259},{4,260},{5,261},{6,262},{7,263},{8... | collective-permute-start | bytes 1572872 | tf_op jit(solution)/shard_map/ppermute | solution.py:47
  22.9 4.0 %collective-permute-start.3 = (bf16[512,512]{1,0:T(8,128)(2,1)S(1)}, bf16[512,512]{1,0:T(8,128)(2,1)S(1)}, u32[]{:S(2)}, u32[]{:S(2)}) collective-permute-start(bf16[512,512]{1,0:T(8,128)(2,1)S(1)} %stack.21.refs_0_), channel_id=1, source_target_pairs={{0,64},{1,65},{2,66},{3,67},{4,68},{5,69},{6,70},{7,71},{8,72},{9,... | collective-permute-start | bytes 1572872 | tf_op jit(solution)/shard_map/ppermute | solution.py:47
  31.1 7.5 %collective-permute-done.2.b = bf16[320,512]{1,0:T(8,128)(2,1)S(1)} collective-permute-done((bf16[320,512]{1,0:T(8,128)(2,1)S(1)}, bf16[320,512]{1,0:T(8,128)(2,1)S(1)}, u32[]{:S(2)}, u32[]{:S(2)}) %collective-permute-start.2) | collective-permute-done | bytes 327712 | tf_op jit(solution)/shard_map/ppermute | solution.py:47
  38.6 3.1 %collective-permute-start.6 = (bf16[128,512]{1,0:T(8,128)(2,1)S(1)}, bf16[128,512]{1,0:T(8,128)(2,1)S(1)}, u32[]{:S(2)}, u32[]{:S(2)}) collective-permute-start(bf16[128,512]{1,0:T(8,128)(2,1)S(1)} %pick.1), channel_id=1, source_target_pairs={{0,64},{1,65},{2,66},{3,67},{4,68},{5,69},{6,70},{7,71},{8,72},{9,... | collective-permute-start | bytes 393224 | tf_op jit(solution)/shard_map/ppermute | solution.py:47
  41.7 5.3 %collective-permute-start.13 = (bf16[512,512]{1,0:T(8,128)(2,1)S(1)}, bf16[512,512]{1,0:T(8,128)(2,1)S(1)}, u32[]{:S(2)}, u32[]{:S(2)}) collective-permute-start(bf16[512,512]{1,0:T(8,128)(2,1)S(1)} %stack.21.refs_0_), channel_id=1, source_target_pairs={{0,32},{1,33},{2,34},{3,35},{4,36},{5,37},{6,38},{7,39},{8,40},{9,... | collective-permute-start | bytes 1572872 | tf_op jit(solution)/shard_map/ppermute | solution.py:47
  47.2 3.9 %collective-permute-start.8 = (bf16[768,512]{1,0:T(8,128)(2,1)S(1)}, bf16[768,512]{1,0:T(8,128)(2,1)S(1)}, u32[]{:S(2)}, u32[]{:S(2)}) collective-permute-start(bf16[768,512]{1,0:T(8,128)(2,1)S(1)} %join.7.refs_1_.w0), channel_id=1, source_target_pairs={{0,384},{1,385},{2,386},{3,387},{4,388},{5,389},{6,390},{7,391},{8... | collective-permute-start | bytes 2359304 | tf_op jit(solution)/shard_map/ppermute | solution.py:47
  56.8 2.8 %collective-permute-start.11 = (bf16[512,512]{1,0:T(8,128)(2,1)S(1)}, bf16[512,512]{1,0:T(8,128)(2,1)S(1)}, u32[]{:S(2)}, u32[]{:S(2)}) collective-permute-start(bf16[512,512]{1,0:T(8,128)(2,1)S(1)} %stack.21.refs_0_), channel_id=1, source_target_pairs={{0,16},{1,17},{2,18},{3,19},{4,20},{5,21},{6,22},{7,23},{8,24},{9,... | collective-permute-start | bytes 1572872 | tf_op jit(solution)/shard_map/ppermute | solution.py:47
  59.7 5.2 %attend.3 = (f32[256,512]{1,0:T(8,128)S(1)}, f32[256,512]{1,0:T(8,128)S(1)}, f32[256,512]{1,0:T(8,128)S(1)}) custom-call(s32[4]{0:T(128)S(1)} %pad_add_fusion.place, s32[7,128]{1,0:T(8,128)S(1)} %bitcast.6, bf16[256,512]{1,0:T(8,128)(2,1)S(1)} %copy-done, bf16[512,512]{1,0:T(8,128)(2,1)S(1)} %stack.21.refs_0_, bf16[768,512]{1,0:T(8,128)(2,1)S(1)} %join.7.refs_1_.w0, ...), custom_call_target="tpu_custom_call" | custom-call | flops 402653184 | bytes 4194304 | tf_op jit(solution)/shard_map/attend/pallas_call | solution.py:240
  65.1 4.7 %collective-permute-done.7.refs_3_.w1 = bf16[768,512]{1,0:T(8,128)(2,1)S(1)} collective-permute-done((bf16[768,512]{1,0:T(8,128)(2,1)S(1)}, bf16[768,512]{1,0:T(8,128)(2,1)S(1)}, u32[]{:S(2)}, u32[]{:S(2)}) %collective-permute-start.7) | collective-permute-done | bytes 786464 | tf_op jit(solution)/shard_map/ppermute | solution.py:47
  71.8 4.6 %collective-permute-start.10 = (bf16[368,512]{1,0:T(8,128)(2,1)S(1)}, bf16[368,512]{1,0:T(8,128)(2,1)S(1)}, u32[]{:S(2)}, u32[]{:S(2)}) collective-permute-start(bf16[368,512]{1,0:T(8,128)(2,1)S(1)} %slice.7), channel_id=1, source_target_pairs={{0,384},{1,385},{2,386},{3,387},{4,388},{5,389},{6,390},{7,391},{8... | collective-permute-start | bytes 1130504 | tf_op jit(solution)/shard_map/ppermute | solution.py:47
  77.2 4.9 %attend.4 = (f32[256,512]{1,0:T(8,128)S(1)}, f32[256,512]{1,0:T(8,128)S(1)}, f32[256,512]{1,0:T(8,128)S(1)}) custom-call(s32[4]{0:T(128)S(1)} %pad_add_fusion.place, s32[7,128]{1,0:T(8,128)S(1)} %bitcast.7, bf16[256,512]{1,0:T(8,128)(2,1)S(1)} %copy-done, f32[256,512]{1,0:T(8,128)S(1)} %get-tuple-element.63.refs_0_, ...), custom_call_target="tpu_custom_call" | custom-call | flops 201326592 | bytes 4194304 | tf_op jit(solution)/shard_map/attend/pallas_call | solution.py:240
  82.2 9.9 %collective-permute-done.12.refs_1_.refs_6_ = bf16[512,512]{1,0:T(8,128)(2,1)S(1)} collective-permute-done((bf16[512,512]{1,0:T(8,128)(2,1)S(1)}, bf16[512,512]{1,0:T(8,128)(2,1)S(1)}, u32[]{:S(2)}, u32[]{:S(2)}) %collective-permute-start.12) | collective-permute-done | bytes 524320 | tf_op jit(solution)/shard_map/ppermute | solution.py:47
  95.9 2.9 %collective-permute-start.16 = (bf16[4,512,512]{2,1,0:T(8,128)(2,1)S(1)}, bf16[4,512,512]{2,1,0:T(8,128)(2,1)S(1)}, u32[]{:S(2)}, u32[]{:S(2)}) collective-permute-start(bf16[4,512,512]{2,1,0:T(8,128)(2,1)S(1)} %pack.1.w_mine), channel_id=1, source_target_pairs={{0,1},{1,0},{2,3},{3,2},{4,5},{5,4},{6,7},{7,6},{8,9},{9,8},{10,11... | collective-permute-start | bytes 6291464 | tf_op jit(solution)/shard_map/ppermute | solution.py:47
  98.8 5.1 %attend.5.mine = bf16[256,512]{1,0:T(8,128)(2,1)S(1)} custom-call(s32[4]{0:T(128)S(1)} %pad_add_fusion.place, s32[7,128]{1,0:T(8,128)S(1)} %bitcast.8, bf16[256,512]{1,0:T(8,128)(2,1)S(1)} %copy-done, f32[256,512]{1,0:T(8,128)S(1)} %get-tuple-element.74.refs_0_, f32[256,512]{1,0:T(8,128)S(1)} %get-tuple-element.75.refs_1_, ...), custom_call_target="tpu_custom_call" | custom-call | flops 201326592 | bytes 4194304 | tf_op jit(solution)/shard_map/attend/pallas_call | solution.py:240
  103.9 2.5 %collective-permute-start.15 = (bf16[256,512]{1,0:T(8,128)(2,1)S(1)}, bf16[256,512]{1,0:T(8,128)(2,1)S(1)}, u32[]{:S(2)}, u32[]{:S(2)}) collective-permute-start(bf16[256,512]{1,0:T(8,128)(2,1)S(1)} %attend.5.mine), channel_id=1, source_target_pairs={{0,0},{1,64},{2,2},{3,66},{4,4},{5,68},{6,6},{7,70},{8,8},{9,72},{... | collective-permute-start | bytes 786440 | tf_op jit(solution)/shard_map/ppermute | solution.py:47
  108.3 4.1 %collective-permute-done.15.got2 = bf16[256,512]{1,0:T(8,128)(2,1)S(1)} collective-permute-done((bf16[256,512]{1,0:T(8,128)(2,1)S(1)}, bf16[256,512]{1,0:T(8,128)(2,1)S(1)}, u32[]{:S(2)}, u32[]{:S(2)}) %collective-permute-start.15) | collective-permute-done | bytes 262176 | tf_op jit(solution)/shard_map/ppermute | solution.py:47
  116.2 3.3 %collective-permute-start.17 = (bf16[256,512]{1,0:T(8,128)(2,1)S(1)}, bf16[256,512]{1,0:T(8,128)(2,1)S(1)}, u32[]{:S(2)}, u32[]{:S(2)}) collective-permute-start(bf16[256,512]{1,0:T(8,128)(2,1)S(1)} %get-tuple-element.83), channel_id=1, source_target_pairs={{0,0},{1,64},{2,2},{3,66},{4,4},{5,68},{6,6},{7,70},{8,8},{9,72},{... | collective-permute-start | bytes 786440 | tf_op jit(solution)/shard_map/ppermute | solution.py:47
  119.6 5.7 %collective-permute-start.18 = (bf16[256,512]{1,0:T(8,128)(2,1)S(1)}, bf16[256,512]{1,0:T(8,128)(2,1)S(1)}, u32[]{:S(2)}, u32[]{:S(2)}) collective-permute-start(bf16[256,512]{1,0:T(8,128)(2,1)S(1)} %get-tuple-element.84), channel_id=1, source_target_pairs={{0,2},{1,66},{2,4},{3,68},{4,6},{5,70},{6,0},{7,64},{8,10},{9,74},... | collective-permute-start | bytes 786440 | tf_op jit(solution)/shard_map/ppermute | solution.py:47
  125.3 7.3 %collective-permute-start.19 = (bf16[256,512]{1,0:T(8,128)(2,1)S(1)}, bf16[256,512]{1,0:T(8,128)(2,1)S(1)}, u32[]{:S(2)}, u32[]{:S(2)}) collective-permute-start(bf16[256,512]{1,0:T(8,128)(2,1)S(1)} %get-tuple-element.85), channel_id=1, source_target_pairs={{0,4},{1,68},{2,6},{3,70},{4,0},{5,64},{6,2},{7,66},{8,12},{9,76},... | collective-permute-start | bytes 786440 | tf_op jit(solution)/shard_map/ppermute | solution.py:47
  132.6 3.4 %collective-permute-start.20 = (bf16[256,512]{1,0:T(8,128)(2,1)S(1)}, bf16[256,512]{1,0:T(8,128)(2,1)S(1)}, u32[]{:S(2)}, u32[]{:S(2)}) collective-permute-start(bf16[256,512]{1,0:T(8,128)(2,1)S(1)} %get-tuple-element.86), channel_id=1, source_target_pairs={{0,6},{1,70},{2,0},{3,64},{4,2},{5,66},{6,4},{7,68},{8,14},{9,78},... | collective-permute-start | bytes 786440 | tf_op jit(solution)/shard_map/ppermute | solution.py:47
  136.0 13.5 %collective-permute-done.19 = bf16[256,512]{1,0:T(8,128)(2,1)S(1)} collective-permute-done((bf16[256,512]{1,0:T(8,128)(2,1)S(1)}, bf16[256,512]{1,0:T(8,128)(2,1)S(1)}, u32[]{:S(2)}, u32[]{:S(2)}) %collective-permute-start.19) | collective-permute-done | bytes 262176 | tf_op jit(solution)/shard_map/ppermute | solution.py:47
  149.5 3.1 %collective-permute-done.20 = bf16[256,512]{1,0:T(8,128)(2,1)S(1)} collective-permute-done((bf16[256,512]{1,0:T(8,128)(2,1)S(1)}, bf16[256,512]{1,0:T(8,128)(2,1)S(1)}, u32[]{:S(2)}, u32[]{:S(2)}) %collective-permute-start.20) | collective-permute-done | bytes 262176 | tf_op jit(solution)/shard_map/ppermute | solution.py:47
  (53 shorter events, 26.7 us)
Async XLA Ops:
  1.3 10.2 %collective-permute-start = (bf16[80,512]{1,0:T(8,128)(2,1)S(1)}, bf16[80,512]{1,0:T(8,128)(2,1)S(1)}, u32[]{:S(2)}, u32[]{:S(2)}) collective-permute-start(bf16[80,512]{1,0:T(8,128)(2,1)S(1)} %prepare.1.a), channel_id=1, source_target_pairs={{0,32},{1,33},{2,34},{3,35},{4,36},{5,37},{6,38},{7,39},{8,40},{9,... | collective-permute-start | bytes 245768 | tf_op jit(solution)/shard_map/ppermute | solution.py:47
  11.5 15.4 %collective-permute-start.1 = (bf16[160,512]{1,0:T(8,128)(2,1)S(1)}, bf16[160,512]{1,0:T(8,128)(2,1)S(1)}, u32[]{:S(2)}, u32[]{:S(2)}) collective-permute-start(bf16[160,512]{1,0:T(8,128)(2,1)S(1)} %join.4.a), channel_id=1, source_target_pairs={{0,16},{1,17},{2,18},{3,19},{4,20},{5,21},{6,22},{7,23},{8,24},{9,... | collective-permute-start | bytes 491528 | tf_op jit(solution)/shard_map/ppermute | solution.py:47
  17.2 33.9 %collective-permute-start.4 = (bf16[512,512]{1,0:T(8,128)(2,1)S(1)}, bf16[512,512]{1,0:T(8,128)(2,1)S(1)}, u32[]{:S(2)}, u32[]{:S(2)}) collective-permute-start(bf16[512,512]{1,0:T(8,128)(2,1)S(1)} %stack.21.refs_0_), channel_id=1, source_target_pairs={{0,256},{1,257},{2,258},{3,259},{4,260},{5,261},{6,262},{7,263},{8... | collective-permute-start | bytes 1572872 | tf_op jit(solution)/shard_map/ppermute | solution.py:47
  22.9 30.1 %collective-permute-start.3 = (bf16[512,512]{1,0:T(8,128)(2,1)S(1)}, bf16[512,512]{1,0:T(8,128)(2,1)S(1)}, u32[]{:S(2)}, u32[]{:S(2)}) collective-permute-start(bf16[512,512]{1,0:T(8,128)(2,1)S(1)} %stack.21.refs_0_), channel_id=1, source_target_pairs={{0,64},{1,65},{2,66},{3,67},{4,68},{5,69},{6,70},{7,71},{8,72},{9,... | collective-permute-start | bytes 1572872 | tf_op jit(solution)/shard_map/ppermute | solution.py:47
  27.0 26.1 %collective-permute-start.5 = (bf16[512,512]{1,0:T(8,128)(2,1)S(1)}, bf16[512,512]{1,0:T(8,128)(2,1)S(1)}, u32[]{:S(2)}, u32[]{:S(2)}) collective-permute-start(bf16[512,512]{1,0:T(8,128)(2,1)S(1)} %stack.21.refs_0_), channel_id=1, source_target_pairs={{0,128},{1,129},{2,130},{3,131},{4,132},{5,133},{6,134},{7,135},{8... | collective-permute-start | bytes 1572872 | tf_op jit(solution)/shard_map/ppermute | solution.py:47
  29.2 9.4 %collective-permute-start.2 = (bf16[320,512]{1,0:T(8,128)(2,1)S(1)}, bf16[320,512]{1,0:T(8,128)(2,1)S(1)}, u32[]{:S(2)}, u32[]{:S(2)}) collective-permute-start(bf16[320,512]{1,0:T(8,128)(2,1)S(1)} %join.5.a), channel_id=1, source_target_pairs={{0,8},{1,9},{2,10},{3,11},{4,12},{5,13},{6,14},{7,15},{8,0},{9,1},... | collective-permute-start | bytes 983048 | tf_op jit(solution)/shard_map/ppermute | solution.py:47
  38.6 8.5 %collective-permute-start.6 = (bf16[128,512]{1,0:T(8,128)(2,1)S(1)}, bf16[128,512]{1,0:T(8,128)(2,1)S(1)}, u32[]{:S(2)}, u32[]{:S(2)}) collective-permute-start(bf16[128,512]{1,0:T(8,128)(2,1)S(1)} %pick.1), channel_id=1, source_target_pairs={{0,64},{1,65},{2,66},{3,67},{4,68},{5,69},{6,70},{7,71},{8,72},{9,... | collective-permute-start | bytes 393224 | tf_op jit(solution)/shard_map/ppermute | solution.py:47
  41.7 34.7 %collective-permute-start.13 = (bf16[512,512]{1,0:T(8,128)(2,1)S(1)}, bf16[512,512]{1,0:T(8,128)(2,1)S(1)}, u32[]{:S(2)}, u32[]{:S(2)}) collective-permute-start(bf16[512,512]{1,0:T(8,128)(2,1)S(1)} %stack.21.refs_0_), channel_id=1, source_target_pairs={{0,32},{1,33},{2,34},{3,35},{4,36},{5,37},{6,38},{7,39},{8,40},{9,... | collective-permute-start | bytes 1572872 | tf_op jit(solution)/shard_map/ppermute | solution.py:47
  47.2 12.5 %copy-start = (bf16[256,512]{1,0:T(8,128)(2,1)S(1)}, bf16[256,512]{1,0:T(8,128)(2,1)}, u32[]{:S(2)}) copy-start(bf16[256,512]{1,0:T(8,128)(2,1)} %q.5) | copy-start | bytes 786436
  47.2 12.5 %copy-start.1 = (s32[128,7]{0,1:T(8,128)S(1)}, s32[128,7]{0,1:T(8,128)}, u32[]{:S(2)}) copy-start(s32[128,7]{0,1:T(8,128)} %param.11) | copy-start | bytes 10756
  47.2 18.0 %collective-permute-start.8 = (bf16[768,512]{1,0:T(8,128)(2,1)S(1)}, bf16[768,512]{1,0:T(8,128)(2,1)S(1)}, u32[]{:S(2)}, u32[]{:S(2)}) collective-permute-start(bf16[768,512]{1,0:T(8,128)(2,1)S(1)} %join.7.refs_1_.w0), channel_id=1, source_target_pairs={{0,384},{1,385},{2,386},{3,387},{4,388},{5,389},{6,390},{7,391},{8... | collective-permute-start | bytes 2359304 | tf_op jit(solution)/shard_map/ppermute | solution.py:47
  51.1 18.8 %collective-permute-start.7 = (bf16[768,512]{1,0:T(8,128)(2,1)S(1)}, bf16[768,512]{1,0:T(8,128)(2,1)S(1)}, u32[]{:S(2)}, u32[]{:S(2)}) collective-permute-start(bf16[768,512]{1,0:T(8,128)(2,1)S(1)} %join.7.refs_1_.w0), channel_id=1, source_target_pairs={{0,128},{1,129},{2,130},{3,131},{4,132},{5,133},{6,134},{7,135},{8... | collective-permute-start | bytes 2359304 | tf_op jit(solution)/shard_map/ppermute | solution.py:47
  54.6 37.4 %collective-permute-start.12 = (bf16[512,512]{1,0:T(8,128)(2,1)S(1)}, bf16[512,512]{1,0:T(8,128)(2,1)S(1)}, u32[]{:S(2)}, u32[]{:S(2)}) collective-permute-start(bf16[512,512]{1,0:T(8,128)(2,1)S(1)} %stack.21.refs_0_), channel_id=1, source_target_pairs={{0,8},{1,9},{2,10},{3,11},{4,12},{5,13},{6,14},{7,15},{8,0},{9,1},... | collective-permute-start | bytes 1572872 | tf_op jit(solution)/shard_map/ppermute | solution.py:47
  56.8 37.5 %collective-permute-start.11 = (bf16[512,512]{1,0:T(8,128)(2,1)S(1)}, bf16[512,512]{1,0:T(8,128)(2,1)S(1)}, u32[]{:S(2)}, u32[]{:S(2)}) collective-permute-start(bf16[512,512]{1,0:T(8,128)(2,1)S(1)} %stack.21.refs_0_), channel_id=1, source_target_pairs={{0,16},{1,17},{2,18},{3,19},{4,20},{5,21},{6,22},{7,23},{8,24},{9,... | collective-permute-start | bytes 1572872 | tf_op jit(solution)/shard_map/ppermute | solution.py:47
  69.9 25.3 %collective-permute-start.9 = (bf16[400,512]{1,0:T(8,128)(2,1)S(1)}, bf16[400,512]{1,0:T(8,128)(2,1)S(1)}, u32[]{:S(2)}, u32[]{:S(2)}) collective-permute-start(bf16[400,512]{1,0:T(8,128)(2,1)S(1)} %slice.6), channel_id=1, source_target_pairs={{0,128},{1,129},{2,130},{3,131},{4,132},{5,133},{6,134},{7,135},{8... | collective-permute-start | bytes 1228808 | tf_op jit(solution)/shard_map/ppermute | solution.py:47
  71.8 23.3 %collective-permute-start.10 = (bf16[368,512]{1,0:T(8,128)(2,1)S(1)}, bf16[368,512]{1,0:T(8,128)(2,1)S(1)}, u32[]{:S(2)}, u32[]{:S(2)}) collective-permute-start(bf16[368,512]{1,0:T(8,128)(2,1)S(1)} %slice.7), channel_id=1, source_target_pairs={{0,384},{1,385},{2,386},{3,387},{4,388},{5,389},{6,390},{7,391},{8... | collective-permute-start | bytes 1130504 | tf_op jit(solution)/shard_map/ppermute | solution.py:47
  92.1 2.3 %copy-start.2 = (bf16[512,512]{1,0:T(8,128)(2,1)}, bf16[512,512]{1,0:T(8,128)(2,1)S(1)}, u32[]{:S(2)}) copy-start(bf16[512,512]{1,0:T(8,128)(2,1)S(1)} %collective-permute-done.12.refs_1_.refs_6_) | copy-start | bytes 1572868
  95.9 18.5 %collective-permute-start.16 = (bf16[4,512,512]{2,1,0:T(8,128)(2,1)S(1)}, bf16[4,512,512]{2,1,0:T(8,128)(2,1)S(1)}, u32[]{:S(2)}, u32[]{:S(2)}) collective-permute-start(bf16[4,512,512]{2,1,0:T(8,128)(2,1)S(1)} %pack.1.w_mine), channel_id=1, source_target_pairs={{0,1},{1,0},{2,3},{3,2},{4,5},{5,4},{6,7},{7,6},{8,9},{9,8},{10,11... | collective-permute-start | bytes 6291464 | tf_op jit(solution)/shard_map/ppermute | solution.py:47
  103.9 8.5 %collective-permute-start.15 = (bf16[256,512]{1,0:T(8,128)(2,1)S(1)}, bf16[256,512]{1,0:T(8,128)(2,1)S(1)}, u32[]{:S(2)}, u32[]{:S(2)}) collective-permute-start(bf16[256,512]{1,0:T(8,128)(2,1)S(1)} %attend.5.mine), channel_id=1, source_target_pairs={{0,0},{1,64},{2,2},{3,66},{4,4},{5,68},{6,6},{7,70},{8,8},{9,72},{... | collective-permute-start | bytes 786440 | tf_op jit(solution)/shard_map/ppermute | solution.py:47
  106.4 8.0 %collective-permute-start.14 = (bf16[256,512]{1,0:T(8,128)(2,1)S(1)}, bf16[256,512]{1,0:T(8,128)(2,1)S(1)}, u32[]{:S(2)}, u32[]{:S(2)}) collective-permute-start(bf16[256,512]{1,0:T(8,128)(2,1)S(1)} %attend.5.mine), channel_id=1, source_target_pairs={{0,64},{1,0},{2,66},{3,2},{4,68},{5,4},{6,70},{7,6},{8,72},{9,8},{... | collective-permute-start | bytes 786440 | tf_op jit(solution)/shard_map/ppermute | solution.py:47
  116.2 19.8 %collective-permute-start.17 = (bf16[256,512]{1,0:T(8,128)(2,1)S(1)}, bf16[256,512]{1,0:T(8,128)(2,1)S(1)}, u32[]{:S(2)}, u32[]{:S(2)}) collective-permute-start(bf16[256,512]{1,0:T(8,128)(2,1)S(1)} %get-tuple-element.83), channel_id=1, source_target_pairs={{0,0},{1,64},{2,2},{3,66},{4,4},{5,68},{6,6},{7,70},{8,8},{9,72},{... | collective-permute-start | bytes 786440 | tf_op jit(solution)/shard_map/ppermute | solution.py:47
  119.6 16.4 %collective-permute-start.18 = (bf16[256,512]{1,0:T(8,128)(2,1)S(1)}, bf16[256,512]{1,0:T(8,128)(2,1)S(1)}, u32[]{:S(2)}, u32[]{:S(2)}) collective-permute-start(bf16[256,512]{1,0:T(8,128)(2,1)S(1)} %get-tuple-element.84), channel_id=1, source_target_pairs={{0,2},{1,66},{2,4},{3,68},{4,6},{5,70},{6,0},{7,64},{8,10},{9,74},... | collective-permute-start | bytes 786440 | tf_op jit(solution)/shard_map/ppermute | solution.py:47
  125.3 24.2 %collective-permute-start.19 = (bf16[256,512]{1,0:T(8,128)(2,1)S(1)}, bf16[256,512]{1,0:T(8,128)(2,1)S(1)}, u32[]{:S(2)}, u32[]{:S(2)}) collective-permute-start(bf16[256,512]{1,0:T(8,128)(2,1)S(1)} %get-tuple-element.85), channel_id=1, source_target_pairs={{0,4},{1,68},{2,6},{3,70},{4,0},{5,64},{6,2},{7,66},{8,12},{9,76},... | collective-permute-start | bytes 786440 | tf_op jit(solution)/shard_map/ppermute | solution.py:47
  132.6 20.0 %collective-permute-start.20 = (bf16[256,512]{1,0:T(8,128)(2,1)S(1)}, bf16[256,512]{1,0:T(8,128)(2,1)S(1)}, u32[]{:S(2)}, u32[]{:S(2)}) collective-permute-start(bf16[256,512]{1,0:T(8,128)(2,1)S(1)} %get-tuple-element.86), channel_id=1, source_target_pairs={{0,6},{1,70},{2,0},{3,64},{4,2},{5,66},{6,4},{7,68},{8,14},{9,78},... | collective-permute-start | bytes 786440 | tf_op jit(solution)/shard_map/ppermute | solution.py:47
  (5 other events, 5.2 us)

commit v5 on v4

--- a/solution.py
+++ b/solution.py
@@ -132,23 +132,34 @@
     )(in_hbm(keys), in_hbm(values))
 
 
-def softmax_step(state, q, ks, vs):
-    scores = [dot_nt(q, k) * SCALE for k in ks]
-    top = functools.reduce(jnp.maximum, [jnp.max(s, axis=1, keepdims=True) for s in scores])
-    if state is not None:
-        old_top, old_sum, old_acc = state
-        top = jnp.maximum(top, old_top)
-    weights = [jnp.exp(s - top) for s in scores]
-    total = sum(jnp.sum(w, axis=1, keepdims=True) for w in weights)
-    acc = sum(
-        jnp.dot(w.astype(BF16), v, preferred_element_type=F32)
-        for w, v in zip(weights, vs, strict=True)
-    )
-    if state is not None:
-        fade = jnp.exp(old_top - top)
-        total = total + old_sum * fade
-        acc = acc + old_acc * fade
-    return top, total, acc
+def softmax_steps(states, qs, ks, vs):
+    scores = [[dot_nt(q, k) * SCALE for k in row] for q, row in zip(qs, ks, strict=True)]
+    tops = [
+        jnp.max(functools.reduce(jnp.maximum, [p for s in row for p in tiles(s)]), axis=1, keepdims=True)
+        for row in scores
+    ]
+    if states[0] is not None:
+        tops = [jnp.maximum(t, old[0]) for t, old in zip(tops, states, strict=True)]
+    weights = [[jnp.exp(s - t) for s in row] for row, t in zip(scores, tops, strict=True)]
+    sums = [
+        jnp.sum(sum(p for w in row for p in tiles(w)), axis=1, keepdims=True) for row in weights
+    ]
+    accs = [
+        sum(
+            jnp.dot(w.astype(BF16), v, preferred_element_type=F32)
+            for w, v in zip(row, vrow, strict=True)
+        )
+        for row, vrow in zip(weights, vs, strict=True)
+    ]
+    if states[0] is not None:
+        fades = [jnp.exp(old[0] - t) for old, t in zip(states, tops, strict=True)]
+        sums = [s + old[1] * f for s, old, f in zip(sums, states, fades, strict=True)]
+        accs = [a + old[2] * f for a, old, f in zip(accs, states, fades, strict=True)]
+    return list(zip(tops, sums, accs, strict=True))
+
+
+def tiles(a):
+    return [a[:, i : i + 128] for i in range(0, a.shape[1], 128)]
 
 
 def mark_starts(lo, hi):
@@ -187,28 +198,38 @@
         copy.start()
     for copy in copies:
         copy.wait()
-    for h in range(4):
-        cols = slice(h * HD, (h + 1) * HD)
-        marks = landmarks(mark_v, cols) if mark else None
-        for j in range(2):
-            rows = slice(j * BLK, (j + 1) * BLK)
-            ks, vs = [], []
-            if own:
-                ks.append(own_ref[0:256, cols])
-                vs.append(own_ref[256:512, cols])
-            if mark:
-                ks.append(marks[0])
-                vs.append(marks[1])
-            for i, level in enumerate(levels):
-                at = pl.multiple_of((pattern[1 + level, place[2] + j] & 1) * BLK, BLK)
-                ks.append(far_v[i, pl.ds(at, BLK), cols])
-                vs.append(far_v[i, pl.ds(256 + at, BLK), cols])
-            state = None
-            if carry:
-                top, total, acc = state_refs
-                first = slice(h * HD, h * HD + 1)
-                state = (top[rows, first], total[rows, first], acc[rows, cols])
-            m, s, a = softmax_step(state, q[rows, cols], ks, vs)
+    streams = 4 if final else 2
+    for pair in range(0, 4, streams):
+        spots, states, qs, kss, vss = [], [], [], [], []
+        for h in range(pair, pair + streams):
+            cols = slice(h * HD, (h + 1) * HD)
+            marks = landmarks(mark_v, cols) if mark else None
+            for j in range(2):
+                rows = slice(j * BLK, (j + 1) * BLK)
+                ks, vs = [], []
+                if own:
+                    ks.append(own_ref[0:256, cols])
+                    vs.append(own_ref[256:512, cols])
+                if mark:
+                    ks.append(marks[0])
+                    vs.append(marks[1])
+                for i, level in enumerate(levels):
+                    at = pl.multiple_of((pattern[1 + level, place[2] + j] & 1) * BLK, BLK)
+                    ks.append(far_v[i, pl.ds(at, BLK), cols])
+                    vs.append(far_v[i, pl.ds(256 + at, BLK), cols])
+                state = None
+                if carry:
+                    top, total, acc = state_refs
+                    first = slice(h * HD, h * HD + 1)
+                    state = (top[rows, first], total[rows, first], acc[rows, cols])
+                spots.append((rows, cols))
+                states.append(state)
+                qs.append(q[rows, cols])
+                kss.append(ks)
+                vss.append(vs)
+        for (rows, cols), (m, s, a) in zip(
+            spots, softmax_steps(states, qs, kss, vss), strict=True
+        ):
             if final:
                 outs[0][rows, cols] = (a / s).astype(BF16)
             else:
@@ -401,17 +422,17 @@
     token = arrived(COST3, far[2])
     state = step((2,), far, state=state, mark=[(wl1, every), (wl3, every)], token=token, cost=COST)
     rest = [(wl2a, mark_starts(0, HALF)), (wl2b, mark_starts(HALF, 768))]
-    late, state = lax.optimization_barrier(((far[1], far[0]), state))
+    pieces = (wl, wl1, wl2a, wl2b, wl3)
+    pieces, state = lax.optimization_barrier((pieces, state))
+    w_mine = pack(place, pieces)
+    late, w_mine = lax.optimization_barrier(((far[1], far[0]), w_mine))
     far[1], far[0] = late
     token = arrived(COST1, *late)
-    pieces = (wl, wl1, wl2a, wl2b, wl3)
-    pieces, token, state = lax.optimization_barrier((pieces, token, state))
     mine = step((1, 0), far, state=state, mark=rest, final=True, token=token)
-    w_mine = pack(place, pieces)
     w_other = send(w_mine, lambda x, zl, y, zh, c: (x, zl, y, zh, 1 - c))
     part = project(place, mine, send(mine, to_first), send(mine, to_second), w_mine, w_other)
     total = 0.0
-    for d in range(4):
+    for d in (2, 1, 3, 0):
         total += send(
             part[d], lambda x, zl, y, zh, c: (x, c, y, (zh + d) % NZH, zl)
         ).astype(F32)

time: 154 us -> 148 us (0.961)
  Pallas kernels: 20.2 us -> 17 us
  waiting for transfers between devices: 48.1 us -> 45.5 us
    pallas_call x3, Pallas kernels: 15.2 us -> 11.9 us  [attend(): pl.pallas_call(functools.partial(attend_kernel, levels, own is not None,...]
    ppermute x21, waiting for transfers between devices: 48.1 us -> 45.5 us  [send(): return lax.ppermute(a, AXES, pairs)]
  transfers between devices with their start and end apart: 21 -> 21, of which waited for: 10 -> 11; matrix products, arithmetic and copies ran while one was open for 0% -> 0% of each run, Pallas kernels for 11% -> 9%
where the time goes in v5:
time: 148 us
  starting transfers between devices  81.4 us (55%)
  waiting for transfers between devices  45.5 us (31%)
  Pallas kernels  17 us (11%)
  local copies, waits for them, and re-layouts  2.47 us (2%)
    ppermute x21, starting transfers between devices, send(): return lax.ppermute(a, AXES, pairs)  81.4 us
    ppermute x21, waiting for transfers between devices, send(): return lax.ppermute(a, AXES, pairs)  45.5 us
    pallas_call x3, Pallas kernels, attend(): pl.pallas_call(functools.partial(attend_kernel, levels, own is not None,...  11.9 us
  transfers between devices with their start and end apart: 21, of which 11 were waited for; matrix products, arithmetic and copies ran while one was open for 0% of the time, Pallas kernels for 9%

profile of v5, /device:TPU:1, one launch (start us, length us, event | category | flops | bytes accessed | tf_op | source)
XLA Modules:
  0.0 147.7 jit_solution(174831736770361993)
XLA Ops:
  1.3 8.3 %collective-permute-start = (bf16[80,512]{1,0:T(8,128)(2,1)S(1)}, bf16[80,512]{1,0:T(8,128)(2,1)S(1)}, u32[]{:S(2)}, u32[]{:S(2)}) collective-permute-start(bf16[80,512]{1,0:T(8,128)(2,1)S(1)} %prepare.1.a), channel_id=1, source_target_pairs={{0,32},{1,33},{2,34},{3,35},{4,36},{5,37},{6,38},{7,39},{8,40},{9,... | collective-permute-start | bytes 245768 | tf_op jit(solution)/shard_map/ppermute | solution.py:47
  11.5 5.7 %collective-permute-start.1 = (bf16[160,512]{1,0:T(8,128)(2,1)S(1)}, bf16[160,512]{1,0:T(8,128)(2,1)S(1)}, u32[]{:S(2)}, u32[]{:S(2)}) collective-permute-start(bf16[160,512]{1,0:T(8,128)(2,1)S(1)} %join.4.a), channel_id=1, source_target_pairs={{0,16},{1,17},{2,18},{3,19},{4,20},{5,21},{6,22},{7,23},{8,24},{9,... | collective-permute-start | bytes 491528 | tf_op jit(solution)/shard_map/ppermute | solution.py:47
  17.2 5.7 %collective-permute-start.4 = (bf16[512,512]{1,0:T(8,128)(2,1)S(1)}, bf16[512,512]{1,0:T(8,128)(2,1)S(1)}, u32[]{:S(2)}, u32[]{:S(2)}) collective-permute-start(bf16[512,512]{1,0:T(8,128)(2,1)S(1)} %stack.21.refs_0_), channel_id=1, source_target_pairs={{0,256},{1,257},{2,258},{3,259},{4,260},{5,261},{6,262},{7,263},{8... | collective-permute-start | bytes 1572872 | tf_op jit(solution)/shard_map/ppermute | solution.py:47
  22.9 4.0 %collective-permute-start.3 = (bf16[512,512]{1,0:T(8,128)(2,1)S(1)}, bf16[512,512]{1,0:T(8,128)(2,1)S(1)}, u32[]{:S(2)}, u32[]{:S(2)}) collective-permute-start(bf16[512,512]{1,0:T(8,128)(2,1)S(1)} %stack.21.refs_0_), channel_id=1, source_target_pairs={{0,64},{1,65},{2,66},{3,67},{4,68},{5,69},{6,70},{7,71},{8,72},{9,... | collective-permute-start | bytes 1572872 | tf_op jit(solution)/shard_map/ppermute | solution.py:47
  31.1 7.5 %collective-permute-done.2.b = bf16[320,512]{1,0:T(8,128)(2,1)S(1)} collective-permute-done((bf16[320,512]{1,0:T(8,128)(2,1)S(1)}, bf16[320,512]{1,0:T(8,128)(2,1)S(1)}, u32[]{:S(2)}, u32[]{:S(2)}) %collective-permute-start.2) | collective-permute-done | bytes 327712 | tf_op jit(solution)/shard_map/ppermute | solution.py:47
  38.6 3.1 %collective-permute-start.6 = (bf16[128,512]{1,0:T(8,128)(2,1)S(1)}, bf16[128,512]{1,0:T(8,128)(2,1)S(1)}, u32[]{:S(2)}, u32[]{:S(2)}) collective-permute-start(bf16[128,512]{1,0:T(8,128)(2,1)S(1)} %pick.1), channel_id=1, source_target_pairs={{0,64},{1,65},{2,66},{3,67},{4,68},{5,69},{6,70},{7,71},{8,72},{9,... | collective-permute-start | bytes 393224 | tf_op jit(solution)/shard_map/ppermute | solution.py:47
  41.7 5.3 %collective-permute-start.11 = (bf16[512,512]{1,0:T(8,128)(2,1)S(1)}, bf16[512,512]{1,0:T(8,128)(2,1)S(1)}, u32[]{:S(2)}, u32[]{:S(2)}) collective-permute-start(bf16[512,512]{1,0:T(8,128)(2,1)S(1)} %stack.21.refs_0_), channel_id=1, source_target_pairs={{0,32},{1,33},{2,34},{3,35},{4,36},{5,37},{6,38},{7,39},{8,40},{9,... | collective-permute-start | bytes 1572872 | tf_op jit(solution)/shard_map/ppermute | solution.py:47
  47.2 3.9 %collective-permute-start.8 = (bf16[768,512]{1,0:T(8,128)(2,1)S(1)}, bf16[768,512]{1,0:T(8,128)(2,1)S(1)}, u32[]{:S(2)}, u32[]{:S(2)}) collective-permute-start(bf16[768,512]{1,0:T(8,128)(2,1)S(1)} %join.7.refs_1_.w0), channel_id=1, source_target_pairs={{0,384},{1,385},{2,386},{3,387},{4,388},{5,389},{6,390},{7,391},{8... | collective-permute-start | bytes 2359304 | tf_op jit(solution)/shard_map/ppermute | solution.py:47
  56.8 2.8 %collective-permute-start.12 = (bf16[512,512]{1,0:T(8,128)(2,1)S(1)}, bf16[512,512]{1,0:T(8,128)(2,1)S(1)}, u32[]{:S(2)}, u32[]{:S(2)}) collective-permute-start(bf16[512,512]{1,0:T(8,128)(2,1)S(1)} %stack.21.refs_0_), channel_id=1, source_target_pairs={{0,16},{1,17},{2,18},{3,19},{4,20},{5,21},{6,22},{7,23},{8,24},{9,... | collective-permute-start | bytes 1572872 | tf_op jit(solution)/shard_map/ppermute | solution.py:47
  59.7 3.9 %attend.3 = (f32[256,512]{1,0:T(8,128)S(1)}, f32[256,512]{1,0:T(8,128)S(1)}, f32[256,512]{1,0:T(8,128)S(1)}) custom-call(s32[4]{0:T(128)S(1)} %pad_add_fusion.place, s32[7,128]{1,0:T(8,128)S(1)} %bitcast.6, bf16[256,512]{1,0:T(8,128)(2,1)S(1)} %copy-done, bf16[512,512]{1,0:T(8,128)(2,1)S(1)} %stack.21.refs_0_, bf16[768,512]{1,0:T(8,128)(2,1)S(1)} %join.7.refs_1_.w0, ...), custom_call_target="tpu_custom_call" | custom-call | flops 402653184 | bytes 4194304 | tf_op jit(solution)/shard_map/attend/pallas_call | solution.py:261
  65.1 4.7 %collective-permute-done.7.refs_3_.w1 = bf16[768,512]{1,0:T(8,128)(2,1)S(1)} collective-permute-done((bf16[768,512]{1,0:T(8,128)(2,1)S(1)}, bf16[768,512]{1,0:T(8,128)(2,1)S(1)}, u32[]{:S(2)}, u32[]{:S(2)}) %collective-permute-start.7) | collective-permute-done | bytes 786464 | tf_op jit(solution)/shard_map/ppermute | solution.py:47
  71.8 4.6 %collective-permute-start.10 = (bf16[368,512]{1,0:T(8,128)(2,1)S(1)}, bf16[368,512]{1,0:T(8,128)(2,1)S(1)}, u32[]{:S(2)}, u32[]{:S(2)}) collective-permute-start(bf16[368,512]{1,0:T(8,128)(2,1)S(1)} %slice.7), channel_id=1, source_target_pairs={{0,384},{1,385},{2,386},{3,387},{4,388},{5,389},{6,390},{7,391},{8... | collective-permute-start | bytes 1130504 | tf_op jit(solution)/shard_map/ppermute | solution.py:47
  77.2 4.4 %attend.4 = (f32[256,512]{1,0:T(8,128)S(1)}, f32[256,512]{1,0:T(8,128)S(1)}, f32[256,512]{1,0:T(8,128)S(1)}) custom-call(s32[4]{0:T(128)S(1)} %pad_add_fusion.place, s32[7,128]{1,0:T(8,128)S(1)} %bitcast.7, bf16[256,512]{1,0:T(8,128)(2,1)S(1)} %copy-done, f32[256,512]{1,0:T(8,128)S(1)} %get-tuple-element.60.refs_0_, ...), custom_call_target="tpu_custom_call" | custom-call | flops 201326592 | bytes 4194304 | tf_op jit(solution)/shard_map/attend/pallas_call | solution.py:261
  82.4 9.7 %collective-permute-done.13.refs_1_.refs_6_ = bf16[512,512]{1,0:T(8,128)(2,1)S(1)} collective-permute-done((bf16[512,512]{1,0:T(8,128)(2,1)S(1)}, bf16[512,512]{1,0:T(8,128)(2,1)S(1)}, u32[]{:S(2)}, u32[]{:S(2)}) %collective-permute-start.13) | collective-permute-done | bytes 524320 | tf_op jit(solution)/shard_map/ppermute | solution.py:47
  94.3 2.9 %collective-permute-start.16 = (bf16[4,512,512]{2,1,0:T(8,128)(2,1)S(1)}, bf16[4,512,512]{2,1,0:T(8,128)(2,1)S(1)}, u32[]{:S(2)}, u32[]{:S(2)}) collective-permute-start(bf16[4,512,512]{2,1,0:T(8,128)(2,1)S(1)} %pack.1.w_mine), channel_id=1, source_target_pairs={{0,1},{1,0},{2,3},{3,2},{4,5},{5,4},{6,7},{7,6},{8,9},{9,8},{10,11... | collective-permute-start | bytes 6291464 | tf_op jit(solution)/shard_map/ppermute | solution.py:47
  97.3 3.6 %attend.5.mine = bf16[256,512]{1,0:T(8,128)(2,1)S(1)} custom-call(s32[4]{0:T(128)S(1)} %pad_add_fusion.place, s32[7,128]{1,0:T(8,128)S(1)} %bitcast.8, bf16[256,512]{1,0:T(8,128)(2,1)S(1)} %copy-done, f32[256,512]{1,0:T(8,128)S(1)} %get-tuple-element.66.refs_0_, f32[256,512]{1,0:T(8,128)S(1)} %get-tuple-element.67.refs_1_, ...), custom_call_target="tpu_custom_call" | custom-call | flops 201326592 | bytes 4194304 | tf_op jit(solution)/shard_map/attend/pallas_call | solution.py:261
  100.9 2.5 %collective-permute-start.15 = (bf16[256,512]{1,0:T(8,128)(2,1)S(1)}, bf16[256,512]{1,0:T(8,128)(2,1)S(1)}, u32[]{:S(2)}, u32[]{:S(2)}) collective-permute-start(bf16[256,512]{1,0:T(8,128)(2,1)S(1)} %attend.5.mine), channel_id=1, source_target_pairs={{0,0},{1,64},{2,2},{3,66},{4,4},{5,68},{6,6},{7,70},{8,8},{9,72},{... | collective-permute-start | bytes 786440 | tf_op jit(solution)/shard_map/ppermute | solution.py:47
  105.3 4.1 %collective-permute-done.15.got2 = bf16[256,512]{1,0:T(8,128)(2,1)S(1)} collective-permute-done((bf16[256,512]{1,0:T(8,128)(2,1)S(1)}, bf16[256,512]{1,0:T(8,128)(2,1)S(1)}, u32[]{:S(2)}, u32[]{:S(2)}) %collective-permute-start.15) | collective-permute-done | bytes 262176 | tf_op jit(solution)/shard_map/ppermute | solution.py:47
  113.3 9.8 %collective-permute-start.17 = (bf16[256,512]{1,0:T(8,128)(2,1)S(1)}, bf16[256,512]{1,0:T(8,128)(2,1)S(1)}, u32[]{:S(2)}, u32[]{:S(2)}) collective-permute-start(bf16[256,512]{1,0:T(8,128)(2,1)S(1)} %get-tuple-element.77), channel_id=1, source_target_pairs={{0,4},{1,68},{2,6},{3,70},{4,0},{5,64},{6,2},{7,66},{8,12},{9,76},... | collective-permute-start | bytes 786440 | tf_op jit(solution)/shard_map/ppermute | solution.py:47
  123.1 4.0 %collective-permute-start.18 = (bf16[256,512]{1,0:T(8,128)(2,1)S(1)}, bf16[256,512]{1,0:T(8,128)(2,1)S(1)}, u32[]{:S(2)}, u32[]{:S(2)}) collective-permute-start(bf16[256,512]{1,0:T(8,128)(2,1)S(1)} %get-tuple-element.78), channel_id=1, source_target_pairs={{0,2},{1,66},{2,4},{3,68},{4,6},{5,70},{6,0},{7,64},{8,10},{9,74},... | collective-permute-start | bytes 786440 | tf_op jit(solution)/shard_map/ppermute | solution.py:47
  127.2 2.7 %collective-permute-start.19 = (bf16[256,512]{1,0:T(8,128)(2,1)S(1)}, bf16[256,512]{1,0:T(8,128)(2,1)S(1)}, u32[]{:S(2)}, u32[]{:S(2)}) collective-permute-start(bf16[256,512]{1,0:T(8,128)(2,1)S(1)} %get-tuple-element.79), channel_id=1, source_target_pairs={{0,6},{1,70},{2,0},{3,64},{4,2},{5,66},{6,4},{7,68},{8,14},{9,78},... | collective-permute-start | bytes 786440 | tf_op jit(solution)/shard_map/ppermute | solution.py:47
  129.9 4.0 %collective-permute-start.20 = (bf16[256,512]{1,0:T(8,128)(2,1)S(1)}, bf16[256,512]{1,0:T(8,128)(2,1)S(1)}, u32[]{:S(2)}, u32[]{:S(2)}) collective-permute-start(bf16[256,512]{1,0:T(8,128)(2,1)S(1)} %get-tuple-element.80), channel_id=1, source_target_pairs={{0,0},{1,64},{2,2},{3,66},{4,4},{5,68},{6,6},{7,70},{8,8},{9,72},{... | collective-permute-start | bytes 786440 | tf_op jit(solution)/shard_map/ppermute | solution.py:47
  133.9 7.5 %collective-permute-done.17 = bf16[256,512]{1,0:T(8,128)(2,1)S(1)} collective-permute-done((bf16[256,512]{1,0:T(8,128)(2,1)S(1)}, bf16[256,512]{1,0:T(8,128)(2,1)S(1)}, u32[]{:S(2)}, u32[]{:S(2)}) %collective-permute-start.17) | collective-permute-done | bytes 262176 | tf_op jit(solution)/shard_map/ppermute | solution.py:47
  141.5 4.4 %collective-permute-done.18 = bf16[256,512]{1,0:T(8,128)(2,1)S(1)} collective-permute-done((bf16[256,512]{1,0:T(8,128)(2,1)S(1)}, bf16[256,512]{1,0:T(8,128)(2,1)S(1)}, u32[]{:S(2)}, u32[]{:S(2)}) %collective-permute-start.18) | collective-permute-done | bytes 262176 | tf_op jit(solution)/shard_map/ppermute | solution.py:47
  (53 shorter events, 28.2 us)
Async XLA Ops:
  1.3 10.2 %collective-permute-start = (bf16[80,512]{1,0:T(8,128)(2,1)S(1)}, bf16[80,512]{1,0:T(8,128)(2,1)S(1)}, u32[]{:S(2)}, u32[]{:S(2)}) collective-permute-start(bf16[80,512]{1,0:T(8,128)(2,1)S(1)} %prepare.1.a), channel_id=1, source_target_pairs={{0,32},{1,33},{2,34},{3,35},{4,36},{5,37},{6,38},{7,39},{8,40},{9,... | collective-permute-start | bytes 245768 | tf_op jit(solution)/shard_map/ppermute | solution.py:47
  11.5 15.4 %collective-permute-start.1 = (bf16[160,512]{1,0:T(8,128)(2,1)S(1)}, bf16[160,512]{1,0:T(8,128)(2,1)S(1)}, u32[]{:S(2)}, u32[]{:S(2)}) collective-permute-start(bf16[160,512]{1,0:T(8,128)(2,1)S(1)} %join.4.a), channel_id=1, source_target_pairs={{0,16},{1,17},{2,18},{3,19},{4,20},{5,21},{6,22},{7,23},{8,24},{9,... | collective-permute-start | bytes 491528 | tf_op jit(solution)/shard_map/ppermute | solution.py:47
  17.2 33.9 %collective-permute-start.4 = (bf16[512,512]{1,0:T(8,128)(2,1)S(1)}, bf16[512,512]{1,0:T(8,128)(2,1)S(1)}, u32[]{:S(2)}, u32[]{:S(2)}) collective-permute-start(bf16[512,512]{1,0:T(8,128)(2,1)S(1)} %stack.21.refs_0_), channel_id=1, source_target_pairs={{0,256},{1,257},{2,258},{3,259},{4,260},{5,261},{6,262},{7,263},{8... | collective-permute-start | bytes 1572872 | tf_op jit(solution)/shard_map/ppermute | solution.py:47
  22.9 30.1 %collective-permute-start.3 = (bf16[512,512]{1,0:T(8,128)(2,1)S(1)}, bf16[512,512]{1,0:T(8,128)(2,1)S(1)}, u32[]{:S(2)}, u32[]{:S(2)}) collective-permute-start(bf16[512,512]{1,0:T(8,128)(2,1)S(1)} %stack.21.refs_0_), channel_id=1, source_target_pairs={{0,64},{1,65},{2,66},{3,67},{4,68},{5,69},{6,70},{7,71},{8,72},{9,... | collective-permute-start | bytes 1572872 | tf_op jit(solution)/shard_map/ppermute | solution.py:47
  27.0 26.1 %collective-permute-start.5 = (bf16[512,512]{1,0:T(8,128)(2,1)S(1)}, bf16[512,512]{1,0:T(8,128)(2,1)S(1)}, u32[]{:S(2)}, u32[]{:S(2)}) collective-permute-start(bf16[512,512]{1,0:T(8,128)(2,1)S(1)} %stack.21.refs_0_), channel_id=1, source_target_pairs={{0,128},{1,129},{2,130},{3,131},{4,132},{5,133},{6,134},{7,135},{8... | collective-permute-start | bytes 1572872 | tf_op jit(solution)/shard_map/ppermute | solution.py:47
  29.2 9.4 %collective-permute-start.2 = (bf16[320,512]{1,0:T(8,128)(2,1)S(1)}, bf16[320,512]{1,0:T(8,128)(2,1)S(1)}, u32[]{:S(2)}, u32[]{:S(2)}) collective-permute-start(bf16[320,512]{1,0:T(8,128)(2,1)S(1)} %join.5.a), channel_id=1, source_target_pairs={{0,8},{1,9},{2,10},{3,11},{4,12},{5,13},{6,14},{7,15},{8,0},{9,1},... | collective-permute-start | bytes 983048 | tf_op jit(solution)/shard_map/ppermute | solution.py:47
  38.6 8.5 %collective-permute-start.6 = (bf16[128,512]{1,0:T(8,128)(2,1)S(1)}, bf16[128,512]{1,0:T(8,128)(2,1)S(1)}, u32[]{:S(2)}, u32[]{:S(2)}) collective-permute-start(bf16[128,512]{1,0:T(8,128)(2,1)S(1)} %pick.1), channel_id=1, source_target_pairs={{0,64},{1,65},{2,66},{3,67},{4,68},{5,69},{6,70},{7,71},{8,72},{9,... | collective-permute-start | bytes 393224 | tf_op jit(solution)/shard_map/ppermute | solution.py:47
  41.7 34.7 %collective-permute-start.11 = (bf16[512,512]{1,0:T(8,128)(2,1)S(1)}, bf16[512,512]{1,0:T(8,128)(2,1)S(1)}, u32[]{:S(2)}, u32[]{:S(2)}) collective-permute-start(bf16[512,512]{1,0:T(8,128)(2,1)S(1)} %stack.21.refs_0_), channel_id=1, source_target_pairs={{0,32},{1,33},{2,34},{3,35},{4,36},{5,37},{6,38},{7,39},{8,40},{9,... | collective-permute-start | bytes 1572872 | tf_op jit(solution)/shard_map/ppermute | solution.py:47
  47.2 12.5 %copy-start = (bf16[256,512]{1,0:T(8,128)(2,1)S(1)}, bf16[256,512]{1,0:T(8,128)(2,1)}, u32[]{:S(2)}) copy-start(bf16[256,512]{1,0:T(8,128)(2,1)} %q.5) | copy-start | bytes 786436
  47.2 12.5 %copy-start.1 = (s32[128,7]{0,1:T(8,128)S(1)}, s32[128,7]{0,1:T(8,128)}, u32[]{:S(2)}) copy-start(s32[128,7]{0,1:T(8,128)} %param.11) | copy-start | bytes 10756
  47.2 18.0 %collective-permute-start.8 = (bf16[768,512]{1,0:T(8,128)(2,1)S(1)}, bf16[768,512]{1,0:T(8,128)(2,1)S(1)}, u32[]{:S(2)}, u32[]{:S(2)}) collective-permute-start(bf16[768,512]{1,0:T(8,128)(2,1)S(1)} %join.7.refs_1_.w0), channel_id=1, source_target_pairs={{0,384},{1,385},{2,386},{3,387},{4,388},{5,389},{6,390},{7,391},{8... | collective-permute-start | bytes 2359304 | tf_op jit(solution)/shard_map/ppermute | solution.py:47
  51.1 18.8 %collective-permute-start.7 = (bf16[768,512]{1,0:T(8,128)(2,1)S(1)}, bf16[768,512]{1,0:T(8,128)(2,1)S(1)}, u32[]{:S(2)}, u32[]{:S(2)}) collective-permute-start(bf16[768,512]{1,0:T(8,128)(2,1)S(1)} %join.7.refs_1_.w0), channel_id=1, source_target_pairs={{0,128},{1,129},{2,130},{3,131},{4,132},{5,133},{6,134},{7,135},{8... | collective-permute-start | bytes 2359304 | tf_op jit(solution)/shard_map/ppermute | solution.py:47
  54.6 37.4 %collective-permute-start.13 = (bf16[512,512]{1,0:T(8,128)(2,1)S(1)}, bf16[512,512]{1,0:T(8,128)(2,1)S(1)}, u32[]{:S(2)}, u32[]{:S(2)}) collective-permute-start(bf16[512,512]{1,0:T(8,128)(2,1)S(1)} %stack.21.refs_0_), channel_id=1, source_target_pairs={{0,8},{1,9},{2,10},{3,11},{4,12},{5,13},{6,14},{7,15},{8,0},{9,1},... | collective-permute-start | bytes 1572872 | tf_op jit(solution)/shard_map/ppermute | solution.py:47
  56.8 37.5 %collective-permute-start.12 = (bf16[512,512]{1,0:T(8,128)(2,1)S(1)}, bf16[512,512]{1,0:T(8,128)(2,1)S(1)}, u32[]{:S(2)}, u32[]{:S(2)}) collective-permute-start(bf16[512,512]{1,0:T(8,128)(2,1)S(1)} %stack.21.refs_0_), channel_id=1, source_target_pairs={{0,16},{1,17},{2,18},{3,19},{4,20},{5,21},{6,22},{7,23},{8,24},{9,... | collective-permute-start | bytes 1572872 | tf_op jit(solution)/shard_map/ppermute | solution.py:47
  69.9 11.8 %collective-permute-start.9 = (bf16[400,512]{1,0:T(8,128)(2,1)S(1)}, bf16[400,512]{1,0:T(8,128)(2,1)S(1)}, u32[]{:S(2)}, u32[]{:S(2)}) collective-permute-start(bf16[400,512]{1,0:T(8,128)(2,1)S(1)} %slice.6), channel_id=1, source_target_pairs={{0,128},{1,129},{2,130},{3,131},{4,132},{5,133},{6,134},{7,135},{8... | collective-permute-start | bytes 1228808 | tf_op jit(solution)/shard_map/ppermute | solution.py:47
  71.8 9.8 %collective-permute-start.10 = (bf16[368,512]{1,0:T(8,128)(2,1)S(1)}, bf16[368,512]{1,0:T(8,128)(2,1)S(1)}, u32[]{:S(2)}, u32[]{:S(2)}) collective-permute-start(bf16[368,512]{1,0:T(8,128)(2,1)S(1)} %slice.7), channel_id=1, source_target_pairs={{0,384},{1,385},{2,386},{3,387},{4,388},{5,389},{6,390},{7,391},{8... | collective-permute-start | bytes 1130504 | tf_op jit(solution)/shard_map/ppermute | solution.py:47
  92.1 5.2 %copy-start.2 = (bf16[512,512]{1,0:T(8,128)(2,1)}, bf16[512,512]{1,0:T(8,128)(2,1)S(1)}, u32[]{:S(2)}) copy-start(bf16[512,512]{1,0:T(8,128)(2,1)S(1)} %collective-permute-done.13.refs_1_.refs_6_) | copy-start | bytes 1572868
  94.3 17.1 %collective-permute-start.16 = (bf16[4,512,512]{2,1,0:T(8,128)(2,1)S(1)}, bf16[4,512,512]{2,1,0:T(8,128)(2,1)S(1)}, u32[]{:S(2)}, u32[]{:S(2)}) collective-permute-start(bf16[4,512,512]{2,1,0:T(8,128)(2,1)S(1)} %pack.1.w_mine), channel_id=1, source_target_pairs={{0,1},{1,0},{2,3},{3,2},{4,5},{5,4},{6,7},{7,6},{8,9},{9,8},{10,11... | collective-permute-start | bytes 6291464 | tf_op jit(solution)/shard_map/ppermute | solution.py:47
  100.9 8.5 %collective-permute-start.15 = (bf16[256,512]{1,0:T(8,128)(2,1)S(1)}, bf16[256,512]{1,0:T(8,128)(2,1)S(1)}, u32[]{:S(2)}, u32[]{:S(2)}) collective-permute-start(bf16[256,512]{1,0:T(8,128)(2,1)S(1)} %attend.5.mine), channel_id=1, source_target_pairs={{0,0},{1,64},{2,2},{3,66},{4,4},{5,68},{6,6},{7,70},{8,8},{9,72},{... | collective-permute-start | bytes 786440 | tf_op jit(solution)/shard_map/ppermute | solution.py:47
  103.4 8.0 %collective-permute-start.14 = (bf16[256,512]{1,0:T(8,128)(2,1)S(1)}, bf16[256,512]{1,0:T(8,128)(2,1)S(1)}, u32[]{:S(2)}, u32[]{:S(2)}) collective-permute-start(bf16[256,512]{1,0:T(8,128)(2,1)S(1)} %attend.5.mine), channel_id=1, source_target_pairs={{0,64},{1,0},{2,66},{3,2},{4,68},{5,4},{6,70},{7,6},{8,72},{9,8},{... | collective-permute-start | bytes 786440 | tf_op jit(solution)/shard_map/ppermute | solution.py:47
  113.3 28.2 %collective-permute-start.17 = (bf16[256,512]{1,0:T(8,128)(2,1)S(1)}, bf16[256,512]{1,0:T(8,128)(2,1)S(1)}, u32[]{:S(2)}, u32[]{:S(2)}) collective-permute-start(bf16[256,512]{1,0:T(8,128)(2,1)S(1)} %get-tuple-element.77), channel_id=1, source_target_pairs={{0,4},{1,68},{2,6},{3,70},{4,0},{5,64},{6,2},{7,66},{8,12},{9,76},... | collective-permute-start | bytes 786440 | tf_op jit(solution)/shard_map/ppermute | solution.py:47
  123.1 22.7 %collective-permute-start.18 = (bf16[256,512]{1,0:T(8,128)(2,1)S(1)}, bf16[256,512]{1,0:T(8,128)(2,1)S(1)}, u32[]{:S(2)}, u32[]{:S(2)}) collective-permute-start(bf16[256,512]{1,0:T(8,128)(2,1)S(1)} %get-tuple-element.78), channel_id=1, source_target_pairs={{0,2},{1,66},{2,4},{3,68},{4,6},{5,70},{6,0},{7,64},{8,10},{9,74},... | collective-permute-start | bytes 786440 | tf_op jit(solution)/shard_map/ppermute | solution.py:47
  127.2 18.7 %collective-permute-start.19 = (bf16[256,512]{1,0:T(8,128)(2,1)S(1)}, bf16[256,512]{1,0:T(8,128)(2,1)S(1)}, u32[]{:S(2)}, u32[]{:S(2)}) collective-permute-start(bf16[256,512]{1,0:T(8,128)(2,1)S(1)} %get-tuple-element.79), channel_id=1, source_target_pairs={{0,6},{1,70},{2,0},{3,64},{4,2},{5,66},{6,4},{7,68},{8,14},{9,78},... | collective-permute-start | bytes 786440 | tf_op jit(solution)/shard_map/ppermute | solution.py:47
  129.9 16.9 %collective-permute-start.20 = (bf16[256,512]{1,0:T(8,128)(2,1)S(1)}, bf16[256,512]{1,0:T(8,128)(2,1)S(1)}, u32[]{:S(2)}, u32[]{:S(2)}) collective-permute-start(bf16[256,512]{1,0:T(8,128)(2,1)S(1)} %get-tuple-element.80), channel_id=1, source_target_pairs={{0,0},{1,64},{2,2},{3,66},{4,4},{5,68},{6,6},{7,70},{8,8},{9,72},{... | collective-permute-start | bytes 786440 | tf_op jit(solution)/shard_map/ppermute | solution.py:47
  (5 other events, 7.3 us)

commit v6 on v5

--- a/solution.py
+++ b/solution.py
@@ -246,8 +246,8 @@
         args, specs = [*args, *state], specs + [VMEM] * 3
     args += [a for a, _ in mark]
     specs += [ANY] * len(mark)
-    args += [in_hbm(far[l]) for l in levels]
-    specs += [HBM] * len(levels)
+    args += [far[l] if final else in_hbm(far[l]) for l in levels]
+    specs += [ANY if final else HBM] * len(levels)
     if token is not None:
         args, specs = [*args, token], [*specs, ANY]
     scratch = [pltpu.VMEM((len(levels), 512, 512), BF16)] if levels else []
@@ -355,12 +355,12 @@
     return pl.pallas_call(
         arrived_kernel,
         out_shape=jax.ShapeDtypeStruct((8, 128), F32),
-        in_specs=[HBM] * len(arrays),
+        in_specs=[ANY] * len(arrays),
         out_specs=VMEM,
         compiler_params=params(),
         name="arrived",
         cost_estimate=pl.CostEstimate(flops=cost << 27, bytes_accessed=4 << 20, transcendentals=0),
-    )(*[in_hbm(a) for a in arrays])
+    )(*arrays)
 
 
 def pick_kernel(a, out):

time: 148 us -> 148 us (level)
  starting transfers between devices: 81.4 us -> 83.5 us
    ppermute x21, starting transfers between devices: 81.4 us -> 83.5 us  [send(): return lax.ppermute(a, AXES, pairs)]
  transfers between devices with their start and end apart: 21 -> 21, of which waited for: 11 -> 10; matrix products, arithmetic and copies ran while one was open for 0% -> 0% of each run, Pallas kernels for 9% -> 9%
where the time goes in v6:
time: 148 us; the launch traced here: 147 us
  starting transfers between devices  83.5 us (56%)
  waiting for transfers between devices  44.1 us (30%)
  Pallas kernels  16.2 us (11%)
  local copies, waits for them, and re-layouts  1.79 us (1%)
    ppermute x21, starting transfers between devices, send(): return lax.ppermute(a, AXES, pairs)  83.5 us
    ppermute x21, waiting for transfers between devices, send(): return lax.ppermute(a, AXES, pairs)  44.1 us
    pallas_call x3, Pallas kernels, attend(): pl.pallas_call(functools.partial(attend_kernel, levels, own is not None,...  11.1 us
  transfers between devices with their start and end apart: 21, of which 10 were waited for; matrix products, arithmetic and copies ran while one was open for 0% of the time, Pallas kernels for 9%

profile of v6, /device:TPU:1, one launch (start us, length us, event | category | flops | bytes accessed | tf_op | source)
XLA Modules:
  0.0 146.9 jit_solution(909752716878704889)
XLA Ops:
  1.3 8.3 %collective-permute-start = (bf16[80,512]{1,0:T(8,128)(2,1)S(1)}, bf16[80,512]{1,0:T(8,128)(2,1)S(1)}, u32[]{:S(2)}, u32[]{:S(2)}) collective-permute-start(bf16[80,512]{1,0:T(8,128)(2,1)S(1)} %prepare.1.a), channel_id=1, source_target_pairs={{0,32},{1,33},{2,34},{3,35},{4,36},{5,37},{6,38},{7,39},{8,40},{9,... | collective-permute-start | bytes 245768 | tf_op jit(solution)/shard_map/ppermute | solution.py:47
  11.5 5.7 %collective-permute-start.1 = (bf16[160,512]{1,0:T(8,128)(2,1)S(1)}, bf16[160,512]{1,0:T(8,128)(2,1)S(1)}, u32[]{:S(2)}, u32[]{:S(2)}) collective-permute-start(bf16[160,512]{1,0:T(8,128)(2,1)S(1)} %join.4.a), channel_id=1, source_target_pairs={{0,16},{1,17},{2,18},{3,19},{4,20},{5,21},{6,22},{7,23},{8,24},{9,... | collective-permute-start | bytes 491528 | tf_op jit(solution)/shard_map/ppermute | solution.py:47
  17.2 5.7 %collective-permute-start.4 = (bf16[512,512]{1,0:T(8,128)(2,1)S(1)}, bf16[512,512]{1,0:T(8,128)(2,1)S(1)}, u32[]{:S(2)}, u32[]{:S(2)}) collective-permute-start(bf16[512,512]{1,0:T(8,128)(2,1)S(1)} %stack.21.refs_0_), channel_id=1, source_target_pairs={{0,256},{1,257},{2,258},{3,259},{4,260},{5,261},{6,262},{7,263},{8... | collective-permute-start | bytes 1572872 | tf_op jit(solution)/shard_map/ppermute | solution.py:47
  22.9 4.0 %collective-permute-start.3 = (bf16[512,512]{1,0:T(8,128)(2,1)S(1)}, bf16[512,512]{1,0:T(8,128)(2,1)S(1)}, u32[]{:S(2)}, u32[]{:S(2)}) collective-permute-start(bf16[512,512]{1,0:T(8,128)(2,1)S(1)} %stack.21.refs_0_), channel_id=1, source_target_pairs={{0,64},{1,65},{2,66},{3,67},{4,68},{5,69},{6,70},{7,71},{8,72},{9,... | collective-permute-start | bytes 1572872 | tf_op jit(solution)/shard_map/ppermute | solution.py:47
  31.1 7.5 %collective-permute-done.2.b = bf16[320,512]{1,0:T(8,128)(2,1)S(1)} collective-permute-done((bf16[320,512]{1,0:T(8,128)(2,1)S(1)}, bf16[320,512]{1,0:T(8,128)(2,1)S(1)}, u32[]{:S(2)}, u32[]{:S(2)}) %collective-permute-start.2) | collective-permute-done | bytes 327712 | tf_op jit(solution)/shard_map/ppermute | solution.py:47
  38.6 3.1 %collective-permute-start.6 = (bf16[128,512]{1,0:T(8,128)(2,1)S(1)}, bf16[128,512]{1,0:T(8,128)(2,1)S(1)}, u32[]{:S(2)}, u32[]{:S(2)}) collective-permute-start(bf16[128,512]{1,0:T(8,128)(2,1)S(1)} %pick.1), channel_id=1, source_target_pairs={{0,64},{1,65},{2,66},{3,67},{4,68},{5,69},{6,70},{7,71},{8,72},{9,... | collective-permute-start | bytes 393224 | tf_op jit(solution)/shard_map/ppermute | solution.py:47
  41.7 5.3 %collective-permute-start.11 = (bf16[512,512]{1,0:T(8,128)(2,1)S(1)}, bf16[512,512]{1,0:T(8,128)(2,1)S(1)}, u32[]{:S(2)}, u32[]{:S(2)}) collective-permute-start(bf16[512,512]{1,0:T(8,128)(2,1)S(1)} %stack.21.refs_0_), channel_id=1, source_target_pairs={{0,32},{1,33},{2,34},{3,35},{4,36},{5,37},{6,38},{7,39},{8,40},{9,... | collective-permute-start | bytes 1572872 | tf_op jit(solution)/shard_map/ppermute | solution.py:47
  47.2 3.9 %collective-permute-start.8 = (bf16[768,512]{1,0:T(8,128)(2,1)S(1)}, bf16[768,512]{1,0:T(8,128)(2,1)S(1)}, u32[]{:S(2)}, u32[]{:S(2)}) collective-permute-start(bf16[768,512]{1,0:T(8,128)(2,1)S(1)} %join.7.refs_1_.w0), channel_id=1, source_target_pairs={{0,384},{1,385},{2,386},{3,387},{4,388},{5,389},{6,390},{7,391},{8... | collective-permute-start | bytes 2359304 | tf_op jit(solution)/shard_map/ppermute | solution.py:47
  56.2 2.8 %collective-permute-start.12 = (bf16[512,512]{1,0:T(8,128)(2,1)S(1)}, bf16[512,512]{1,0:T(8,128)(2,1)S(1)}, u32[]{:S(2)}, u32[]{:S(2)}) collective-permute-start(bf16[512,512]{1,0:T(8,128)(2,1)S(1)} %stack.21.refs_0_), channel_id=1, source_target_pairs={{0,16},{1,17},{2,18},{3,19},{4,20},{5,21},{6,22},{7,23},{8,24},{9,... | collective-permute-start | bytes 1572872 | tf_op jit(solution)/shard_map/ppermute | solution.py:47
  59.1 3.9 %attend.3 = (f32[256,512]{1,0:T(8,128)S(1)}, f32[256,512]{1,0:T(8,128)S(1)}, f32[256,512]{1,0:T(8,128)S(1)}) custom-call(s32[4]{0:T(128)S(1)} %pad_add_fusion.place, s32[7,128]{1,0:T(8,128)S(1)} %bitcast.6, bf16[256,512]{1,0:T(8,128)(2,1)S(1)} %copy-done, bf16[512,512]{1,0:T(8,128)(2,1)S(1)} %stack.21.refs_0_, bf16[768,512]{1,0:T(8,128)(2,1)S(1)} %join.7.refs_1_.w0, ...), custom_call_target="tpu_custom_call" | custom-call | flops 402653184 | bytes 4194304 | tf_op jit(solution)/shard_map/attend/pallas_call | solution.py:261
  65.1 4.7 %collective-permute-done.7.refs_3_.w1 = bf16[768,512]{1,0:T(8,128)(2,1)S(1)} collective-permute-done((bf16[768,512]{1,0:T(8,128)(2,1)S(1)}, bf16[768,512]{1,0:T(8,128)(2,1)S(1)}, u32[]{:S(2)}, u32[]{:S(2)}) %collective-permute-start.7) | collective-permute-done | bytes 786464 | tf_op jit(solution)/shard_map/ppermute | solution.py:47
  71.8 4.6 %collective-permute-start.10 = (bf16[368,512]{1,0:T(8,128)(2,1)S(1)}, bf16[368,512]{1,0:T(8,128)(2,1)S(1)}, u32[]{:S(2)}, u32[]{:S(2)}) collective-permute-start(bf16[368,512]{1,0:T(8,128)(2,1)S(1)} %slice.7), channel_id=1, source_target_pairs={{0,384},{1,385},{2,386},{3,387},{4,388},{5,389},{6,390},{7,391},{8... | collective-permute-start | bytes 1130504 | tf_op jit(solution)/shard_map/ppermute | solution.py:47
  77.2 4.4 %attend.4 = (f32[256,512]{1,0:T(8,128)S(1)}, f32[256,512]{1,0:T(8,128)S(1)}, f32[256,512]{1,0:T(8,128)S(1)}) custom-call(s32[4]{0:T(128)S(1)} %pad_add_fusion.place, s32[7,128]{1,0:T(8,128)S(1)} %bitcast.7, bf16[256,512]{1,0:T(8,128)(2,1)S(1)} %copy-done, f32[256,512]{1,0:T(8,128)S(1)} %get-tuple-element.60.refs_0_, ...), custom_call_target="tpu_custom_call" | custom-call | flops 201326592 | bytes 4194304 | tf_op jit(solution)/shard_map/attend/pallas_call | solution.py:261
  82.4 9.8 %collective-permute-done.13.refs_1_.refs_6_ = bf16[512,512]{1,0:T(8,128)(2,1)S(1)} collective-permute-done((bf16[512,512]{1,0:T(8,128)(2,1)S(1)}, bf16[512,512]{1,0:T(8,128)(2,1)S(1)}, u32[]{:S(2)}, u32[]{:S(2)}) %collective-permute-start.13) | collective-permute-done | bytes 524320 | tf_op jit(solution)/shard_map/ppermute | solution.py:47
  92.1 5.1 %collective-permute-start.16 = (bf16[4,512,512]{2,1,0:T(8,128)(2,1)S(1)}, bf16[4,512,512]{2,1,0:T(8,128)(2,1)S(1)}, u32[]{:S(2)}, u32[]{:S(2)}) collective-permute-start(bf16[4,512,512]{2,1,0:T(8,128)(2,1)S(1)} %pack.1.w_mine), channel_id=1, source_target_pairs={{0,1},{1,0},{2,3},{3,2},{4,5},{5,4},{6,7},{7,6},{8,9},{9,8},{10,11... | collective-permute-start | bytes 6291464 | tf_op jit(solution)/shard_map/ppermute | solution.py:47
  97.2 2.8 %attend.5.mine = bf16[256,512]{1,0:T(8,128)(2,1)S(1)} custom-call(s32[4]{0:T(128)S(1)} %pad_add_fusion.place, s32[7,128]{1,0:T(8,128)S(1)} %bitcast.8, bf16[256,512]{1,0:T(8,128)(2,1)S(1)} %copy-done, f32[256,512]{1,0:T(8,128)S(1)} %get-tuple-element.66.refs_0_, f32[256,512]{1,0:T(8,128)S(1)} %get-tuple-element.67.refs_1_, ...), custom_call_target="tpu_custom_call" | custom-call | flops 201326592 | bytes 4194304 | tf_op jit(solution)/shard_map/attend/pallas_call | solution.py:261
  100.0 2.3 %collective-permute-start.15 = (bf16[256,512]{1,0:T(8,128)(2,1)S(1)}, bf16[256,512]{1,0:T(8,128)(2,1)S(1)}, u32[]{:S(2)}, u32[]{:S(2)}) collective-permute-start(bf16[256,512]{1,0:T(8,128)(2,1)S(1)} %attend.5.mine), channel_id=1, source_target_pairs={{0,0},{1,64},{2,2},{3,66},{4,4},{5,68},{6,6},{7,70},{8,8},{9,72},{... | collective-permute-start | bytes 786440 | tf_op jit(solution)/shard_map/ppermute | solution.py:47
  104.3 4.5 %collective-permute-done.15.got2 = bf16[256,512]{1,0:T(8,128)(2,1)S(1)} collective-permute-done((bf16[256,512]{1,0:T(8,128)(2,1)S(1)}, bf16[256,512]{1,0:T(8,128)(2,1)S(1)}, u32[]{:S(2)}, u32[]{:S(2)}) %collective-permute-start.15) | collective-permute-done | bytes 262176 | tf_op jit(solution)/shard_map/ppermute | solution.py:47
  112.4 9.9 %collective-permute-start.17 = (bf16[256,512]{1,0:T(8,128)(2,1)S(1)}, bf16[256,512]{1,0:T(8,128)(2,1)S(1)}, u32[]{:S(2)}, u32[]{:S(2)}) collective-permute-start(bf16[256,512]{1,0:T(8,128)(2,1)S(1)} %get-tuple-element.77), channel_id=1, source_target_pairs={{0,4},{1,68},{2,6},{3,70},{4,0},{5,64},{6,2},{7,66},{8,12},{9,76},... | collective-permute-start | bytes 786440 | tf_op jit(solution)/shard_map/ppermute | solution.py:47
  122.3 4.0 %collective-permute-start.18 = (bf16[256,512]{1,0:T(8,128)(2,1)S(1)}, bf16[256,512]{1,0:T(8,128)(2,1)S(1)}, u32[]{:S(2)}, u32[]{:S(2)}) collective-permute-start(bf16[256,512]{1,0:T(8,128)(2,1)S(1)} %get-tuple-element.78), channel_id=1, source_target_pairs={{0,2},{1,66},{2,4},{3,68},{4,6},{5,70},{6,0},{7,64},{8,10},{9,74},... | collective-permute-start | bytes 786440 | tf_op jit(solution)/shard_map/ppermute | solution.py:47
  126.4 2.7 %collective-permute-start.19 = (bf16[256,512]{1,0:T(8,128)(2,1)S(1)}, bf16[256,512]{1,0:T(8,128)(2,1)S(1)}, u32[]{:S(2)}, u32[]{:S(2)}) collective-permute-start(bf16[256,512]{1,0:T(8,128)(2,1)S(1)} %get-tuple-element.79), channel_id=1, source_target_pairs={{0,6},{1,70},{2,0},{3,64},{4,2},{5,66},{6,4},{7,68},{8,14},{9,78},... | collective-permute-start | bytes 786440 | tf_op jit(solution)/shard_map/ppermute | solution.py:47
  129.1 4.0 %collective-permute-start.20 = (bf16[256,512]{1,0:T(8,128)(2,1)S(1)}, bf16[256,512]{1,0:T(8,128)(2,1)S(1)}, u32[]{:S(2)}, u32[]{:S(2)}) collective-permute-start(bf16[256,512]{1,0:T(8,128)(2,1)S(1)} %get-tuple-element.80), channel_id=1, source_target_pairs={{0,0},{1,64},{2,2},{3,66},{4,4},{5,68},{6,6},{7,70},{8,8},{9,72},{... | collective-permute-start | bytes 786440 | tf_op jit(solution)/shard_map/ppermute | solution.py:47
  133.1 7.5 %collective-permute-done.17 = bf16[256,512]{1,0:T(8,128)(2,1)S(1)} collective-permute-done((bf16[256,512]{1,0:T(8,128)(2,1)S(1)}, bf16[256,512]{1,0:T(8,128)(2,1)S(1)}, u32[]{:S(2)}, u32[]{:S(2)}) %collective-permute-start.17) | collective-permute-done | bytes 262176 | tf_op jit(solution)/shard_map/ppermute | solution.py:47
  140.7 4.4 %collective-permute-done.18 = bf16[256,512]{1,0:T(8,128)(2,1)S(1)} collective-permute-done((bf16[256,512]{1,0:T(8,128)(2,1)S(1)}, bf16[256,512]{1,0:T(8,128)(2,1)S(1)}, u32[]{:S(2)}, u32[]{:S(2)}) %collective-permute-start.18) | collective-permute-done | bytes 262176 | tf_op jit(solution)/shard_map/ppermute | solution.py:47
  (49 shorter events, 25.7 us)
Async XLA Ops:
  1.3 10.2 %collective-permute-start = (bf16[80,512]{1,0:T(8,128)(2,1)S(1)}, bf16[80,512]{1,0:T(8,128)(2,1)S(1)}, u32[]{:S(2)}, u32[]{:S(2)}) collective-permute-start(bf16[80,512]{1,0:T(8,128)(2,1)S(1)} %prepare.1.a), channel_id=1, source_target_pairs={{0,32},{1,33},{2,34},{3,35},{4,36},{5,37},{6,38},{7,39},{8,40},{9,... | collective-permute-start | bytes 245768 | tf_op jit(solution)/shard_map/ppermute | solution.py:47
  11.5 15.4 %collective-permute-start.1 = (bf16[160,512]{1,0:T(8,128)(2,1)S(1)}, bf16[160,512]{1,0:T(8,128)(2,1)S(1)}, u32[]{:S(2)}, u32[]{:S(2)}) collective-permute-start(bf16[160,512]{1,0:T(8,128)(2,1)S(1)} %join.4.a), channel_id=1, source_target_pairs={{0,16},{1,17},{2,18},{3,19},{4,20},{5,21},{6,22},{7,23},{8,24},{9,... | collective-permute-start | bytes 491528 | tf_op jit(solution)/shard_map/ppermute | solution.py:47
  17.2 33.9 %collective-permute-start.4 = (bf16[512,512]{1,0:T(8,128)(2,1)S(1)}, bf16[512,512]{1,0:T(8,128)(2,1)S(1)}, u32[]{:S(2)}, u32[]{:S(2)}) collective-permute-start(bf16[512,512]{1,0:T(8,128)(2,1)S(1)} %stack.21.refs_0_), channel_id=1, source_target_pairs={{0,256},{1,257},{2,258},{3,259},{4,260},{5,261},{6,262},{7,263},{8... | collective-permute-start | bytes 1572872 | tf_op jit(solution)/shard_map/ppermute | solution.py:47
  22.9 30.1 %collective-permute-start.3 = (bf16[512,512]{1,0:T(8,128)(2,1)S(1)}, bf16[512,512]{1,0:T(8,128)(2,1)S(1)}, u32[]{:S(2)}, u32[]{:S(2)}) collective-permute-start(bf16[512,512]{1,0:T(8,128)(2,1)S(1)} %stack.21.refs_0_), channel_id=1, source_target_pairs={{0,64},{1,65},{2,66},{3,67},{4,68},{5,69},{6,70},{7,71},{8,72},{9,... | collective-permute-start | bytes 1572872 | tf_op jit(solution)/shard_map/ppermute | solution.py:47
  27.0 26.1 %collective-permute-start.5 = (bf16[512,512]{1,0:T(8,128)(2,1)S(1)}, bf16[512,512]{1,0:T(8,128)(2,1)S(1)}, u32[]{:S(2)}, u32[]{:S(2)}) collective-permute-start(bf16[512,512]{1,0:T(8,128)(2,1)S(1)} %stack.21.refs_0_), channel_id=1, source_target_pairs={{0,128},{1,129},{2,130},{3,131},{4,132},{5,133},{6,134},{7,135},{8... | collective-permute-start | bytes 1572872 | tf_op jit(solution)/shard_map/ppermute | solution.py:47
  29.2 9.4 %collective-permute-start.2 = (bf16[320,512]{1,0:T(8,128)(2,1)S(1)}, bf16[320,512]{1,0:T(8,128)(2,1)S(1)}, u32[]{:S(2)}, u32[]{:S(2)}) collective-permute-start(bf16[320,512]{1,0:T(8,128)(2,1)S(1)} %join.5.a), channel_id=1, source_target_pairs={{0,8},{1,9},{2,10},{3,11},{4,12},{5,13},{6,14},{7,15},{8,0},{9,1},... | collective-permute-start | bytes 983048 | tf_op jit(solution)/shard_map/ppermute | solution.py:47
  38.6 8.5 %collective-permute-start.6 = (bf16[128,512]{1,0:T(8,128)(2,1)S(1)}, bf16[128,512]{1,0:T(8,128)(2,1)S(1)}, u32[]{:S(2)}, u32[]{:S(2)}) collective-permute-start(bf16[128,512]{1,0:T(8,128)(2,1)S(1)} %pick.1), channel_id=1, source_target_pairs={{0,64},{1,65},{2,66},{3,67},{4,68},{5,69},{6,70},{7,71},{8,72},{9,... | collective-permute-start | bytes 393224 | tf_op jit(solution)/shard_map/ppermute | solution.py:47
  41.7 34.7 %collective-permute-start.11 = (bf16[512,512]{1,0:T(8,128)(2,1)S(1)}, bf16[512,512]{1,0:T(8,128)(2,1)S(1)}, u32[]{:S(2)}, u32[]{:S(2)}) collective-permute-start(bf16[512,512]{1,0:T(8,128)(2,1)S(1)} %stack.21.refs_0_), channel_id=1, source_target_pairs={{0,32},{1,33},{2,34},{3,35},{4,36},{5,37},{6,38},{7,39},{8,40},{9,... | collective-permute-start | bytes 1572872 | tf_op jit(solution)/shard_map/ppermute | solution.py:47
  47.2 11.9 %copy-start = (bf16[256,512]{1,0:T(8,128)(2,1)S(1)}, bf16[256,512]{1,0:T(8,128)(2,1)}, u32[]{:S(2)}) copy-start(bf16[256,512]{1,0:T(8,128)(2,1)} %q.5) | copy-start | bytes 786436
  47.2 11.9 %copy-start.5 = (s32[128,7]{0,1:T(8,128)S(1)}, s32[128,7]{0,1:T(8,128)}, u32[]{:S(2)}) copy-start(s32[128,7]{0,1:T(8,128)} %param.11) | copy-start | bytes 10756
  47.2 18.0 %collective-permute-start.8 = (bf16[768,512]{1,0:T(8,128)(2,1)S(1)}, bf16[768,512]{1,0:T(8,128)(2,1)S(1)}, u32[]{:S(2)}, u32[]{:S(2)}) collective-permute-start(bf16[768,512]{1,0:T(8,128)(2,1)S(1)} %join.7.refs_1_.w0), channel_id=1, source_target_pairs={{0,384},{1,385},{2,386},{3,387},{4,388},{5,389},{6,390},{7,391},{8... | collective-permute-start | bytes 2359304 | tf_op jit(solution)/shard_map/ppermute | solution.py:47
  51.1 2.0 %copy-start.2 = (bf16[512,512]{1,0:T(8,128)(2,1)}, bf16[512,512]{1,0:T(8,128)(2,1)S(1)}, u32[]{:S(2)}) copy-start(bf16[512,512]{1,0:T(8,128)(2,1)S(1)} %collective-permute-done.4.refs_1_.refs_3_) | copy-start | bytes 1572868
  51.1 18.8 %collective-permute-start.7 = (bf16[768,512]{1,0:T(8,128)(2,1)S(1)}, bf16[768,512]{1,0:T(8,128)(2,1)S(1)}, u32[]{:S(2)}, u32[]{:S(2)}) collective-permute-start(bf16[768,512]{1,0:T(8,128)(2,1)S(1)} %join.7.refs_1_.w0), channel_id=1, source_target_pairs={{0,128},{1,129},{2,130},{3,131},{4,132},{5,133},{6,134},{7,135},{8... | collective-permute-start | bytes 2359304 | tf_op jit(solution)/shard_map/ppermute | solution.py:47
  54.0 38.1 %collective-permute-start.13 = (bf16[512,512]{1,0:T(8,128)(2,1)S(1)}, bf16[512,512]{1,0:T(8,128)(2,1)S(1)}, u32[]{:S(2)}, u32[]{:S(2)}) collective-permute-start(bf16[512,512]{1,0:T(8,128)(2,1)S(1)} %stack.21.refs_0_), channel_id=1, source_target_pairs={{0,8},{1,9},{2,10},{3,11},{4,12},{5,13},{6,14},{7,15},{8,0},{9,1},... | collective-permute-start | bytes 1572872 | tf_op jit(solution)/shard_map/ppermute | solution.py:47
  56.2 35.9 %collective-permute-start.12 = (bf16[512,512]{1,0:T(8,128)(2,1)S(1)}, bf16[512,512]{1,0:T(8,128)(2,1)S(1)}, u32[]{:S(2)}, u32[]{:S(2)}) collective-permute-start(bf16[512,512]{1,0:T(8,128)(2,1)S(1)} %stack.21.refs_0_), channel_id=1, source_target_pairs={{0,16},{1,17},{2,18},{3,19},{4,20},{5,21},{6,22},{7,23},{8,24},{9,... | collective-permute-start | bytes 1572872 | tf_op jit(solution)/shard_map/ppermute | solution.py:47
  69.9 11.8 %collective-permute-start.9 = (bf16[400,512]{1,0:T(8,128)(2,1)S(1)}, bf16[400,512]{1,0:T(8,128)(2,1)S(1)}, u32[]{:S(2)}, u32[]{:S(2)}) collective-permute-start(bf16[400,512]{1,0:T(8,128)(2,1)S(1)} %slice.6), channel_id=1, source_target_pairs={{0,128},{1,129},{2,130},{3,131},{4,132},{5,133},{6,134},{7,135},{8... | collective-permute-start | bytes 1228808 | tf_op jit(solution)/shard_map/ppermute | solution.py:47
  71.8 9.8 %collective-permute-start.10 = (bf16[368,512]{1,0:T(8,128)(2,1)S(1)}, bf16[368,512]{1,0:T(8,128)(2,1)S(1)}, u32[]{:S(2)}, u32[]{:S(2)}) collective-permute-start(bf16[368,512]{1,0:T(8,128)(2,1)S(1)} %slice.7), channel_id=1, source_target_pairs={{0,384},{1,385},{2,386},{3,387},{4,388},{5,389},{6,390},{7,391},{8... | collective-permute-start | bytes 1130504 | tf_op jit(solution)/shard_map/ppermute | solution.py:47
  92.1 18.4 %collective-permute-start.16 = (bf16[4,512,512]{2,1,0:T(8,128)(2,1)S(1)}, bf16[4,512,512]{2,1,0:T(8,128)(2,1)S(1)}, u32[]{:S(2)}, u32[]{:S(2)}) collective-permute-start(bf16[4,512,512]{2,1,0:T(8,128)(2,1)S(1)} %pack.1.w_mine), channel_id=1, source_target_pairs={{0,1},{1,0},{2,3},{3,2},{4,5},{5,4},{6,7},{7,6},{8,9},{9,8},{10,11... | collective-permute-start | bytes 6291464 | tf_op jit(solution)/shard_map/ppermute | solution.py:47
  100.0 8.7 %collective-permute-start.15 = (bf16[256,512]{1,0:T(8,128)(2,1)S(1)}, bf16[256,512]{1,0:T(8,128)(2,1)S(1)}, u32[]{:S(2)}, u32[]{:S(2)}) collective-permute-start(bf16[256,512]{1,0:T(8,128)(2,1)S(1)} %attend.5.mine), channel_id=1, source_target_pairs={{0,0},{1,64},{2,2},{3,66},{4,4},{5,68},{6,6},{7,70},{8,8},{9,72},{... | collective-permute-start | bytes 786440 | tf_op jit(solution)/shard_map/ppermute | solution.py:47
  102.3 8.2 %collective-permute-start.14 = (bf16[256,512]{1,0:T(8,128)(2,1)S(1)}, bf16[256,512]{1,0:T(8,128)(2,1)S(1)}, u32[]{:S(2)}, u32[]{:S(2)}) collective-permute-start(bf16[256,512]{1,0:T(8,128)(2,1)S(1)} %attend.5.mine), channel_id=1, source_target_pairs={{0,64},{1,0},{2,66},{3,2},{4,68},{5,4},{6,70},{7,6},{8,72},{9,8},{... | collective-permute-start | bytes 786440 | tf_op jit(solution)/shard_map/ppermute | solution.py:47
  112.4 28.3 %collective-permute-start.17 = (bf16[256,512]{1,0:T(8,128)(2,1)S(1)}, bf16[256,512]{1,0:T(8,128)(2,1)S(1)}, u32[]{:S(2)}, u32[]{:S(2)}) collective-permute-start(bf16[256,512]{1,0:T(8,128)(2,1)S(1)} %get-tuple-element.77), channel_id=1, source_target_pairs={{0,4},{1,68},{2,6},{3,70},{4,0},{5,64},{6,2},{7,66},{8,12},{9,76},... | collective-permute-start | bytes 786440 | tf_op jit(solution)/shard_map/ppermute | solution.py:47
  122.3 22.7 %collective-permute-start.18 = (bf16[256,512]{1,0:T(8,128)(2,1)S(1)}, bf16[256,512]{1,0:T(8,128)(2,1)S(1)}, u32[]{:S(2)}, u32[]{:S(2)}) collective-permute-start(bf16[256,512]{1,0:T(8,128)(2,1)S(1)} %get-tuple-element.78), channel_id=1, source_target_pairs={{0,2},{1,66},{2,4},{3,68},{4,6},{5,70},{6,0},{7,64},{8,10},{9,74},... | collective-permute-start | bytes 786440 | tf_op jit(solution)/shard_map/ppermute | solution.py:47
  126.4 18.7 %collective-permute-start.19 = (bf16[256,512]{1,0:T(8,128)(2,1)S(1)}, bf16[256,512]{1,0:T(8,128)(2,1)S(1)}, u32[]{:S(2)}, u32[]{:S(2)}) collective-permute-start(bf16[256,512]{1,0:T(8,128)(2,1)S(1)} %get-tuple-element.79), channel_id=1, source_target_pairs={{0,6},{1,70},{2,0},{3,64},{4,2},{5,66},{6,4},{7,68},{8,14},{9,78},... | collective-permute-start | bytes 786440 | tf_op jit(solution)/shard_map/ppermute | solution.py:47
  129.1 16.9 %collective-permute-start.20 = (bf16[256,512]{1,0:T(8,128)(2,1)S(1)}, bf16[256,512]{1,0:T(8,128)(2,1)S(1)}, u32[]{:S(2)}, u32[]{:S(2)}) collective-permute-start(bf16[256,512]{1,0:T(8,128)(2,1)S(1)} %get-tuple-element.80), channel_id=1, source_target_pairs={{0,0},{1,64},{2,2},{3,66},{4,4},{5,68},{6,6},{7,70},{8,8},{9,72},{... | collective-permute-start | bytes 786440 | tf_op jit(solution)/shard_map/ppermute | solution.py:47
  (3 other events, 2.6 us)
